TPU v7x, 512 devices: a whole 4x8x8 slice. The times are simulated.
512 devices in a mesh: section: 4 (over x), dom: 128 (over y, z, core).
Axes of the slice: x: 4, y: 8, z: 8, core: 2. Of those that a mesh axis runs over, the one named last changes fastest.
Arguments:
- features: bfloat16 [2, 131072, 128], P(None, 'dom'), may hold values from -6 to 6
- counts: int32 [128], P('dom'), may hold values from 512 to 1024, as said below
- row_blocks: int32 [3072], P('dom'), may hold values from 0 to 7
- col_blocks: int32 [3072], P('dom'), may hold values from 0 to 9, as said below
- adjacency: bfloat16 [3072, 128, 128], P('dom'), may hold values from -0.3125 to 0.3125
- send_up: int32 [128], P('dom'), may hold values from 0 to 3
- send_down: int32 [128], P('dom'), may hold values from 0 to 3
- w_message: bfloat16 [8, 128, 128], P('section'), may hold values from -0.5 to 0.5
- w_hidden: bfloat16 [8, 256, 128], P('section'), may hold values from -0.375 to 0.375
- b_hidden: bfloat16 [8, 128], P('section'), may hold values from -3 to 3
- w_out: bfloat16 [8, 128, 128], P('section'), may hold values from -0.5 to 0.5
- b_out: bfloat16 [8, 128], P('section'), may hold values from -3 to 3
- gain: bfloat16 [8, 128], P('section'), may hold values from 0.099609375 to 1.8984375
Outputs:
- checkpoints: bfloat16 [4, 2, 131072, 128], P('section', None, 'dom')
Inputs may be any that keep to these rules, and one draw needn't show every extreme that they name: `counts`: some partition has exactly 1024 live nodes. `col_blocks`: each of the last 2 extended block indices is named by some adjacency block of every partition.
All inputs are finite; a program needn't handle non-finite values.
Results may differ from a plain program's by a relative error of at most 0.015.
Values may be sent and summed in bfloat16 or wider, within the bound.
No kernel may reach another device: no remote copies, remote signals or barrier semaphores. Data moves between devices by JAX's collectives and lax.ppermute only.
A program may use at most 64 MiB of HBM per device.

v0:
```python
import jax
import jax.numpy as jnp
from jax import lax
from jax.experimental import pallas as pl
from jax.experimental.pallas import tpu as pltpu
from jax.sharding import PartitionSpec as P

BF = jnp.bfloat16
F32 = jnp.float32
VM = pl.BlockSpec(memory_space=pltpu.VMEM)
SM = pl.BlockSpec(memory_space=pltpu.SMEM)


def call(body, outs, ins, name, scratch=(), room=8):
    return pl.pallas_call(
        body,
        out_shape=outs,
        in_specs=ins,
        out_specs=jax.tree.map(lambda _: VM, outs),
        scratch_shapes=list(scratch),
        name=name,
        compiler_params=pltpu.CompilerParams(vmem_limit_bytes=room << 20),
    )


def silu(v):
    return 0.5 * v * (1.0 + jnp.tanh(0.5 * v))


def twice(w):
    zero = jnp.zeros_like(w)
    return jnp.concatenate(
        [jnp.concatenate([w, zero], axis=1), jnp.concatenate([zero, w], axis=1)], axis=0
    )


def pack_body(wm, wh, bh, wo, bo, gain, out):
    d = wm.shape[1]
    for i in range(2):
        out[i * d : (i + 1) * d] = wm[i]
        out[2 * d + i * 2 * d : 2 * d + (i + 1) * 2 * d] = wh[i]
        w = wo[i].astype(F32)
        out[6 * d + i * d : 6 * d + (i + 1) * d] = (w - jnp.mean(w, axis=1, keepdims=True)).astype(BF)
    b = bo[...].astype(F32)
    b = b - jnp.mean(b, axis=1, keepdims=True)
    high = b.astype(BF)
    low = (b - high.astype(F32)).astype(BF)
    pad = jnp.zeros((8, d), F32)
    vectors = [bh[...].astype(F32), high.astype(F32), low.astype(F32), gain[...].astype(F32), pad]
    out[8 * d :] = jnp.concatenate(vectors, axis=0).astype(BF)


def prep_body(meta, rows, cols, x, adj, h, send, dense, acc):
    count, even = meta[0], meta[1]
    n, d = x.shape[1], x.shape[2]
    blk = adj.shape[1]
    live = lax.broadcasted_iota(jnp.int32, (n, d), 0) < count
    for m in range(2):
        h[:, m * d : (m + 1) * d] = jnp.where(live, x[m], jnp.zeros_like(x[m]))
    for i in range(2):
        send[i] = h[pl.ds(pl.multiple_of(meta[2 + i] * blk, blk), blk), :]
    acc[...] = jnp.zeros_like(acc)
    last = n // blk
    for k in range(adj.shape[0]):
        c = cols[k]
        c = jnp.where(c < last, c, jnp.where(even == 1, 2 * last + 1 - c, c))
        at = (rows[k], c)
        acc[at] = acc[at] + adj[k].astype(F32)
    for r in range(n // blk):
        for c in range(last + 2):
            dense[r * blk : (r + 1) * blk, c * blk : (c + 1) * blk] = acc[r, c].astype(BF)


def messages(h, pack, i):
    d = pack.shape[1]
    wm = twice(pack[i * d : (i + 1) * d])
    return silu(jnp.dot(h, wm, preferred_element_type=F32)).astype(BF)


def update(h, a_local, a_halo, m, halo, live, pack, i):
    d = pack.shape[1]
    agg = jnp.dot(a_local, m, preferred_element_type=F32)
    agg = (agg + jnp.dot(a_halo, halo, preferred_element_type=F32)).astype(BF)
    wh = pack[2 * d + i * 2 * d : 2 * d + (i + 1) * 2 * d]
    wo = twice(pack[6 * d + i * d : 6 * d + (i + 1) * d])
    v = pack[8 * d :].astype(F32)

    def row(j):
        r = v[j + i : j + i + 1]
        return jnp.concatenate([r, r], axis=1)

    pre = jnp.concatenate(
        [
            jnp.dot(
                jnp.concatenate([h[:, s : s + d], agg[:, s : s + d]], axis=1),
                wh,
                preferred_element_type=F32,
            )
            for s in (0, d)
        ],
        axis=1,
    )
    hidden = silu(pre + row(0)).astype(BF)
    c = jnp.dot(hidden, wo, preferred_element_type=F32) + (row(2) + row(4))
    mean = twice(jnp.full((d, d), 1.0 / d, BF))
    var = jnp.dot((c * c).astype(BF), mean, preferred_element_type=F32)
    new = h.astype(F32) + c * lax.rsqrt(var + 1e-05) * row(6)
    return jnp.where(live, new, 0.0).astype(BF)


def first_body(meta, h, haloq, halor, pack, m, halo):
    m[...] = messages(h[...], pack, 0)
    blk = halor.shape[0]
    halo[:blk] = messages(haloq[meta[1]], pack, 0)
    halo[blk:] = messages(halor[...], pack, 0)


def gather_halo(meta, haloq, halor):
    return jnp.concatenate([haloq[meta[1]], halor[...]], axis=0)


def send_body(step, first):
    def body(meta, h, m, haloq, halor, dense, pack, nxt, outq, outr):
        n = m.shape[0]
        blk = halor.shape[0] // (2 if first else 1)
        halo = halor[...] if first else gather_halo(meta, haloq, halor)
        for i, out in ((0, outq), (1, outr)):
            at = pl.ds(pl.multiple_of(meta[2 + i] * blk, blk), blk)
            row = meta[2 + i] * blk + lax.broadcasted_iota(jnp.int32, (blk, h.shape[1]), 0)
            new = update(
                h[at, :], dense[at, :n], dense[at, n:], m[...], halo, row < meta[0], pack, step % 2
            )
            out[...] = messages(new, nxt, (step + 1) % 2)

    return body


def rows_body(step, first, last):
    def body(meta, h, m, haloq, halor, dense, pack, nxt, *outs):
        n, d2 = m.shape
        halo = halor[...] if first else gather_halo(meta, haloq, halor)
        chunk = 256
        for r in range(0, n, chunk):
            at = slice(r, r + chunk)
            live = r + lax.broadcasted_iota(jnp.int32, (chunk, d2), 0) < meta[0]
            new = update(h[at], dense[at, :n], dense[at, n:], m[...], halo, live, pack, step % 2)
            if last:
                outs[0][0, at] = new[:, : d2 // 2]
                outs[0][1, at] = new[:, d2 // 2 :]
            else:
                outs[0][at] = new
                outs[1][at] = messages(new, nxt, (step + 1) % 2)

    return body


def shards(
    features,
    counts,
    row_blocks,
    col_blocks,
    adjacency,
    send_up,
    send_down,
    w_message,
    w_hidden,
    b_hidden,
    w_out,
    b_out,
    gain,
):
    n, d = features.shape[1:]
    blk = adjacency.shape[1]
    doms = lax.axis_size("dom")
    sections = lax.axis_size("section")
    layers = w_message.shape[0]
    odd = lax.axis_index("dom") % 2
    even = 1 - odd
    near = jnp.where(odd == 1, send_down[0], send_up[0])
    far = jnp.where(odd == 1, send_up[0], send_down[0])
    meta = jnp.stack([counts[0], even, near, far]).astype(jnp.int32)
    pairs = [[i, i + 1] for i in range(0, doms, 2)]
    across = [(i, i + 1) for i in range(1, doms - 1, 2)] + [(i + 1, i) for i in range(1, doms - 1, 2)]

    def s(*shape, dtype=BF):
        return jax.ShapeDtypeStruct(shape, dtype)

    def exchange(q, r):
        halor = lax.ppermute(r, "dom", across)
        haloq = lax.all_gather(q, "dom", axis_index_groups=pairs)
        return haloq, halor

    rows = w_message.shape[0] * 4 * d + 16
    own = call(pack_body, s(rows, d), [VM] * 6, "pack")(
        w_message, w_hidden, b_hidden, w_out, b_out, gain
    )
    packs = [
        lax.ppermute(own, "section", [(i, i + k) for i in range(sections - k)])
        for k in range(sections - 1, 0, -1)
    ] + [own]
    h, send, dense = call(
        prep_body,
        (s(n, 2 * d), s(2, blk, 2 * d), s(n, n + 2 * blk)),
        [SM, SM, SM, VM, VM],
        "prep",
        [pltpu.VMEM((n // blk, n // blk + 2, blk, blk), F32)],
        16,
    )(meta, row_blocks, col_blocks, features, adjacency)
    haloq, halor = exchange(send[0], send[1])
    m, halor = call(first_body, (s(n, 2 * d), s(2 * blk, 2 * d)), [SM] + [VM] * 4, "first")(
        meta, h, haloq, halor, packs[0]
    )
    steps = layers * sections
    for step in range(steps):
        pack = packs[step // layers]
        nxt = packs[min(step + 1, steps - 1) // layers]
        args = (meta, h, m, haloq, halor, dense, pack, nxt)
        ins = [SM] + [VM] * 7
        if step + 1 == steps:
            out = call(rows_body(step, step == 0, True), s(2, n, d), ins, f"rows{step}")(*args)
            return out[None]
        q, r = call(
            send_body(step, step == 0), (s(blk, 2 * d), s(blk, 2 * d)), ins, f"send{step}"
        )(*args)
        haloq, halor = exchange(q, r)
        h, m = call(
            rows_body(step, step == 0, False), (s(n, 2 * d), s(n, 2 * d)), ins, f"rows{step}"
        )(*args)


def solution(mesh):
    placed = (
        P(None, "dom", None),
        P("dom"),
        P("dom"),
        P("dom"),
        P("dom", None, None),
        P("dom"),
        P("dom"),
        P("section", None, None),
        P("section", None, None),
        P("section", None),
        P("section", None, None),
        P("section", None),
        P("section", None),
    )
    return jax.shard_map(
        shards,
        mesh=mesh,
        in_specs=placed,
        out_specs=P("section", None, "dom", None),
        check_vma=False,
    )
```

profile of v0, /device:TPU:33, one launch (start us, length us, event | category | flops | bytes accessed | tf_op | source)
XLA Modules:
  0.0 125.1 jit_solution(3556742204803580414)
XLA Ops:
  4.7 4.4 %collective-permute-start.1 = (bf16[1040,128]{1,0:T(8,128)(2,1)S(1)}, bf16[1040,128]{1,0:T(8,128)(2,1)S(1)}, u32[]{:S(2)}, u32[]{:S(2)}) collective-permute-start(bf16[1040,128]{1,0:T(8,128)(2,1)S(1)} %pack.1.nxt), channel_id=1, source_target_pairs={{0,384},{1,385},{2,386},{3,387},{4,388},{5,389},{6,390},{7,391},{8... | collective-permute-start | bytes 798728 | tf_op jit(solution)/shard_map/ppermute | solution.py:198
  10.4 2.5 %collective-permute-start.6 = (bf16[1040,128]{1,0:T(8,128)(2,1)S(1)}, bf16[1040,128]{1,0:T(8,128)(2,1)S(1)}, u32[]{:S(2)}, u32[]{:S(2)}) collective-permute-start(bf16[1040,128]{1,0:T(8,128)(2,1)S(1)} %pack.1.nxt), channel_id=1, source_target_pairs={{0,128},{128,256},{256,384},{1,129},{129,257},{257,385},{2,130},{1... | collective-permute-start | bytes 798728 | tf_op jit(solution)/shard_map/ppermute | solution.py:198
  20.0 5.1 %collective-permute-start = (bf16[128,256]{1,0:T(8,128)(2,1)S(1)}, bf16[128,256]{1,0:T(8,128)(2,1)S(1)}, u32[]{:S(2)}, u32[]{:S(2)}) collective-permute-start(bf16[128,256]{1,0:T(8,128)(2,1)S(1)} %get-tuple-element.71), channel_id=1, source_target_pairs={{1,2},{3,4},{5,6},{7,8},{9,10},{11,12},{13,14},{15,16},{17,18},{19... | collective-permute-start | bytes 196616 | tf_op jit(solution)/shard_map/ppermute | solution.py:189
  25.1 7.4 %all_gather.45.haloq = bf16[2,128,256]{2,1,0:T(8,128)(2,1)S(1)} all-gather(bf16[1,128,256]{2,1,0:T(8,128)(2,1)S(1)} %get-tuple-element.72), channel_id=1, replica_groups={{0,1},{2,3},{4,5},{6,7},{8,9},{10,11},{12,13},{14,15},{16,17},{18,19},{..., dimensions={0}, use_global_device_ids=true | all-gather | bytes 196608 | tf_op jit(solution)/shard_map/all_gather | solution.py:190
  33.4 2.1 %send0.1 = (bf16[128,256]{1,0:T(8,128)(2,1)S(1)}, bf16[128,256]{1,0:T(8,128)(2,1)S(1)}) custom-call(s32[4]{0:T(128)S(1)} %pad_add_fusion.meta, bf16[1024,256]{1,0:T(8,128)(2,1)S(1)} %get-tuple-element.38.h, bf16[1024,256]{1,0:T(8,128)(2,1)S(1)} %get-tuple-element.40.m, bf16[2,128,256]{2,1,0:T(8,128)(2,1)S(1)} %all_gather.45.haloq, ...), custom_call_target="tpu_custom_call" | custom-call | tf_op jit(solution)/shard_map/send0/pallas_call | solution.py:222
  37.5 3.6 %rows0.1 = (bf16[1024,256]{1,0:T(8,128)(2,1)S(1)}, bf16[1024,256]{1,0:T(8,128)(2,1)S(1)}) custom-call(s32[4]{0:T(128)S(1)} %pad_add_fusion.meta, bf16[1024,256]{1,0:T(8,128)(2,1)S(1)} %get-tuple-element.38.h, bf16[1024,256]{1,0:T(8,128)(2,1)S(1)} %get-tuple-element.40.m, bf16[2,128,256]{2,1,0:T(8,128)(2,1)S(1)} %all_gather.45.haloq, ...), custom_call_target="tpu_custom_call" | custom-call | tf_op jit(solution)/shard_map/rows0/pallas_call | solution.py:226
  41.1 7.0 %all-gather = bf16[256,256]{1,0:T(8,128)(2,1)S(1)} all-gather(bf16[128,256]{1,0:T(8,128)(2,1)S(1)} %get-tuple-element.45), channel_id=2, replica_groups={{0,1},{2,3},{4,5},{6,7},{8,9},{10,11},{12,13},{14,15},{16,17},{18,19},{..., dimensions={0}, use_global_device_ids=true | all-gather | bytes 196608 | tf_op jit(solution)/shard_map/all_gather | solution.py:190
  52.1 3.6 %rows1.1 = (bf16[1024,256]{1,0:T(8,128)(2,1)S(1)}, bf16[1024,256]{1,0:T(8,128)(2,1)S(1)}) custom-call(s32[4]{0:T(128)S(1)} %pad_add_fusion.meta, bf16[1024,256]{1,0:T(8,128)(2,1)S(1)} %get-tuple-element.43.h, bf16[1024,256]{1,0:T(8,128)(2,1)S(1)} %get-tuple-element.44.m, bf16[2,128,256]{2,1,0:T(8,128)(2,1)S(1)} %bitcast.20, ...), custom_call_target="tpu_custom_call" | custom-call | tf_op jit(solution)/shard_map/rows1/pallas_call | solution.py:226
  55.7 3.4 %all-gather.1 = bf16[256,256]{1,0:T(8,128)(2,1)S(1)} all-gather(bf16[128,256]{1,0:T(8,128)(2,1)S(1)} %get-tuple-element.49), channel_id=3, replica_groups={{0,1},{2,3},{4,5},{6,7},{8,9},{10,11},{12,13},{14,15},{16,17},{18,19},{..., dimensions={0}, use_global_device_ids=true | all-gather | bytes 196608 | tf_op jit(solution)/shard_map/all_gather | solution.py:190
  61.2 2.2 %collective-permute-start.5 = (bf16[128,256]{1,0:T(8,128)(2,1)S(1)}, bf16[128,256]{1,0:T(8,128)(2,1)S(1)}, u32[]{:S(2)}, u32[]{:S(2)}) collective-permute-start(bf16[128,256]{1,0:T(8,128)(2,1)S(1)} %get-tuple-element.54), channel_id=1, source_target_pairs={{1,2},{3,4},{5,6},{7,8},{9,10},{11,12},{13,14},{15,16},{17,18},{19... | collective-permute-start | bytes 196616 | tf_op jit(solution)/shard_map/ppermute | solution.py:189
  63.4 3.6 %rows2.1 = (bf16[1024,256]{1,0:T(8,128)(2,1)S(1)}, bf16[1024,256]{1,0:T(8,128)(2,1)S(1)}) custom-call(s32[4]{0:T(128)S(1)} %pad_add_fusion.meta, bf16[1024,256]{1,0:T(8,128)(2,1)S(1)} %get-tuple-element.47.h, bf16[1024,256]{1,0:T(8,128)(2,1)S(1)} %get-tuple-element.48.m, bf16[2,128,256]{2,1,0:T(8,128)(2,1)S(1)} %bitcast.26, ...), custom_call_target="tpu_custom_call" | custom-call | tf_op jit(solution)/shard_map/rows2/pallas_call | solution.py:226
  67.0 5.4 %all-gather.2 = bf16[256,256]{1,0:T(8,128)(2,1)S(1)} all-gather(bf16[128,256]{1,0:T(8,128)(2,1)S(1)} %get-tuple-element.53), channel_id=4, replica_groups={{0,1},{2,3},{4,5},{6,7},{8,9},{10,11},{12,13},{14,15},{16,17},{18,19},{..., dimensions={0}, use_global_device_ids=true | all-gather | bytes 196608 | tf_op jit(solution)/shard_map/all_gather | solution.py:190
  72.4 2.1 %send3.1 = (bf16[128,256]{1,0:T(8,128)(2,1)S(1)}, bf16[128,256]{1,0:T(8,128)(2,1)S(1)}) custom-call(s32[4]{0:T(128)S(1)} %pad_add_fusion.meta, bf16[1024,256]{1,0:T(8,128)(2,1)S(1)} %get-tuple-element.51.h, bf16[1024,256]{1,0:T(8,128)(2,1)S(1)} %get-tuple-element.52.m, bf16[2,128,256]{2,1,0:T(8,128)(2,1)S(1)} %bitcast.21, ...), custom_call_target="tpu_custom_call" | custom-call | tf_op jit(solution)/shard_map/send3/pallas_call | solution.py:222
  76.4 3.6 %rows3.1 = (bf16[1024,256]{1,0:T(8,128)(2,1)S(1)}, bf16[1024,256]{1,0:T(8,128)(2,1)S(1)}) custom-call(s32[4]{0:T(128)S(1)} %pad_add_fusion.meta, bf16[1024,256]{1,0:T(8,128)(2,1)S(1)} %get-tuple-element.51.h, bf16[1024,256]{1,0:T(8,128)(2,1)S(1)} %get-tuple-element.52.m, bf16[2,128,256]{2,1,0:T(8,128)(2,1)S(1)} %bitcast.22, ...), custom_call_target="tpu_custom_call" | custom-call | tf_op jit(solution)/shard_map/rows3/pallas_call | solution.py:226
  80.0 3.4 %all-gather.3 = bf16[256,256]{1,0:T(8,128)(2,1)S(1)} all-gather(bf16[128,256]{1,0:T(8,128)(2,1)S(1)} %get-tuple-element.57), channel_id=5, replica_groups={{0,1},{2,3},{4,5},{6,7},{8,9},{10,11},{12,13},{14,15},{16,17},{18,19},{..., dimensions={0}, use_global_device_ids=true | all-gather | bytes 196608 | tf_op jit(solution)/shard_map/all_gather | solution.py:190
  85.5 2.2 %collective-permute-start.8 = (bf16[128,256]{1,0:T(8,128)(2,1)S(1)}, bf16[128,256]{1,0:T(8,128)(2,1)S(1)}, u32[]{:S(2)}, u32[]{:S(2)}) collective-permute-start(bf16[128,256]{1,0:T(8,128)(2,1)S(1)} %get-tuple-element.62), channel_id=1, source_target_pairs={{1,2},{3,4},{5,6},{7,8},{9,10},{11,12},{13,14},{15,16},{17,18},{19... | collective-permute-start | bytes 196616 | tf_op jit(solution)/shard_map/ppermute | solution.py:189
  87.7 3.6 %rows4.1 = (bf16[1024,256]{1,0:T(8,128)(2,1)S(1)}, bf16[1024,256]{1,0:T(8,128)(2,1)S(1)}) custom-call(s32[4]{0:T(128)S(1)} %pad_add_fusion.meta, bf16[1024,256]{1,0:T(8,128)(2,1)S(1)} %get-tuple-element.55.h, bf16[1024,256]{1,0:T(8,128)(2,1)S(1)} %get-tuple-element.56.m, bf16[2,128,256]{2,1,0:T(8,128)(2,1)S(1)} %bitcast.28, ...), custom_call_target="tpu_custom_call" | custom-call | tf_op jit(solution)/shard_map/rows4/pallas_call | solution.py:226
  91.3 5.2 %all-gather.4 = bf16[256,256]{1,0:T(8,128)(2,1)S(1)} all-gather(bf16[128,256]{1,0:T(8,128)(2,1)S(1)} %get-tuple-element.61), channel_id=6, replica_groups={{0,1},{2,3},{4,5},{6,7},{8,9},{10,11},{12,13},{14,15},{16,17},{18,19},{..., dimensions={0}, use_global_device_ids=true | all-gather | bytes 196608 | tf_op jit(solution)/shard_map/all_gather | solution.py:190
  100.5 3.6 %rows5.1 = (bf16[1024,256]{1,0:T(8,128)(2,1)S(1)}, bf16[1024,256]{1,0:T(8,128)(2,1)S(1)}) custom-call(s32[4]{0:T(128)S(1)} %pad_add_fusion.meta, bf16[1024,256]{1,0:T(8,128)(2,1)S(1)} %get-tuple-element.59.h, bf16[1024,256]{1,0:T(8,128)(2,1)S(1)} %get-tuple-element.60.m, bf16[2,128,256]{2,1,0:T(8,128)(2,1)S(1)} %bitcast.24, ...), custom_call_target="tpu_custom_call" | custom-call | tf_op jit(solution)/shard_map/rows5/pallas_call | solution.py:226
  104.1 3.4 %all-gather.5 = bf16[256,256]{1,0:T(8,128)(2,1)S(1)} all-gather(bf16[128,256]{1,0:T(8,128)(2,1)S(1)} %get-tuple-element.65), channel_id=7, replica_groups={{0,1},{2,3},{4,5},{6,7},{8,9},{10,11},{12,13},{14,15},{16,17},{18,19},{..., dimensions={0}, use_global_device_ids=true | all-gather | bytes 196608 | tf_op jit(solution)/shard_map/all_gather | solution.py:190
  109.6 2.4 %collective-permute-start.10 = (bf16[128,256]{1,0:T(8,128)(2,1)S(1)}, bf16[128,256]{1,0:T(8,128)(2,1)S(1)}, u32[]{:S(2)}, u32[]{:S(2)}) collective-permute-start(bf16[128,256]{1,0:T(8,128)(2,1)S(1)} %get-tuple-element.70), channel_id=1, source_target_pairs={{1,2},{3,4},{5,6},{7,8},{9,10},{11,12},{13,14},{15,16},{17,18},{19... | collective-permute-start | bytes 196616 | tf_op jit(solution)/shard_map/ppermute | solution.py:189
  112.0 3.6 %rows6.1 = (bf16[1024,256]{1,0:T(8,128)(2,1)S(1)}, bf16[1024,256]{1,0:T(8,128)(2,1)S(1)}) custom-call(s32[4]{0:T(128)S(1)} %pad_add_fusion.meta, bf16[1024,256]{1,0:T(8,128)(2,1)S(1)} %get-tuple-element.63.h, bf16[1024,256]{1,0:T(8,128)(2,1)S(1)} %get-tuple-element.64.m, bf16[2,128,256]{2,1,0:T(8,128)(2,1)S(1)} %bitcast.30, ...), custom_call_target="tpu_custom_call" | custom-call | tf_op jit(solution)/shard_map/rows6/pallas_call | solution.py:226
  115.6 5.2 %all-gather.6 = bf16[256,256]{1,0:T(8,128)(2,1)S(1)} all-gather(bf16[128,256]{1,0:T(8,128)(2,1)S(1)} %get-tuple-element.69), channel_id=8, replica_groups={{0,1},{2,3},{4,5},{6,7},{8,9},{10,11},{12,13},{14,15},{16,17},{18,19},{..., dimensions={0}, use_global_device_ids=true | all-gather | bytes 196608 | tf_op jit(solution)/shard_map/all_gather | solution.py:190
  120.8 4.3 %rows7.1 = bf16[2,1024,128]{2,1,0:T(8,128)(2,1)} custom-call(s32[4]{0:T(128)S(1)} %pad_add_fusion.meta, bf16[1024,256]{1,0:T(8,128)(2,1)S(1)} %get-tuple-element.67.h, bf16[1024,256]{1,0:T(8,128)(2,1)S(1)} %get-tuple-element.68.m, bf16[2,128,256]{2,1,0:T(8,128)(2,1)S(1)} %bitcast.31, bf16[128,256]{1,0:T(8,128)(2,1)S(1)} %collective-permute-done.10.halor, ...), custom_call_target="tpu_custom_call" | custom-call | tf_op jit(solution)/shard_map/rows7/pallas_call | solution.py:220
  (46 shorter events, 30.3 us)
Async XLA Ops:
  0.0 0.9 copy-start.2
  0.9 0.8 copy-start.3
  1.7 0.8 copy-start.4
  2.6 0.7 copy-start.5
  3.2 0.7 copy-start.6
  3.9 0.7 copy-start.7
  4.7 27.8 %collective-permute-start.1 = (bf16[1040,128]{1,0:T(8,128)(2,1)S(1)}, bf16[1040,128]{1,0:T(8,128)(2,1)S(1)}, u32[]{:S(2)}, u32[]{:S(2)}) collective-permute-start(bf16[1040,128]{1,0:T(8,128)(2,1)S(1)} %pack.1.nxt), channel_id=1, source_target_pairs={{0,384},{1,385},{2,386},{3,387},{4,388},{5,389},{6,390},{7,391},{8... | collective-permute-start | bytes 798728 | tf_op jit(solution)/shard_map/ppermute | solution.py:198
  9.1 39.0 %collective-permute-start.3 = (bf16[1040,128]{1,0:T(8,128)(2,1)S(1)}, bf16[1040,128]{1,0:T(8,128)(2,1)S(1)}, u32[]{:S(2)}, u32[]{:S(2)}) collective-permute-start(bf16[1040,128]{1,0:T(8,128)(2,1)S(1)} %pack.1.nxt), channel_id=1, source_target_pairs={{0,256},{128,384},{1,257},{129,385},{2,258},{130,386},{3,259},{131... | collective-permute-start | bytes 798728 | tf_op jit(solution)/shard_map/ppermute | solution.py:198
  10.4 62.0 %collective-permute-start.6 = (bf16[1040,128]{1,0:T(8,128)(2,1)S(1)}, bf16[1040,128]{1,0:T(8,128)(2,1)S(1)}, u32[]{:S(2)}, u32[]{:S(2)}) collective-permute-start(bf16[1040,128]{1,0:T(8,128)(2,1)S(1)} %pack.1.nxt), channel_id=1, source_target_pairs={{0,128},{128,256},{256,384},{1,129},{129,257},{257,385},{2,130},{1... | collective-permute-start | bytes 798728 | tf_op jit(solution)/shard_map/ppermute | solution.py:198
  14.9 1.1 copy-start
  16.1 1.0 copy-start.1
  17.1 0.7 copy-start.8
  17.8 0.7 copy-start.9
  20.0 12.5 %collective-permute-start = (bf16[128,256]{1,0:T(8,128)(2,1)S(1)}, bf16[128,256]{1,0:T(8,128)(2,1)S(1)}, u32[]{:S(2)}, u32[]{:S(2)}) collective-permute-start(bf16[128,256]{1,0:T(8,128)(2,1)S(1)} %get-tuple-element.71), channel_id=1, source_target_pairs={{1,2},{3,4},{5,6},{7,8},{9,10},{11,12},{13,14},{15,16},{17,18},{19... | collective-permute-start | bytes 196616 | tf_op jit(solution)/shard_map/ppermute | solution.py:189
  35.5 12.5 %collective-permute-start.2 = (bf16[128,256]{1,0:T(8,128)(2,1)S(1)}, bf16[128,256]{1,0:T(8,128)(2,1)S(1)}, u32[]{:S(2)}, u32[]{:S(2)}) collective-permute-start(bf16[128,256]{1,0:T(8,128)(2,1)S(1)} %get-tuple-element.46), channel_id=1, source_target_pairs={{1,2},{3,4},{5,6},{7,8},{9,10},{11,12},{13,14},{15,16},{17,18},{19... | collective-permute-start | bytes 196616 | tf_op jit(solution)/shard_map/ppermute | solution.py:189
  50.2 8.9 %collective-permute-start.4 = (bf16[128,256]{1,0:T(8,128)(2,1)S(1)}, bf16[128,256]{1,0:T(8,128)(2,1)S(1)}, u32[]{:S(2)}, u32[]{:S(2)}) collective-permute-start(bf16[128,256]{1,0:T(8,128)(2,1)S(1)} %get-tuple-element.50), channel_id=1, source_target_pairs={{1,2},{3,4},{5,6},{7,8},{9,10},{11,12},{13,14},{15,16},{17,18},{19... | collective-permute-start | bytes 196616 | tf_op jit(solution)/shard_map/ppermute | solution.py:189
  61.2 11.2 %collective-permute-start.5 = (bf16[128,256]{1,0:T(8,128)(2,1)S(1)}, bf16[128,256]{1,0:T(8,128)(2,1)S(1)}, u32[]{:S(2)}, u32[]{:S(2)}) collective-permute-start(bf16[128,256]{1,0:T(8,128)(2,1)S(1)} %get-tuple-element.54), channel_id=1, source_target_pairs={{1,2},{3,4},{5,6},{7,8},{9,10},{11,12},{13,14},{15,16},{17,18},{19... | collective-permute-start | bytes 196616 | tf_op jit(solution)/shard_map/ppermute | solution.py:189
  74.5 8.9 %collective-permute-start.7 = (bf16[128,256]{1,0:T(8,128)(2,1)S(1)}, bf16[128,256]{1,0:T(8,128)(2,1)S(1)}, u32[]{:S(2)}, u32[]{:S(2)}) collective-permute-start(bf16[128,256]{1,0:T(8,128)(2,1)S(1)} %get-tuple-element.58), channel_id=1, source_target_pairs={{1,2},{3,4},{5,6},{7,8},{9,10},{11,12},{13,14},{15,16},{17,18},{19... | collective-permute-start | bytes 196616 | tf_op jit(solution)/shard_map/ppermute | solution.py:189
  85.5 11.0 %collective-permute-start.8 = (bf16[128,256]{1,0:T(8,128)(2,1)S(1)}, bf16[128,256]{1,0:T(8,128)(2,1)S(1)}, u32[]{:S(2)}, u32[]{:S(2)}) collective-permute-start(bf16[128,256]{1,0:T(8,128)(2,1)S(1)} %get-tuple-element.62), channel_id=1, source_target_pairs={{1,2},{3,4},{5,6},{7,8},{9,10},{11,12},{13,14},{15,16},{17,18},{19... | collective-permute-start | bytes 196616 | tf_op jit(solution)/shard_map/ppermute | solution.py:189
  98.6 8.9 %collective-permute-start.9 = (bf16[128,256]{1,0:T(8,128)(2,1)S(1)}, bf16[128,256]{1,0:T(8,128)(2,1)S(1)}, u32[]{:S(2)}, u32[]{:S(2)}) collective-permute-start(bf16[128,256]{1,0:T(8,128)(2,1)S(1)} %get-tuple-element.66), channel_id=1, source_target_pairs={{1,2},{3,4},{5,6},{7,8},{9,10},{11,12},{13,14},{15,16},{17,18},{19... | collective-permute-start | bytes 196616 | tf_op jit(solution)/shard_map/ppermute | solution.py:189
  109.6 11.2 %collective-permute-start.10 = (bf16[128,256]{1,0:T(8,128)(2,1)S(1)}, bf16[128,256]{1,0:T(8,128)(2,1)S(1)}, u32[]{:S(2)}, u32[]{:S(2)}) collective-permute-start(bf16[128,256]{1,0:T(8,128)(2,1)S(1)} %get-tuple-element.70), channel_id=1, source_target_pairs={{1,2},{3,4},{5,6},{7,8},{9,10},{11,12},{13,14},{15,16},{17,18},{19... | collective-permute-start | bytes 196616 | tf_op jit(solution)/shard_map/ppermute | solution.py:189
where the time goes:
time: 126 us; the launch traced here: 125 us
  Pallas kernels  46.7 us (37%)
  blocking collectives  40.3 us (32%)
  starting transfers between devices  27.7 us (22%)
  local copies, waits for them, and re-layouts  8.04 us (6%)
  between operations  2.18 us (2%)
    all_gather x8, blocking collectives, exchange(): haloq = lax.all_gather(q, 'dom', axis_index_groups=pairs)  40.3 us
    pallas_call x7, Pallas kernels, shards(): call(rows_body(step, step == 0, False), (s(n, 2 * d), s(n, 2 * d)), ins,...  25.2 us
    ppermute x8, starting transfers between devices, exchange(): halor = lax.ppermute(r, 'dom', across)  19.5 us
    pallas_call x7, Pallas kernels, shards(): call(send_body(step, step == 0), (s(blk, 2 * d), s(blk, 2 * d)), ins, f's...  14.7 us
    ppermute x3, starting transfers between devices, shards(): lax.ppermute(own, 'section', [(i, i + k) for i in range(sections - k)])  8.19 us
    unnamed x20, local copies, waits for them, and re-layouts  8.03 us
    pallas_call x1, Pallas kernels, shards(): call(rows_body(step, step == 0, True), s(2, n, d), ins, f'rows{step}')  4.25 us
  transfers between devices with their start and end apart: 11, of which 0 were waited for; matrix products, arithmetic and copies ran while one was open for 0% of the time, Pallas kernels for 27%

commit v1 on v0

v1 whole, which is shorter than its diff:
```python
import jax
import jax.numpy as jnp
from jax import lax
from jax.experimental import pallas as pl
from jax.experimental.pallas import tpu as pltpu
from jax.sharding import PartitionSpec as P


BF = jnp.bfloat16
F32 = jnp.float32
VM = pl.BlockSpec(memory_space=pltpu.VMEM)
SM = pl.BlockSpec(memory_space=pltpu.SMEM)
HB = pl.BlockSpec(memory_space=pltpu.HBM)
CHUNK = 256


def call(body, outs, ins, scratch=(), room=8, spaces=None):
    return pl.pallas_call(
        body,
        out_shape=outs,
        in_specs=ins,
        out_specs=spaces or jax.tree.map(lambda _: VM, outs),
        scratch_shapes=list(scratch),
        compiler_params=pltpu.CompilerParams(vmem_limit_bytes=room << 20),
    )


def in_hbm(a):
    return pltpu.with_memory_space_constraint(a, pltpu.HBM)


def dot(a, b):
    return jnp.dot(a, b, preferred_element_type=F32)


def silu_of_twice(u):
    return (u + u * jnp.tanh(u)).astype(BF)


def twice(w):
    zero = jnp.zeros_like(w)
    return jnp.concatenate(
        [jnp.concatenate([w, zero], axis=1), jnp.concatenate([zero, w], axis=1)], axis=0
    )


def begin_body(meta, x, wm, wh, bh, wo, bo, gain, out, sq, sr, xs, am, ah, ao, vb, vo, vg, sem):
    d = wm.shape[2]
    blk = sq.shape[0]
    copies = [
        pltpu.make_async_copy(src, dst, sem.at[i])
        for i, (src, dst) in enumerate(
            [(wm, am), (wh, ah), (wo, ao), (bh, vb), (bo, vo), (gain, vg)]
            + [
                (x.at[:, pl.ds(pl.multiple_of(meta[2 + i] * blk, blk), blk), :], xs.at[i])
                for i in range(2)
            ]
        )
    ]
    for copy in copies:
        copy.start()
    for copy in copies[:6]:
        copy.wait()
    for i in range(2):
        out[i * d : (i + 1) * d] = (am[i].astype(F32) * 0.5).astype(BF)
        at = 2 * d + i * 2 * d
        out[at : at + 2 * d] = (ah[i].astype(F32) * 0.5).astype(BF)
        w = ao[i].astype(F32)
        at = 6 * d + i * d
        out[at : at + d] = (w - jnp.mean(w, axis=1, keepdims=True)).astype(BF)
    b = vo[...].astype(F32)
    b = b - jnp.mean(b, axis=1, keepdims=True)
    high = b.astype(BF).astype(F32)
    pad = jnp.zeros((8, d), F32)
    vectors = [vb[...].astype(F32) * 0.5, high, b - high, vg[...].astype(F32), pad]
    out[8 * d :] = jnp.concatenate(vectors, axis=0).astype(BF)
    for copy in copies[6:]:
        copy.wait()
    for i, dst in ((0, sq), (1, sr)):
        row = meta[2 + i] * blk + lax.broadcasted_iota(jnp.int32, (blk, d), 0)
        for m in range(2):
            dst[:, m * d : (m + 1) * d] = jnp.where(row < meta[0], xs[i, m], jnp.zeros_like(xs[i, m]))


def prep_body(meta, rows, cols, x, adj, h, hs, dense, ds, mask, ms, pick, acc, xv, av, sem):
    count, even = meta[0], meta[1]
    n, d = xv.shape[1], xv.shape[2]
    blk = av.shape[1]
    copies = [
        pltpu.make_async_copy(x, xv, sem.at[0]),
        pltpu.make_async_copy(adj, av, sem.at[1]),
    ]
    for copy in copies:
        copy.start()
    acc[...] = jnp.zeros_like(acc)
    mask[...] = jnp.where(
        lax.broadcasted_iota(jnp.int32, (n, 2 * d), 0) < count, jnp.float32(1), jnp.float32(0)
    ).astype(BF)
    for i in range(2):
        chosen = jnp.where(even == i, jnp.float32(1), jnp.float32(0))
        pick[i] = jnp.full((blk, 2 * d), chosen, F32).astype(BF)
    copies[0].wait()
    for m in range(2):
        h[:, m * d : (m + 1) * d] = xv[m] * mask[:, :d]
    copies[1].wait()
    last = n // blk
    for k in range(av.shape[0]):
        c = cols[k]
        c = jnp.where(c < last, c, jnp.where(even == 1, 2 * last + 1 - c, c))
        at = (rows[k], c)
        acc[at] = acc[at] + av[k].astype(F32)
    for r in range(n // blk):
        for c in range(last + 2):
            dense[r * blk : (r + 1) * blk, c * blk : (c + 1) * blk] = acc[r, c].astype(BF)
    for i in range(2):
        at = pl.ds(pl.multiple_of(meta[2 + i] * blk, blk), blk)
        to = slice(i * blk, (i + 1) * blk)
        hs[to] = h[at, :]
        ms[to] = mask[at, :]
        ds[to] = dense[at, :]


def message_weight(pack, i):
    d = pack.shape[1]
    return twice(pack[i * d : (i + 1) * d])


def gather_halo(pick, haloq, halor):
    near = haloq[0] * pick[0] + haloq[1] * pick[1]
    return jnp.concatenate([near, halor[...]], axis=0)


def first_body(h, pick, haloq, halor, pack, m, halo):
    w = message_weight(pack, 0)
    m[...] = silu_of_twice(dot(h[...], w))
    halo[...] = silu_of_twice(dot(gather_halo(pick, haloq, halor), w))


def layer(h, m, halo, dense, mask, pack, i, agg, hidden, c, chunk):
    d = pack.shape[1]
    n = m.shape[0]
    rows = [slice(r, r + chunk) for r in range(0, h.shape[0], chunk)]
    wh = pack[2 * d + i * 2 * d : 2 * d + (i + 1) * 2 * d]
    wo = twice(pack[6 * d + i * d : 6 * d + (i + 1) * d])
    v = pack[8 * d :].astype(F32)

    def row(j):
        r = v[j + i : j + i + 1]
        return jnp.concatenate([r, r], axis=1)

    for at in rows:
        agg[at] = (dot(dense[at, :n], m[...]) + dot(dense[at, n:], halo)).astype(BF)
    b = row(0)
    for at in rows:
        pre = [
            dot(jnp.concatenate([h[at, s : s + d], agg[at, s : s + d]], axis=1), wh) for s in (0, d)
        ]
        hidden[at] = silu_of_twice(jnp.concatenate(pre, axis=1) + b)
    b = row(2) + row(4)
    for at in rows:
        c[at] = dot(hidden[at], wo) + b
    mean = twice(jnp.full((d, d), 1.0 / d, BF))
    gain = row(6)
    for at in rows:
        now = c[at]
        var = dot((now * now).astype(BF), mean)
        new = (h[at].astype(F32) + now * lax.rsqrt(var + 1e-05) * gain).astype(BF) * mask[at]
        yield at, new


def send_body(step, first):
    def body(hs, m, pick, haloq, halor, ds, ms, pack, nxt, new_hs, outq, outr, agg, hidden, c):
        blk = outq.shape[0]
        halo = halor[...] if first else gather_halo(pick, haloq, halor)
        for at, new in layer(hs, m, halo, ds, ms, pack, step % 2, agg, hidden, c, 2 * blk):
            new_hs[at] = new
            out = silu_of_twice(dot(new, message_weight(nxt, (step + 1) % 2)))
            outq[...] = out[:blk]
            outr[...] = out[blk:]

    return body


def rows_body(step, first):
    def body(h, m, pick, haloq, halor, dense, mask, pack, nxt, new_h, new_m, agg, hidden, c):
        halo = halor[...] if first else gather_halo(pick, haloq, halor)
        for at, new in layer(h, m, halo, dense, mask, pack, step % 2, agg, hidden, c, CHUNK):
            new_h[at] = new
        w = message_weight(nxt, (step + 1) % 2)
        for r in range(0, h.shape[0], CHUNK):
            at = slice(r, r + CHUNK)
            new_m[at] = silu_of_twice(dot(new_h[at], w))

    return body


def last_body(step):
    def body(h, m, pick, haloq, halor, dense, mask, pack, out, agg, hidden, c, stage, sem):
        halo = gather_halo(pick, haloq, halor)
        d = pack.shape[1]
        copies = []
        for at, new in layer(h, m, halo, dense, mask, pack, step % 2, agg, hidden, c, CHUNK):
            stage[0, at] = new[:, :d]
            stage[1, at] = new[:, d:]
            copies.append(
                pltpu.make_async_copy(stage.at[:, at, :], out.at[:, at, :], sem.at[len(copies)])
            )
            copies[-1].start()
        for copy in copies:
            copy.wait()

    return body


def shards(
    features,
    counts,
    row_blocks,
    col_blocks,
    adjacency,
    send_up,
    send_down,
    w_message,
    w_hidden,
    b_hidden,
    w_out,
    b_out,
    gain,
):
    n, d = features.shape[1:]
    blk = adjacency.shape[1]
    doms = lax.axis_size("dom")
    sections = lax.axis_size("section")
    layers = w_message.shape[0]
    odd = lax.axis_index("dom") % 2
    near = jnp.where(odd == 1, send_down[0], send_up[0])
    far = jnp.where(odd == 1, send_up[0], send_down[0])
    meta = jnp.stack([counts[0], 1 - odd, near, far]).astype(jnp.int32)
    pairs = [[i, i + 1] for i in range(0, doms, 2)]
    across = [(i, i + 1) for i in range(1, doms - 1, 2)] + [(i + 1, i) for i in range(1, doms - 1, 2)]

    def s(*shape, dtype=BF):
        return jax.ShapeDtypeStruct(shape, dtype)

    def exchange(q, r):
        halor = lax.ppermute(r, "dom", across)
        haloq = lax.all_gather(q, "dom", axis_index_groups=pairs)
        return haloq, halor

    def fetch(own, k):
        return lax.ppermute(own, "section", [(i, i + k) for i in range(sections - k)])

    vec = pltpu.VMEM((layers, d), BF)
    own, q, r = call(
        begin_body,
        (s(layers * 4 * d + 16, d), s(blk, 2 * d), s(blk, 2 * d)),
        [SM] + [HB] * 7,
        [
            pltpu.VMEM((2, 2, blk, d), BF),
            pltpu.VMEM((layers, d, d), BF),
            pltpu.VMEM((layers, 2 * d, d), BF),
            pltpu.VMEM((layers, d, d), BF),
            vec,
            vec,
            vec,
            pltpu.SemaphoreType.DMA((8,)),
        ],
    )(meta, *map(in_hbm, (features, w_message, w_hidden, b_hidden, w_out, b_out, gain)))
    packs = [fetch(own, sections - 1)]
    wide = n + 2 * blk
    halor = lax.ppermute(r, "dom", across)
    prep = call(
        prep_body,
        (
            s(n, 2 * d),
            s(2 * blk, 2 * d),
            s(n, wide),
            s(2 * blk, wide),
            s(n, 2 * d),
            s(2 * blk, 2 * d),
            s(2, blk, 2 * d),
        ),
        [SM, SM, SM, HB, HB],
        [
            pltpu.VMEM((n // blk, n // blk + 2, blk, blk), F32),
            pltpu.VMEM(features.shape, BF),
            pltpu.VMEM(adjacency.shape, BF),
            pltpu.SemaphoreType.DMA((2,)),
        ],
        16,
    )
    h, hs, dense, ds, mask, ms, pick = prep(meta, row_blocks, col_blocks, in_hbm(features), in_hbm(adjacency))
    q, pick = lax.optimization_barrier((q, pick))
    haloq = lax.all_gather(q, "dom", axis_index_groups=pairs)
    later, haloq = lax.optimization_barrier((own, haloq))
    packs += [fetch(later, k) for k in range(sections - 2, 0, -1)] + [own]
    m, halor = call(first_body, (s(n, 2 * d), s(2 * blk, 2 * d)), [VM] * 5)(
        h, pick, haloq, halor, packs[0]
    )

    def stages(rows):
        return [
            pltpu.VMEM((rows, 2 * d), BF),
            pltpu.VMEM((rows, 2 * d), BF),
            pltpu.VMEM((rows, 2 * d), F32),
        ]

    steps = layers * sections
    for step in range(steps):
        pack = packs[step // layers]
        if step + 1 == steps:
            out = call(
                last_body(step),
                s(2, n, d),
                [VM] * 8,
                stages(n) + [pltpu.VMEM((2, n, d), BF), pltpu.SemaphoreType.DMA((n // CHUNK,))],
                spaces=HB,
            )(h, m, pick, haloq, halor, dense, mask, pack)
            return out[None]
        nxt = packs[(step + 1) // layers]
        hs, q, r = call(
            send_body(step, step == 0),
            (s(2 * blk, 2 * d), s(blk, 2 * d), s(blk, 2 * d)),
            [VM] * 9,
            stages(2 * blk),
        )(hs, m, pick, haloq, halor, ds, ms, pack, nxt)
        far_halo, near_halo = halor, haloq
        haloq, halor = exchange(q, r)
        h, m = call(
            rows_body(step, step == 0), (s(n, 2 * d), s(n, 2 * d)), [VM] * 9, stages(n)
        )(h, m, pick, near_halo, far_halo, dense, mask, pack, nxt)


def solution(mesh):
    placed = (
        P(None, "dom", None),
        P("dom"),
        P("dom"),
        P("dom"),
        P("dom", None, None),
        P("dom"),
        P("dom"),
        P("section", None, None),
        P("section", None, None),
        P("section", None),
        P("section", None, None),
        P("section", None),
        P("section", None),
    )
    return jax.shard_map(
        shards,
        mesh=mesh,
        in_specs=placed,
        out_specs=P("section", None, "dom", None),
        check_vma=False,
    )
```

time: 126 us -> 106 us (0.84)
  Pallas kernels: 46.7 us -> 27.2 us
  local copies, waits for them, and re-layouts: 8.04 us -> 1.31 us
  blocking collectives: 40.3 us -> 44.7 us
  waiting for transfers between devices: 0.03 us -> 1.96 us
    pallas_call x18, Pallas kernels: 46.7 us -> 27.2 us  [the longest x7 12.1 us: shards(): call(rows_body(step, step == 0), (s(n, 2 * d), s(n, 2 * d)), [VM] * 9, st...]
    unnamed x20 -> x4, local copies, waits for them, and re-layouts: 8.03 us -> 1.31 us
    ppermute x3 -> x4, starting transfers between devices: 8.19 us -> 12.7 us  [the longest x3 7.9 us: fetch(): lax.ppermute(own, 'section', [(i, i + k) for i in range(sections - k)])]
    ppermute x8 -> x7, starting transfers between devices: 19.5 us -> 15.3 us  [exchange(): halor = lax.ppermute(r, 'dom', across)]
    all_gather x0 -> x1, blocking collectives: none -> 2.5 us  [shards(): haloq = lax.all_gather(q, 'dom', axis_index_groups=pairs)]
    ppermute x3 -> x4, waiting for transfers between devices: 0.01 us -> 1.94 us  [the longest x1 1.93 us: shards(): halor = lax.ppermute(r, 'dom', across)]
    all_gather x8 -> x7, blocking collectives: 40.3 us -> 42.2 us  [exchange(): haloq = lax.all_gather(q, 'dom', axis_index_groups=pairs)]
  transfers between devices with their start and end apart: 11 -> 11, of which waited for: 0 -> 1; matrix products, arithmetic and copies ran while one was open for 0% -> 0% of each run, Pallas kernels for 27% -> 17%
where the time goes in v1:
time: 106 us
  blocking collectives  44.7 us (42%)
  starting transfers between devices  28 us (26%)
  Pallas kernels  27.2 us (26%)
  between operations  2.33 us (2%)
  waiting for transfers between devices  1.96 us (2%)
  local copies, waits for them, and re-layouts  1.31 us (1%)
    all_gather x7, blocking collectives, exchange(): haloq = lax.all_gather(q, 'dom', axis_index_groups=pairs)  42.2 us
    ppermute x7, starting transfers between devices, exchange(): halor = lax.ppermute(r, 'dom', across)  15.3 us
    pallas_call x7, Pallas kernels, shards(): call(rows_body(step, step == 0), (s(n, 2 * d), s(n, 2 * d)), [VM] * 9, st...  12.1 us
    pallas_call x7, Pallas kernels, shards(): call(send_body(step, step == 0), (s(2 * blk, 2 * d), s(blk, 2 * d), s(blk...  8.24 us
    ppermute x3, starting transfers between devices, fetch(): lax.ppermute(own, 'section', [(i, i + k) for i in range(sections - k)])  7.9 us
    ppermute x1, starting transfers between devices, shards(): halor = lax.ppermute(r, 'dom', across)  4.8 us
    all_gather x1, blocking collectives, shards(): haloq = lax.all_gather(q, 'dom', axis_index_groups=pairs)  2.5 us
    pallas_call x1, Pallas kernels, shards(): prep(meta, row_blocks, col_blocks, in_hbm(features), in_hbm(adjacency))  2.47 us
  transfers between devices with their start and end apart: 11, of which 1 were waited for; matrix products, arithmetic and copies ran while one was open for 0% of the time, Pallas kernels for 17%

profile of v1, /device:TPU:33, one launch (start us, length us, event | category | flops | bytes accessed | tf_op | source)
XLA Modules:
  0.0 105.6 jit_solution(13673605153401335129)
XLA Ops:
  2.0 1.7 %shard_map.128 = (bf16[1040,128]{1,0:T(8,128)(2,1)S(1)}, bf16[128,256]{1,0:T(8,128)(2,1)S(1)}, bf16[128,256]{1,0:T(8,128)(2,1)S(1)}) custom-call(s32[4]{0:T(128)S(1)} %pad_add_fusion.meta, bf16[2,1024,128]{2,1,0:T(8,128)(2,1)} %x.3, bf16[2,128,128]{2,1,0:T(8,128)(2,1)} %wm.1, bf16[2,256,128]{2,1,0:T(8,128)(2,1)} %wh.1, bf16[2,128]{1,0:T(2,128)(2,1)} %bh.1, ...), custom_call_target="tpu_custom_call" | custom-call | tf_op jit(solution)/shard_map/pallas_call | solution.py:254
  3.8 4.4 %collective-permute-start.1 = (bf16[1040,128]{1,0:T(8,128)(2,1)S(1)}, bf16[1040,128]{1,0:T(8,128)(2,1)S(1)}, u32[]{:S(2)}, u32[]{:S(2)}) collective-permute-start(bf16[1040,128]{1,0:T(8,128)(2,1)S(1)} %get-tuple-element.74.nxt.pack), channel_id=1, source_target_pairs={{0,384},{1,385},{2,386},{3,387},{4,388},{5,389},{6,390},{7,391},{8... | collective-permute-start | bytes 798728 | tf_op jit(solution)/shard_map/ppermute | solution.py:251
  9.5 2.5 %shard_map.127 = (bf16[1024,256]{1,0:T(8,128)(2,1)S(1)}, bf16[256,256]{1,0:T(8,128)(2,1)S(1)}, bf16[1024,1280]{1,0:T(8,128)(2,1)S(1)}, bf16[256,1280]{1,0:T(8,12...) custom-call(s32[4]{0:T(128)S(1)} %pad_add_fusion.meta, ...), custom_call_target="tpu_custom_call" | custom-call | tf_op jit(solution)/shard_map/pallas_call | solution.py:292
  12.0 2.5 %all-gather = bf16[256,256]{1,0:T(8,128)(2,1)S(1)} all-gather(bf16[128,256]{1,0:T(8,128)(2,1)S(1)} %get-tuple-element.60), channel_id=2, replica_groups={{0,1},{2,3},{4,5},{6,7},{8,9},{10,11},{12,13},{14,15},{16,17},{18,19},{..., dimensions={0}, use_global_device_ids=true | all-gather | bytes 196608 | tf_op jit(solution)/shard_map/all_gather | solution.py:294
  15.8 2.2 %collective-permute-start.6 = (bf16[1040,128]{1,0:T(8,128)(2,1)S(1)}, bf16[1040,128]{1,0:T(8,128)(2,1)S(1)}, u32[]{:S(2)}, u32[]{:S(2)}) collective-permute-start(bf16[1040,128]{1,0:T(8,128)(2,1)S(1)} %get-tuple-element.74.nxt.pack), channel_id=1, source_target_pairs={{0,128},{128,256},{256,384},{1,129},{129,257},{257,385},{2,130},{1... | collective-permute-start | bytes 798728 | tf_op jit(solution)/shard_map/ppermute | solution.py:251
  18.0 4.8 %collective-permute-start = (bf16[128,256]{1,0:T(8,128)(2,1)S(1)}, bf16[128,256]{1,0:T(8,128)(2,1)S(1)}, u32[]{:S(2)}, u32[]{:S(2)}) collective-permute-start(bf16[128,256]{1,0:T(8,128)(2,1)S(1)} %get-tuple-element.62), channel_id=1, source_target_pairs={{1,2},{3,4},{5,6},{7,8},{9,10},{11,12},{13,14},{15,16},{17,18},{19... | collective-permute-start | bytes 196616 | tf_op jit(solution)/shard_map/ppermute | solution.py:271
  22.8 1.9 %collective-permute-done.halor = bf16[128,256]{1,0:T(8,128)(2,1)S(1)} collective-permute-done((bf16[128,256]{1,0:T(8,128)(2,1)S(1)}, bf16[128,256]{1,0:T(8,128)(2,1)S(1)}, u32[]{:S(2)}, u32[]{:S(2)}) %collective-permute-start) | collective-permute-done | bytes 65568 | tf_op jit(solution)/shard_map/ppermute | solution.py:271
  26.2 3.6 %collective-permute-start.2 = (bf16[128,256]{1,0:T(8,128)(2,1)S(1)}, bf16[128,256]{1,0:T(8,128)(2,1)S(1)}, u32[]{:S(2)}, u32[]{:S(2)}) collective-permute-start(bf16[128,256]{1,0:T(8,128)(2,1)S(1)} %get-tuple-element.73), channel_id=1, source_target_pairs={{1,2},{3,4},{5,6},{7,8},{9,10},{11,12},{13,14},{15,16},{17,18},{19... | collective-permute-start | bytes 196616 | tf_op jit(solution)/shard_map/ppermute | solution.py:246
  31.6 11.0 %all-gather.1 = bf16[256,256]{1,0:T(8,128)(2,1)S(1)} all-gather(bf16[128,256]{1,0:T(8,128)(2,1)S(1)} %get-tuple-element.72), channel_id=3, replica_groups={{0,1},{2,3},{4,5},{6,7},{8,9},{10,11},{12,13},{14,15},{16,17},{18,19},{..., dimensions={0}, use_global_device_ids=true | all-gather | bytes 196608 | tf_op jit(solution)/shard_map/all_gather | solution.py:247
  43.7 1.9 %collective-permute-start.4 = (bf16[128,256]{1,0:T(8,128)(2,1)S(1)}, bf16[128,256]{1,0:T(8,128)(2,1)S(1)}, u32[]{:S(2)}, u32[]{:S(2)}) collective-permute-start(bf16[128,256]{1,0:T(8,128)(2,1)S(1)} %get-tuple-element.79), channel_id=1, source_target_pairs={{1,2},{3,4},{5,6},{7,8},{9,10},{11,12},{13,14},{15,16},{17,18},{19... | collective-permute-start | bytes 196616 | tf_op jit(solution)/shard_map/ppermute | solution.py:246
  47.4 5.2 %all-gather.2 = bf16[256,256]{1,0:T(8,128)(2,1)S(1)} all-gather(bf16[128,256]{1,0:T(8,128)(2,1)S(1)} %get-tuple-element.78), channel_id=4, replica_groups={{0,1},{2,3},{4,5},{6,7},{8,9},{10,11},{12,13},{14,15},{16,17},{18,19},{..., dimensions={0}, use_global_device_ids=true | all-gather | bytes 196608 | tf_op jit(solution)/shard_map/all_gather | solution.py:247
  53.7 1.9 %collective-permute-start.5 = (bf16[128,256]{1,0:T(8,128)(2,1)S(1)}, bf16[128,256]{1,0:T(8,128)(2,1)S(1)}, u32[]{:S(2)}, u32[]{:S(2)}) collective-permute-start(bf16[128,256]{1,0:T(8,128)(2,1)S(1)} %get-tuple-element.84), channel_id=1, source_target_pairs={{1,2},{3,4},{5,6},{7,8},{9,10},{11,12},{13,14},{15,16},{17,18},{19... | collective-permute-start | bytes 196616 | tf_op jit(solution)/shard_map/ppermute | solution.py:246
  55.6 1.7 %shard_map.134 = (bf16[1024,256]{1,0:T(8,128)(2,1)S(1)}, bf16[1024,256]{1,0:T(8,128)(2,1)S(1)}) custom-call(bf16[1024,256]{1,0:T(8,128)(2,1)S(1)} %get-tuple-element.75.h, bf16[1024,256]{1,0:T(8,128)(2,1)S(1)} %get-tuple-element.76.m, bf16[2,128,256]{2,1,0:T(8,128)(2,1)S(1)} %get-tuple-element.58.pick, bf16[2,128,256]{2,1,0:T(8,128)(2,1)S(1)} %bitcast.30, ...), custom_call_target="tpu_custom_call" | custom-call | tf_op jit(solution)/shard_map/pallas_call | solution.py:329
  57.4 5.2 %all-gather.3 = bf16[256,256]{1,0:T(8,128)(2,1)S(1)} all-gather(bf16[128,256]{1,0:T(8,128)(2,1)S(1)} %get-tuple-element.83), channel_id=5, replica_groups={{0,1},{2,3},{4,5},{6,7},{8,9},{10,11},{12,13},{14,15},{16,17},{18,19},{..., dimensions={0}, use_global_device_ids=true | all-gather | bytes 196608 | tf_op jit(solution)/shard_map/all_gather | solution.py:247
  63.7 1.9 %collective-permute-start.7 = (bf16[128,256]{1,0:T(8,128)(2,1)S(1)}, bf16[128,256]{1,0:T(8,128)(2,1)S(1)}, u32[]{:S(2)}, u32[]{:S(2)}) collective-permute-start(bf16[128,256]{1,0:T(8,128)(2,1)S(1)} %get-tuple-element.89), channel_id=1, source_target_pairs={{1,2},{3,4},{5,6},{7,8},{9,10},{11,12},{13,14},{15,16},{17,18},{19... | collective-permute-start | bytes 196616 | tf_op jit(solution)/shard_map/ppermute | solution.py:246
  65.7 1.7 %shard_map.136 = (bf16[1024,256]{1,0:T(8,128)(2,1)S(1)}, bf16[1024,256]{1,0:T(8,128)(2,1)S(1)}) custom-call(bf16[1024,256]{1,0:T(8,128)(2,1)S(1)} %get-tuple-element.80.h, bf16[1024,256]{1,0:T(8,128)(2,1)S(1)} %get-tuple-element.81.m, bf16[2,128,256]{2,1,0:T(8,128)(2,1)S(1)} %get-tuple-element.58.pick, bf16[2,128,256]{2,1,0:T(8,128)(2,1)S(1)} %bitcast.24, ...), custom_call_target="tpu_custom_call" | custom-call | tf_op jit(solution)/shard_map/pallas_call | solution.py:329
  67.4 5.2 %all-gather.4 = bf16[256,256]{1,0:T(8,128)(2,1)S(1)} all-gather(bf16[128,256]{1,0:T(8,128)(2,1)S(1)} %get-tuple-element.88), channel_id=6, replica_groups={{0,1},{2,3},{4,5},{6,7},{8,9},{10,11},{12,13},{14,15},{16,17},{18,19},{..., dimensions={0}, use_global_device_ids=true | all-gather | bytes 196608 | tf_op jit(solution)/shard_map/all_gather | solution.py:247
  73.7 2.1 %collective-permute-start.8 = (bf16[128,256]{1,0:T(8,128)(2,1)S(1)}, bf16[128,256]{1,0:T(8,128)(2,1)S(1)}, u32[]{:S(2)}, u32[]{:S(2)}) collective-permute-start(bf16[128,256]{1,0:T(8,128)(2,1)S(1)} %get-tuple-element.94), channel_id=1, source_target_pairs={{1,2},{3,4},{5,6},{7,8},{9,10},{11,12},{13,14},{15,16},{17,18},{19... | collective-permute-start | bytes 196616 | tf_op jit(solution)/shard_map/ppermute | solution.py:246
  77.6 5.2 %all-gather.5 = bf16[256,256]{1,0:T(8,128)(2,1)S(1)} all-gather(bf16[128,256]{1,0:T(8,128)(2,1)S(1)} %get-tuple-element.93), channel_id=7, replica_groups={{0,1},{2,3},{4,5},{6,7},{8,9},{10,11},{12,13},{14,15},{16,17},{18,19},{..., dimensions={0}, use_global_device_ids=true | all-gather | bytes 196608 | tf_op jit(solution)/shard_map/all_gather | solution.py:247
  83.9 1.9 %collective-permute-start.9 = (bf16[128,256]{1,0:T(8,128)(2,1)S(1)}, bf16[128,256]{1,0:T(8,128)(2,1)S(1)}, u32[]{:S(2)}, u32[]{:S(2)}) collective-permute-start(bf16[128,256]{1,0:T(8,128)(2,1)S(1)} %get-tuple-element.99), channel_id=1, source_target_pairs={{1,2},{3,4},{5,6},{7,8},{9,10},{11,12},{13,14},{15,16},{17,18},{19... | collective-permute-start | bytes 196616 | tf_op jit(solution)/shard_map/ppermute | solution.py:246
  87.6 5.1 %all-gather.6 = bf16[256,256]{1,0:T(8,128)(2,1)S(1)} all-gather(bf16[128,256]{1,0:T(8,128)(2,1)S(1)} %get-tuple-element.98), channel_id=8, replica_groups={{0,1},{2,3},{4,5},{6,7},{8,9},{10,11},{12,13},{14,15},{16,17},{18,19},{..., dimensions={0}, use_global_device_ids=true | all-gather | bytes 196608 | tf_op jit(solution)/shard_map/all_gather | solution.py:247
  94.3 1.9 %collective-permute-start.10 = (bf16[128,256]{1,0:T(8,128)(2,1)S(1)}, bf16[128,256]{1,0:T(8,128)(2,1)S(1)}, u32[]{:S(2)}, u32[]{:S(2)}) collective-permute-start(bf16[128,256]{1,0:T(8,128)(2,1)S(1)} %get-tuple-element.104), channel_id=1, source_target_pairs={{1,2},{3,4},{5,6},{7,8},{9,10},{11,12},{13,14},{15,16},{17,18},{19... | collective-permute-start | bytes 196616 | tf_op jit(solution)/shard_map/ppermute | solution.py:246
  97.9 5.2 %all-gather.7 = bf16[256,256]{1,0:T(8,128)(2,1)S(1)} all-gather(bf16[128,256]{1,0:T(8,128)(2,1)S(1)} %get-tuple-element.103), channel_id=9, replica_groups={{0,1},{2,3},{4,5},{6,7},{8,9},{10,11},{12,13},{14,15},{16,17},{18,19},{..., dimensions={0}, use_global_device_ids=true | all-gather | bytes 196608 | tf_op jit(solution)/shard_map/all_gather | solution.py:247
  103.2 2.3 %shard_map.144 = bf16[2,1024,128]{2,1,0:T(8,128)(2,1)} custom-call(bf16[1024,256]{1,0:T(8,128)(2,1)S(1)} %get-tuple-element.100.h, bf16[1024,256]{1,0:T(8,128)(2,1)S(1)} %get-tuple-element.101.m, bf16[2,128,256]{2,1,0:T(8,128)(2,1)S(1)} %get-tuple-element.58.pick, bf16[2,128,256]{2,1,0:T(8,128)(2,1)S(1)} %bitcast.33, ...), custom_call_target="tpu_custom_call" | custom-call | tf_op jit(solution)/shard_map/pallas_call | solution.py:312
  (29 shorter events, 19.9 us)
Async XLA Ops:
  3.8 21.0 %collective-permute-start.1 = (bf16[1040,128]{1,0:T(8,128)(2,1)S(1)}, bf16[1040,128]{1,0:T(8,128)(2,1)S(1)}, u32[]{:S(2)}, u32[]{:S(2)}) collective-permute-start(bf16[1040,128]{1,0:T(8,128)(2,1)S(1)} %get-tuple-element.74.nxt.pack), channel_id=1, source_target_pairs={{0,384},{1,385},{2,386},{3,387},{4,388},{5,389},{6,390},{7,391},{8... | collective-permute-start | bytes 798728 | tf_op jit(solution)/shard_map/ppermute | solution.py:251
  8.2 0.7 copy-start
  8.8 0.7 copy-start.1
  14.5 28.1 %collective-permute-start.3 = (bf16[1040,128]{1,0:T(8,128)(2,1)S(1)}, bf16[1040,128]{1,0:T(8,128)(2,1)S(1)}, u32[]{:S(2)}, u32[]{:S(2)}) collective-permute-start(bf16[1040,128]{1,0:T(8,128)(2,1)S(1)} %get-tuple-element.74.nxt.pack), channel_id=1, source_target_pairs={{0,256},{128,384},{1,257},{129,385},{2,258},{130,386},{3,259},{131... | collective-permute-start | bytes 798728 | tf_op jit(solution)/shard_map/ppermute | solution.py:251
  15.8 46.8 %collective-permute-start.6 = (bf16[1040,128]{1,0:T(8,128)(2,1)S(1)}, bf16[1040,128]{1,0:T(8,128)(2,1)S(1)}, u32[]{:S(2)}, u32[]{:S(2)}) collective-permute-start(bf16[1040,128]{1,0:T(8,128)(2,1)S(1)} %get-tuple-element.74.nxt.pack), channel_id=1, source_target_pairs={{0,128},{128,256},{256,384},{1,129},{129,257},{257,385},{2,130},{1... | collective-permute-start | bytes 798728 | tf_op jit(solution)/shard_map/ppermute | solution.py:251
  18.0 6.7 %collective-permute-start = (bf16[128,256]{1,0:T(8,128)(2,1)S(1)}, bf16[128,256]{1,0:T(8,128)(2,1)S(1)}, u32[]{:S(2)}, u32[]{:S(2)}) collective-permute-start(bf16[128,256]{1,0:T(8,128)(2,1)S(1)} %get-tuple-element.62), channel_id=1, source_target_pairs={{1,2},{3,4},{5,6},{7,8},{9,10},{11,12},{13,14},{15,16},{17,18},{19... | collective-permute-start | bytes 196616 | tf_op jit(solution)/shard_map/ppermute | solution.py:271
  26.2 16.4 %collective-permute-start.2 = (bf16[128,256]{1,0:T(8,128)(2,1)S(1)}, bf16[128,256]{1,0:T(8,128)(2,1)S(1)}, u32[]{:S(2)}, u32[]{:S(2)}) collective-permute-start(bf16[128,256]{1,0:T(8,128)(2,1)S(1)} %get-tuple-element.73), channel_id=1, source_target_pairs={{1,2},{3,4},{5,6},{7,8},{9,10},{11,12},{13,14},{15,16},{17,18},{19... | collective-permute-start | bytes 196616 | tf_op jit(solution)/shard_map/ppermute | solution.py:246
  43.7 8.9 %collective-permute-start.4 = (bf16[128,256]{1,0:T(8,128)(2,1)S(1)}, bf16[128,256]{1,0:T(8,128)(2,1)S(1)}, u32[]{:S(2)}, u32[]{:S(2)}) collective-permute-start(bf16[128,256]{1,0:T(8,128)(2,1)S(1)} %get-tuple-element.79), channel_id=1, source_target_pairs={{1,2},{3,4},{5,6},{7,8},{9,10},{11,12},{13,14},{15,16},{17,18},{19... | collective-permute-start | bytes 196616 | tf_op jit(solution)/shard_map/ppermute | solution.py:246
  53.7 8.9 %collective-permute-start.5 = (bf16[128,256]{1,0:T(8,128)(2,1)S(1)}, bf16[128,256]{1,0:T(8,128)(2,1)S(1)}, u32[]{:S(2)}, u32[]{:S(2)}) collective-permute-start(bf16[128,256]{1,0:T(8,128)(2,1)S(1)} %get-tuple-element.84), channel_id=1, source_target_pairs={{1,2},{3,4},{5,6},{7,8},{9,10},{11,12},{13,14},{15,16},{17,18},{19... | collective-permute-start | bytes 196616 | tf_op jit(solution)/shard_map/ppermute | solution.py:246
  63.7 8.9 %collective-permute-start.7 = (bf16[128,256]{1,0:T(8,128)(2,1)S(1)}, bf16[128,256]{1,0:T(8,128)(2,1)S(1)}, u32[]{:S(2)}, u32[]{:S(2)}) collective-permute-start(bf16[128,256]{1,0:T(8,128)(2,1)S(1)} %get-tuple-element.89), channel_id=1, source_target_pairs={{1,2},{3,4},{5,6},{7,8},{9,10},{11,12},{13,14},{15,16},{17,18},{19... | collective-permute-start | bytes 196616 | tf_op jit(solution)/shard_map/ppermute | solution.py:246
  73.7 9.1 %collective-permute-start.8 = (bf16[128,256]{1,0:T(8,128)(2,1)S(1)}, bf16[128,256]{1,0:T(8,128)(2,1)S(1)}, u32[]{:S(2)}, u32[]{:S(2)}) collective-permute-start(bf16[128,256]{1,0:T(8,128)(2,1)S(1)} %get-tuple-element.94), channel_id=1, source_target_pairs={{1,2},{3,4},{5,6},{7,8},{9,10},{11,12},{13,14},{15,16},{17,18},{19... | collective-permute-start | bytes 196616 | tf_op jit(solution)/shard_map/ppermute | solution.py:246
  83.9 8.7 %collective-permute-start.9 = (bf16[128,256]{1,0:T(8,128)(2,1)S(1)}, bf16[128,256]{1,0:T(8,128)(2,1)S(1)}, u32[]{:S(2)}, u32[]{:S(2)}) collective-permute-start(bf16[128,256]{1,0:T(8,128)(2,1)S(1)} %get-tuple-element.99), channel_id=1, source_target_pairs={{1,2},{3,4},{5,6},{7,8},{9,10},{11,12},{13,14},{15,16},{17,18},{19... | collective-permute-start | bytes 196616 | tf_op jit(solution)/shard_map/ppermute | solution.py:246
  94.3 8.9 %collective-permute-start.10 = (bf16[128,256]{1,0:T(8,128)(2,1)S(1)}, bf16[128,256]{1,0:T(8,128)(2,1)S(1)}, u32[]{:S(2)}, u32[]{:S(2)}) collective-permute-start(bf16[128,256]{1,0:T(8,128)(2,1)S(1)} %get-tuple-element.104), channel_id=1, source_target_pairs={{1,2},{3,4},{5,6},{7,8},{9,10},{11,12},{13,14},{15,16},{17,18},{19... | collective-permute-start | bytes 196616 | tf_op jit(solution)/shard_map/ppermute | solution.py:246

commit v2 on v1

v2 whole, which is shorter than its diff:
```python
import jax
import jax.numpy as jnp
from jax import lax
from jax.experimental import pallas as pl
from jax.experimental.pallas import tpu as pltpu
from jax.sharding import PartitionSpec as P


BF = jnp.bfloat16
F32 = jnp.float32
VM = pl.BlockSpec(memory_space=pltpu.VMEM)
SM = pl.BlockSpec(memory_space=pltpu.SMEM)
HB = pl.BlockSpec(memory_space=pltpu.HBM)
CHUNK = 256


def call(body, outs, ins, scratch=(), room=8, spaces=None):
    return pl.pallas_call(
        body,
        out_shape=outs,
        in_specs=ins,
        out_specs=spaces or jax.tree.map(lambda _: VM, outs),
        scratch_shapes=list(scratch),
        compiler_params=pltpu.CompilerParams(vmem_limit_bytes=room << 20),
    )


def in_hbm(*arrays):
    return [pltpu.with_memory_space_constraint(a, pltpu.HBM) for a in arrays]


def dot(a, b):
    return jnp.dot(a, b, preferred_element_type=F32)


def silu_of_twice(u):
    return (u + u * jnp.tanh(u)).astype(BF)


def twice(w):
    zero = jnp.zeros_like(w)
    return jnp.concatenate(
        [jnp.concatenate([w, zero], axis=1), jnp.concatenate([zero, w], axis=1)], axis=0
    )


def flags(cond, shape):
    return jnp.full(shape, jnp.where(cond, jnp.float32(1), jnp.float32(0)), F32).astype(BF)


def choose(pick, a, b):
    return a * pick[0] + b * pick[1]


def fetch_all(pairs, sem):
    copies = [pltpu.make_async_copy(src, dst, sem.at[i]) for i, (src, dst) in enumerate(pairs)]
    for copy in copies:
        copy.start()
    return copies


def parity():
    return lax.axis_index("dom") % 2


def to_partners(up, down):
    odd = parity() == 1
    return jnp.where(odd, down, up), jnp.where(odd, up, down)


def exchange_of(near, far, block, back):
    moved = jnp.where(far == near, 0, jnp.where(far == 0, near, far))

    def first(b):
        return jnp.where(b == near, 0, jnp.where(b == 0, near, b))

    def second(b):
        swapped = jnp.where(b == moved, 1, jnp.where(b == 1, moved, b))
        return jnp.where(moved == 0, b, swapped)

    return first(second(block)) if back else second(first(block))


def pack_body(wm, wh, bh, wo, bo, gain, out, am, ah, ao, vb, vo, vg, sem):
    d = wm.shape[2]
    for copy in fetch_all([(wm, am), (wh, ah), (wo, ao), (bh, vb), (bo, vo), (gain, vg)], sem):
        copy.wait()
    for i in range(2):
        out[i * d : (i + 1) * d] = (am[i].astype(F32) * 0.5).astype(BF)
        at = 2 * d + i * 2 * d
        out[at : at + 2 * d] = (ah[i].astype(F32) * 0.5).astype(BF)
        w = ao[i].astype(F32)
        at = 6 * d + i * d
        out[at : at + d] = (w - jnp.mean(w, axis=1, keepdims=True)).astype(BF)
    b = vo[...].astype(F32)
    b = b - jnp.mean(b, axis=1, keepdims=True)
    high = b.astype(BF).astype(F32)
    pad = jnp.zeros((8, d), F32)
    vectors = [vb[...].astype(F32) * 0.5, high, b - high, vg[...].astype(F32), pad]
    out[8 * d :] = jnp.concatenate(vectors, axis=0).astype(BF)


def blocks_body(count, up, down, rows, cols, x, adj, q, pay, sr, sk, xs, av, sem):
    blk, d = av.shape[1], av.shape[2]
    copies = fetch_all([(rows, sr), (cols, sk), (adj, av)], sem)
    blocks = to_partners(up[0], down[0])
    for i, block in enumerate(blocks):
        at = pl.ds(pl.multiple_of(block * blk, blk), blk)
        copies.append(pltpu.make_async_copy(x.at[:, at, :], xs.at[i], sem.at[3 + i]))
        copies[-1].start()
    for copy in copies:
        copy.wait()
    for i, (block, dst) in enumerate(zip(blocks, (q, pay))):
        row = block * blk + lax.broadcasted_iota(jnp.int32, (blk, d), 0)
        keep = jnp.where(row < count[0], jnp.float32(1), jnp.float32(0)).astype(BF)
        for m in range(2):
            dst[:blk, m * d : (m + 1) * d] = xs[i, m] * keep
    pay[blk:, d:] = keep
    far_col = jnp.where(parity() == 1, 9, 8)
    seen = jnp.zeros((blk, d), F32)
    for k in range(av.shape[0]):
        hit = (sr[k] == blocks[1]) & (sk[k] == far_col)
        seen = seen + av[k].astype(F32) * jnp.where(hit, jnp.float32(1), jnp.float32(0))
    pay[blk:, :d] = seen.astype(BF)


def prep_body(
    count, up, down, rows, cols, x, adj,
    h, dense, df, mask, pick, fpick, fsel,
    sr, sk, xv, av, acc, sem,
):
    n, d = xv.shape[1], xv.shape[2]
    blk = av.shape[1]
    last = n // blk
    copies = fetch_all([(rows, sr), (cols, sk), (x, xv), (adj, av)], sem)
    acc[...] = jnp.zeros_like(acc)
    wide = (blk, 2 * d)
    dom = lax.axis_index("dom")
    odd = parity() == 1
    alone = (dom == 0) | (dom == lax.axis_size("dom") - 1)
    pick[0] = flags(odd, wide)
    pick[1] = flags(jnp.logical_not(odd), wide)
    fpick[0] = flags(jnp.logical_not(odd | alone), wide)
    fpick[1] = flags(odd & jnp.logical_not(alone), wide)
    near, far = to_partners(up[0], down[0])
    fsel[0] = flags(near == far, wide)
    fsel[1] = flags(near != far, wide)
    copies[2].wait()
    for b in range(last):
        at = pl.ds(pl.multiple_of(exchange_of(near, far, b, False) * blk, blk), blk)
        row = b * blk + lax.broadcasted_iota(jnp.int32, wide, 0)
        keep = jnp.where(row < count[0], jnp.float32(1), jnp.float32(0)).astype(BF)
        mask[at, :] = keep
        both = [xv[m, b * blk : (b + 1) * blk] for m in range(2)]
        h[at, :] = jnp.concatenate(both, axis=1) * keep
    for copy in copies[:2] + copies[3:]:
        copy.wait()
    for k in range(av.shape[0]):
        c = sk[k]
        halo = jnp.where(odd, c, 2 * last + 1 - c)
        at = (
            exchange_of(near, far, sr[k], False),
            jnp.where(c < last, exchange_of(near, far, c, False), halo),
        )
        acc[at] = acc[at] + av[k].astype(F32)
    for r in range(last):
        for c in range(last + 2):
            dense[r * blk : (r + 1) * blk, c * blk : (c + 1) * blk] = acc[r, c].astype(BF)
    at = pl.ds(pl.multiple_of(jnp.where(near == far, 0, 1) * blk, blk), blk)
    df[...] = dense[at, :]


def message_weight(pack, i):
    d = pack.shape[1]
    return twice(pack[i * d : (i + 1) * d])


def first_body(h, pick, haloq, halor, pack, m, halo):
    w = message_weight(pack, 0)
    m[...] = silu_of_twice(dot(h[...], w))
    blk = haloq.shape[1]
    both = jnp.concatenate([choose(pick, haloq[0], haloq[1]), halor[:blk]], axis=0)
    halo[...] = silu_of_twice(dot(both, w))


def own_rows(h, m, halo, dense, mask):
    n = m.shape[0]

    def aggregate(at):
        return lambda: dot(dense[at, :n], m[...]) + dot(dense[at, n:], halo)

    chunks = [slice(r, r + CHUNK) for r in range(0, n, CHUNK)]
    return [(at, h.at[at], aggregate(at), mask.at[at]) for at in chunks]


def layer(chunks, pack, i, agg, hidden, c):
    d = pack.shape[1]
    wh = pack[2 * d + i * 2 * d : 2 * d + (i + 1) * 2 * d]
    wo = twice(pack[6 * d + i * d : 6 * d + (i + 1) * d])
    v = pack[8 * d :].astype(F32)

    def row(j):
        r = v[j + i : j + i + 1]
        return jnp.concatenate([r, r], axis=1)

    for at, _, aggregate, _ in chunks:
        agg[at] = aggregate().astype(BF)
    b = row(0)
    for at, h, _, _ in chunks:
        pre = [
            dot(jnp.concatenate([h[:, s : s + d], agg[at, s : s + d]], axis=1), wh) for s in (0, d)
        ]
        hidden[at] = silu_of_twice(jnp.concatenate(pre, axis=1) + b)
    b = row(2) + row(4)
    for at, _, _, _ in chunks:
        c[at] = dot(hidden[at], wo) + b
    mean = twice(jnp.full((d, d), 1.0 / d, BF))
    gain = row(6)
    for at, h, _, mask in chunks:
        now = c[at]
        var = dot((now * now).astype(BF), mean)
        new = (h[...].astype(F32) + now * lax.rsqrt(var + 1e-05) * gain).astype(BF) * mask[...]
        yield at, new


def send_messages(new_h, new_m, outq, nxt, i):
    w = message_weight(nxt, i)
    for r in range(0, new_m.shape[0], CHUNK):
        at = slice(r, r + CHUNK)
        out = silu_of_twice(dot(new_h[at], w))
        new_m[at] = out
        if r == 0:
            outq[...] = out[: outq.shape[0]]


def far_block(fsel, ref, blk):
    return choose(fsel, ref[:blk], ref[blk : 2 * blk])


def second_body(step, given, tail):
    def body(h, m, pick, haloq, halor, dense, df, mask, fsel, pack, nxt, *rest):
        new_h, new_m, outq = rest[:3]
        agg, hidden, c = rest[-3:]
        blk = outq.shape[0]
        if given:
            halo = halor[...]
        else:
            near = choose(pick, haloq[0], haloq[1])
            halo = jnp.concatenate([near, halor[...]], axis=0)
        for at, new in layer(own_rows(h, m, halo, dense, mask), pack, step % 2, agg, hidden, c):
            new_h[at] = new
        send_messages(new_h, new_m, outq, nxt, (step + 1) % 2)
        if tail:
            rest[3][...] = far_block(fsel, new_m, blk)
        else:
            rest[3][...] = far_block(fsel, new_h, blk)
            rest[4][...] = dot(df[:, : new_m.shape[0]], new_m[...])

    return body


def pay_body(pick, haloq, df, far_h, part, pay):
    blk = far_h.shape[0]
    n = df.shape[1] - 2 * blk
    near = choose(pick, haloq[0], haloq[1])
    pay[:blk] = far_h[...]
    pay[blk:] = (part[...] + dot(df[:, n : n + blk], near)).astype(BF)


def first_of_two_body(step):
    def body(h, m, pick, haloq, fpick, far, dense, mask, fsel, seen, pack, nxt, *rest):
        new_h, new_m, outq, far_m, agg, hidden, c, hx, mx = rest
        n = m.shape[0]
        blk, d2 = hx.shape
        d = d2 // 2
        hx[...] = choose(fpick, far[0, :blk], far[1, :blk])
        part = choose(fpick, far[0, blk:], far[1, blk:])
        view = seen[blk:]
        mx[...] = jnp.concatenate([view[:, d:], view[:, d:]], axis=1)
        theirs = silu_of_twice(dot(hx[...], message_weight(pack, step % 2)))
        halo = jnp.concatenate([choose(pick, haloq[0], haloq[1]), theirs], axis=0)
        mine = far_block(fsel, m, blk)
        chunks = own_rows(h, m, halo, dense, mask)
        chunks.append(
            (slice(n, n + blk), hx, lambda: part.astype(F32) + dot(view[:, :d], mine), mx)
        )
        for at, new in layer(chunks, pack, step % 2, agg, hidden, c):
            if at.start < n:
                new_h[at] = new
            else:
                hx[...] = new
        send_messages(new_h, new_m, outq, nxt, (step + 1) % 2)
        far_m[...] = silu_of_twice(dot(hx[...], message_weight(nxt, (step + 1) % 2)))

    return body


def last_body(step):
    def body(h, m, pick, haloq, halor, dense, mask, pack, up, down, out, *rest):
        agg, hidden, c, stage, sem = rest
        d = pack.shape[1]
        blk = halor.shape[0]
        halo = jnp.concatenate([choose(pick, haloq[0], haloq[1]), halor[...]], axis=0)
        near, far = to_partners(up[0], down[0])
        copies = []
        for at, new in layer(own_rows(h, m, halo, dense, mask), pack, step % 2, agg, hidden, c):
            stage[0, at] = new[:, :d]
            stage[1, at] = new[:, d:]
            for b in range(at.start // blk, at.stop // blk):
                to = pl.multiple_of(exchange_of(near, far, b, True) * blk, blk)
                copies.append(
                    pltpu.make_async_copy(
                        stage.at[:, b * blk : (b + 1) * blk, :],
                        out.at[:, pl.ds(to, blk), :],
                        sem.at[b],
                    )
                )
                copies[-1].start()
        for copy in copies:
            copy.wait()

    return body


def shards(
    features,
    counts,
    row_blocks,
    col_blocks,
    adjacency,
    send_up,
    send_down,
    w_message,
    w_hidden,
    b_hidden,
    w_out,
    b_out,
    gain,
):
    n, d = features.shape[1:]
    blk = adjacency.shape[1]
    doms = lax.axis_size("dom")
    sections = lax.axis_size("section")
    layers = w_message.shape[0]
    steps = layers * sections
    near_pairs = [[i, i + 1] for i in range(0, doms, 2)]
    far_pairs = [[i, i + 1] for i in range(1, doms - 1, 2)]
    across = [(a, b) for a, b in far_pairs] + [(b, a) for a, b in far_pairs]
    far_pairs = far_pairs + [[0, doms - 1]]

    def s(*shape, dtype=BF):
        return jax.ShapeDtypeStruct(shape, dtype)

    def near_gather(q):
        return lax.all_gather(q, "dom", axis_index_groups=near_pairs)

    def fetch(own, k):
        return lax.ppermute(own, "section", [(i, i + k) for i in range(sections - k)])

    def integers(*sizes):
        return [pltpu.SMEM((k,), jnp.int32) for k in sizes]

    wide = s(blk, 2 * d)
    rows = s(n, 2 * d)
    two = s(2, blk, 2 * d)
    span = n + 2 * blk
    count_k = adjacency.shape[0]
    vec = pltpu.VMEM((layers, d), BF)
    weights = in_hbm(w_message, w_hidden, b_hidden, w_out, b_out, gain)
    own = call(
        pack_body,
        s(layers * 4 * d + 16, d),
        [HB] * 6,
        [
            pltpu.VMEM((layers, d, d), BF),
            pltpu.VMEM((layers, 2 * d, d), BF),
            pltpu.VMEM((layers, d, d), BF),
            vec,
            vec,
            vec,
            pltpu.SemaphoreType.DMA((6,)),
        ],
    )(*weights)
    packs = [fetch(own, sections - 1)]
    graph = [counts, send_up, send_down, *in_hbm(row_blocks, col_blocks, features, adjacency)]
    q, pay = call(
        blocks_body,
        (wide, s(2 * blk, 2 * d)),
        [SM] * 3 + [HB] * 4,
        integers(count_k, count_k)
        + [
            pltpu.VMEM((2, 2, blk, d), BF),
            pltpu.VMEM(adjacency.shape, BF),
            pltpu.SemaphoreType.DMA((5,)),
        ],
    )(*graph)
    seen = lax.ppermute(pay, "dom", across)
    prep = call(
        prep_body,
        (rows, s(n, span), s(blk, span), rows, two, two, two),
        [SM] * 3 + [HB] * 4,
        integers(count_k, count_k)
        + [
            pltpu.VMEM(features.shape, BF),
            pltpu.VMEM(adjacency.shape, BF),
            pltpu.VMEM((n // blk, n // blk + 2, blk, blk), F32),
            pltpu.SemaphoreType.DMA((4,)),
        ],
        16,
    )
    h, dense, df, mask, pick, fpick, fsel = prep(*graph)
    q, pick = lax.optimization_barrier((q, pick))
    haloq = near_gather(q)
    later, haloq = lax.optimization_barrier((own, haloq))
    packs += [fetch(later, k) for k in range(sections - 2, 0, -1)] + [own]
    m, halo = call(first_body, (rows, s(2 * blk, 2 * d)), [VM] * 5)(h, pick, haloq, seen, packs[0])

    def stages(k):
        return [
            pltpu.VMEM((k, 2 * d), BF),
            pltpu.VMEM((k, 2 * d), BF),
            pltpu.VMEM((k, 2 * d), F32),
        ]

    def second(step, halo, given):
        tail = step + 2 == steps
        outs = (rows, rows, wide, wide) + (() if tail else (s(blk, 2 * d, dtype=F32),))
        return call(second_body(step, given, tail), outs, [VM] * 11, stages(n))(
            h, m, pick, haloq, halo, dense, df, mask, fsel,
            packs[step // layers], packs[(step + 1) // layers],
        )

    h, m, q, *far = second(0, halo, True)
    for step in range(1, steps - 1, 2):
        haloq = near_gather(q)
        pay = call(pay_body, s(2 * blk, 2 * d), [VM] * 5)(pick, haloq, df, *far)
        asked = lax.all_gather(pay, "dom", axis_index_groups=far_pairs)
        h, m, q, far_m = call(
            first_of_two_body(step),
            (rows, rows, wide, wide),
            [VM] * 12,
            stages(n + blk) + [pltpu.VMEM((blk, 2 * d), BF)] * 2,
        )(
            h, m, pick, haloq, fpick, asked, dense, mask, fsel, seen,
            packs[step // layers], packs[(step + 1) // layers],
        )
        haloq = near_gather(q)
        h, m, q, *far = second(step + 1, far_m, False)
    far_m = lax.ppermute(far[0], "dom", across)
    haloq = near_gather(q)
    out = call(
        last_body(steps - 1),
        s(2, n, d),
        [VM] * 8 + [SM] * 2,
        stages(n)
        + [pltpu.VMEM((2, n, d), BF)]
        + [pltpu.SemaphoreType.DMA((n // blk,))],
        spaces=HB,
    )(h, m, pick, haloq, far_m, dense, mask, packs[-1], send_up, send_down)
    return out[None]


def solution(mesh):
    placed = (
        P(None, "dom", None),
        P("dom"),
        P("dom"),
        P("dom"),
        P("dom", None, None),
        P("dom"),
        P("dom"),
        P("section", None, None),
        P("section", None, None),
        P("section", None),
        P("section", None, None),
        P("section", None),
        P("section", None),
    )
    return jax.shard_map(
        shards,
        mesh=mesh,
        in_specs=placed,
        out_specs=P("section", None, "dom", None),
        check_vma=False,
    )
```

time: 106 us -> 90.8 us (0.86)
  starting transfers between devices: 28 us -> 14.3 us
  blocking collectives: 44.7 us -> 52.6 us
  Pallas kernels: 27.2 us -> 21.2 us
  waiting for transfers between devices: 1.96 us -> 0.16 us
  local copies, waits for them, and re-layouts: 1.31 us -> 0 us
    ppermute x8 -> x2, starting transfers between devices: 20.1 us -> 6.16 us  [the longest x1 4.24 us: shards(): seen = lax.ppermute(pay, 'dom', across)]
    all_gather x8 -> x11, blocking collectives: 44.7 us -> 52.6 us  [the longest x8 37.2 us: near_gather(): return lax.all_gather(q, 'dom', axis_index_groups=near_pairs)]
    pallas_call x18 -> x15, Pallas kernels: 27.2 us -> 21.2 us  [the longest x4 7.49 us: second(): call(second_body(step, given, tail), outs, [VM] * 11, stages(n))]
    ppermute x8 -> x2, waiting for transfers between devices: 1.95 us -> 0.15 us  [the longest x1 0.15 us: shards(): seen = lax.ppermute(pay, 'dom', across)]
    unnamed x4 -> x0, local copies, waits for them, and re-layouts: 1.31 us -> none
  transfers between devices with their start and end apart: 11 -> 5, of which waited for: 1 -> 1; matrix products, arithmetic and copies ran while one was open for 0% -> 0% of each run, Pallas kernels for 17% -> 11%
where the time goes in v2:
time: 90.8 us; the launch traced here: 90.5 us
  blocking collectives  52.6 us (58%)
  Pallas kernels  21.2 us (23%)
  starting transfers between devices  14.3 us (16%)
  between operations  2.24 us (2%)
    all_gather x8, blocking collectives, near_gather(): return lax.all_gather(q, 'dom', axis_index_groups=near_pairs)  37.2 us
    all_gather x3, blocking collectives, shards(): asked = lax.all_gather(pay, 'dom', axis_index_groups=far_pairs)  15.4 us
    ppermute x3, starting transfers between devices, fetch(): lax.ppermute(own, 'section', [(i, i + k) for i in range(sections - k)])  8.18 us
    pallas_call x4, Pallas kernels, second(): call(second_body(step, given, tail), outs, [VM] * 11, stages(n))  7.49 us
    pallas_call x3, Pallas kernels, shards(): call(first_of_two_body(step), (rows, rows, wide, wide), [VM] * 12, stages...  6.08 us
    ppermute x1, starting transfers between devices, shards(): seen = lax.ppermute(pay, 'dom', across)  4.24 us
    pallas_call x1, Pallas kernels, shards(): call(last_body(steps - 1), s(2, n, d), [VM] * 8 + [SM] * 2, stages(n) + [...  2.34 us
    ppermute x1, starting transfers between devices, shards(): far_m = lax.ppermute(far[0], 'dom', across)  1.92 us
  transfers between devices with their start and end apart: 5, of which 1 were waited for; matrix products, arithmetic and copies ran while one was open for 0% of the time, Pallas kernels for 11%

profile of v2, /device:TPU:33, one launch (start us, length us, event | category | flops | bytes accessed | tf_op | source)
XLA Modules:
  0.0 90.5 jit_solution(7902361500313004635)
XLA Ops:
  1.2 4.4 %collective-permute-start.1 = (bf16[1040,128]{1,0:T(8,128)(2,1)S(1)}, bf16[1040,128]{1,0:T(8,128)(2,1)S(1)}, u32[]{:S(2)}, u32[]{:S(2)}) collective-permute-start(bf16[1040,128]{1,0:T(8,128)(2,1)S(1)} %shard_map.129.nxt.pack), channel_id=1, source_target_pairs={{0,384},{1,385},{2,386},{3,387},{4,388},{5,389},{6,390},{7,391},{8... | collective-permute-start | bytes 798728 | tf_op jit(solution)/shard_map/ppermute | solution.py:358
  7.5 1.9 %shard_map.127 = (bf16[1024,256]{1,0:T(8,128)(2,1)S(1)}, bf16[1024,1280]{1,0:T(8,128)(2,1)S(1)}, bf16[128,1280]{1,0:T(8,128)(2,1)S(1)}, bf16[1024,256]{1,0:T(8,1...) custom-call(s32[1]{0:T(128)S(6)} %copy.14.count, ...), custom_call_target="tpu_custom_call" | custom-call | tf_op jit(solution)/shard_map/pallas_call | solution.py:411
  10.8 2.5 %all-gather = bf16[256,256]{1,0:T(8,128)(2,1)S(1)} all-gather(bf16[128,256]{1,0:T(8,128)(2,1)S(1)} %get-tuple-element.55), channel_id=2, replica_groups={{0,1},{2,3},{4,5},{6,7},{8,9},{10,11},{12,13},{14,15},{16,17},{18,19},{..., dimensions={0}, use_global_device_ids=true | all-gather | bytes 196608 | tf_op jit(solution)/shard_map/all_gather | solution.py:355
  14.6 4.2 %collective-permute-start = (bf16[256,256]{1,0:T(8,128)(2,1)S(1)}, bf16[256,256]{1,0:T(8,128)(2,1)S(1)}, u32[]{:S(2)}, u32[]{:S(2)}) collective-permute-start(bf16[256,256]{1,0:T(8,128)(2,1)S(1)} %get-tuple-element.57), channel_id=1, source_target_pairs={{1,2},{3,4},{5,6},{7,8},{9,10},{11,12},{13,14},{15,16},{17,18},{19... | collective-permute-start | bytes 393224 | tf_op jit(solution)/shard_map/ppermute | solution.py:397
  18.9 2.5 %collective-permute-start.3 = (bf16[1040,128]{1,0:T(8,128)(2,1)S(1)}, bf16[1040,128]{1,0:T(8,128)(2,1)S(1)}, u32[]{:S(2)}, u32[]{:S(2)}) collective-permute-start(bf16[1040,128]{1,0:T(8,128)(2,1)S(1)} %shard_map.129.nxt.pack), channel_id=1, source_target_pairs={{0,128},{128,256},{256,384},{1,129},{129,257},{257,385},{2,130},{1... | collective-permute-start | bytes 798728 | tf_op jit(solution)/shard_map/ppermute | solution.py:358
  21.9 1.9 %shard_map.131 = (bf16[1024,256]{1,0:T(8,128)(2,1)S(1)}, bf16[1024,256]{1,0:T(8,128)(2,1)S(1)}, bf16[128,256]{1,0:T(8,128)(2,1)S(1)}, bf16[128,256]{1,0:T(8,128)(2,1)S(1)}, f32[128,256]{1,0:T(8,128)S(1)}) custom-call(bf16[1024,256]{1,0:T(8,128)(2,1)S(1)} %get-tuple-element.51.h, bf16[1024,256]{1,0:T(8,128)(2,1)S(1)} %get-tuple-element.58.m, ...), custom_call_target="tpu_custom_call" | custom-call | tf_op jit(solution)/shard_map/pallas_call | solution.py:428
  23.8 8.3 %all-gather.1 = bf16[256,256]{1,0:T(8,128)(2,1)S(1)} all-gather(bf16[128,256]{1,0:T(8,128)(2,1)S(1)} %get-tuple-element.66), channel_id=3, replica_groups={{0,1},{2,3},{4,5},{6,7},{8,9},{10,11},{12,13},{14,15},{16,17},{18,19},{..., dimensions={0}, use_global_device_ids=true | all-gather | bytes 196608 | tf_op jit(solution)/shard_map/all_gather | solution.py:355
  32.2 5.1 %all-gather.2 = bf16[512,256]{1,0:T(8,128)(2,1)S(1)} all-gather(bf16[256,256]{1,0:T(8,128)(2,1)S(1)} %shard_map.132), channel_id=4, replica_groups={{1,2},{3,4},{5,6},{7,8},{9,10},{11,12},{13,14},{15,16},{17,18},{19,20},..., dimensions={0}, use_global_device_ids=true | all-gather | bytes 393216 | tf_op jit(solution)/shard_map/all_gather | solution.py:437
  37.3 2.0 %shard_map.133 = (bf16[1024,256]{1,0:T(8,128)(2,1)S(1)}, bf16[1024,256]{1,0:T(8,128)(2,1)S(1)}, bf16[128,256]{1,0:T(8,128)(2,1)S(1)}, bf16[128,256]{1,0:T(8,128)(2,1)S(1)}) custom-call(bf16[1024,256]{1,0:T(8,128)(2,1)S(1)} %get-tuple-element.64.h, bf16[1024,256]{1,0:T(8,128)(2,1)S(1)} %get-tuple-element.65.m, ...), custom_call_target="tpu_custom_call" | custom-call | tf_op jit(solution)/shard_map/pallas_call | solution.py:438
  39.3 5.2 %all-gather.3 = bf16[256,256]{1,0:T(8,128)(2,1)S(1)} all-gather(bf16[128,256]{1,0:T(8,128)(2,1)S(1)} %get-tuple-element.73), channel_id=5, replica_groups={{0,1},{2,3},{4,5},{6,7},{8,9},{10,11},{12,13},{14,15},{16,17},{18,19},{..., dimensions={0}, use_global_device_ids=true | all-gather | bytes 196608 | tf_op jit(solution)/shard_map/all_gather | solution.py:355
  44.5 1.9 %shard_map.134 = (bf16[1024,256]{1,0:T(8,128)(2,1)S(1)}, bf16[1024,256]{1,0:T(8,128)(2,1)S(1)}, bf16[128,256]{1,0:T(8,128)(2,1)S(1)}, bf16[128,256]{1,0:T(8,128)(2,1)S(1)}, f32[128,256]{1,0:T(8,128)S(1)}) custom-call(bf16[1024,256]{1,0:T(8,128)(2,1)S(1)} %get-tuple-element.71.h, bf16[1024,256]{1,0:T(8,128)(2,1)S(1)} %get-tuple-element.72.m, ...), custom_call_target="tpu_custom_call" | custom-call | tf_op jit(solution)/shard_map/pallas_call | solution.py:428
  46.4 1.9 %all-gather.4 = bf16[256,256]{1,0:T(8,128)(2,1)S(1)} all-gather(bf16[128,256]{1,0:T(8,128)(2,1)S(1)} %get-tuple-element.77), channel_id=6, replica_groups={{0,1},{2,3},{4,5},{6,7},{8,9},{10,11},{12,13},{14,15},{16,17},{18,19},{..., dimensions={0}, use_global_device_ids=true | all-gather | bytes 196608 | tf_op jit(solution)/shard_map/all_gather | solution.py:355
  48.5 5.1 %all-gather.5 = bf16[512,256]{1,0:T(8,128)(2,1)S(1)} all-gather(bf16[256,256]{1,0:T(8,128)(2,1)S(1)} %shard_map.135), channel_id=7, replica_groups={{1,2},{3,4},{5,6},{7,8},{9,10},{11,12},{13,14},{15,16},{17,18},{19,20},..., dimensions={0}, use_global_device_ids=true | all-gather | bytes 393216 | tf_op jit(solution)/shard_map/all_gather | solution.py:437
  53.6 2.0 %shard_map.136 = (bf16[1024,256]{1,0:T(8,128)(2,1)S(1)}, bf16[1024,256]{1,0:T(8,128)(2,1)S(1)}, bf16[128,256]{1,0:T(8,128)(2,1)S(1)}, bf16[128,256]{1,0:T(8,128)(2,1)S(1)}) custom-call(bf16[1024,256]{1,0:T(8,128)(2,1)S(1)} %get-tuple-element.75.h, bf16[1024,256]{1,0:T(8,128)(2,1)S(1)} %get-tuple-element.76.m, ...), custom_call_target="tpu_custom_call" | custom-call | tf_op jit(solution)/shard_map/pallas_call | solution.py:438
  55.6 5.2 %all-gather.6 = bf16[256,256]{1,0:T(8,128)(2,1)S(1)} all-gather(bf16[128,256]{1,0:T(8,128)(2,1)S(1)} %get-tuple-element.82), channel_id=8, replica_groups={{0,1},{2,3},{4,5},{6,7},{8,9},{10,11},{12,13},{14,15},{16,17},{18,19},{..., dimensions={0}, use_global_device_ids=true | all-gather | bytes 196608 | tf_op jit(solution)/shard_map/all_gather | solution.py:355
  60.8 1.9 %shard_map.137 = (bf16[1024,256]{1,0:T(8,128)(2,1)S(1)}, bf16[1024,256]{1,0:T(8,128)(2,1)S(1)}, bf16[128,256]{1,0:T(8,128)(2,1)S(1)}, bf16[128,256]{1,0:T(8,128)(2,1)S(1)}, f32[128,256]{1,0:T(8,128)S(1)}) custom-call(bf16[1024,256]{1,0:T(8,128)(2,1)S(1)} %get-tuple-element.80.h, bf16[1024,256]{1,0:T(8,128)(2,1)S(1)} %get-tuple-element.81.m, ...), custom_call_target="tpu_custom_call" | custom-call | tf_op jit(solution)/shard_map/pallas_call | solution.py:428
  62.8 1.9 %all-gather.7 = bf16[256,256]{1,0:T(8,128)(2,1)S(1)} all-gather(bf16[128,256]{1,0:T(8,128)(2,1)S(1)} %get-tuple-element.86), channel_id=9, replica_groups={{0,1},{2,3},{4,5},{6,7},{8,9},{10,11},{12,13},{14,15},{16,17},{18,19},{..., dimensions={0}, use_global_device_ids=true | all-gather | bytes 196608 | tf_op jit(solution)/shard_map/all_gather | solution.py:355
  64.8 5.3 %all-gather.8 = bf16[512,256]{1,0:T(8,128)(2,1)S(1)} all-gather(bf16[256,256]{1,0:T(8,128)(2,1)S(1)} %shard_map.138), channel_id=10, replica_groups={{1,2},{3,4},{5,6},{7,8},{9,10},{11,12},{13,14},{15,16},{17,18},{19,20},..., dimensions={0}, use_global_device_ids=true | all-gather | bytes 393216 | tf_op jit(solution)/shard_map/all_gather | solution.py:437
  70.1 2.0 %shard_map.139 = (bf16[1024,256]{1,0:T(8,128)(2,1)S(1)}, bf16[1024,256]{1,0:T(8,128)(2,1)S(1)}, bf16[128,256]{1,0:T(8,128)(2,1)S(1)}, bf16[128,256]{1,0:T(8,128)(2,1)S(1)}) custom-call(bf16[1024,256]{1,0:T(8,128)(2,1)S(1)} %get-tuple-element.84.h, bf16[1024,256]{1,0:T(8,128)(2,1)S(1)} %get-tuple-element.85.m, ...), custom_call_target="tpu_custom_call" | custom-call | tf_op jit(solution)/shard_map/pallas_call | solution.py:438
  72.1 5.2 %all-gather.9 = bf16[256,256]{1,0:T(8,128)(2,1)S(1)} all-gather(bf16[128,256]{1,0:T(8,128)(2,1)S(1)} %get-tuple-element.91), channel_id=11, replica_groups={{0,1},{2,3},{4,5},{6,7},{8,9},{10,11},{12,13},{14,15},{16,17},{18,19},{..., dimensions={0}, use_global_device_ids=true | all-gather | bytes 196608 | tf_op jit(solution)/shard_map/all_gather | solution.py:355
  77.3 1.7 %shard_map.140 = (bf16[1024,256]{1,0:T(8,128)(2,1)S(1)}, bf16[1024,256]{1,0:T(8,128)(2,1)S(1)}, bf16[128,256]{1,0:T(8,128)(2,1)S(1)}, bf16[128,256]{1,0:T(8,128)(2,1)S(1)}) custom-call(bf16[1024,256]{1,0:T(8,128)(2,1)S(1)} %get-tuple-element.89.h, bf16[1024,256]{1,0:T(8,128)(2,1)S(1)} %get-tuple-element.90.m, ...), custom_call_target="tpu_custom_call" | custom-call | tf_op jit(solution)/shard_map/pallas_call | solution.py:428
  79.0 1.9 %collective-permute-start.4 = (bf16[128,256]{1,0:T(8,128)(2,1)S(1)}, bf16[128,256]{1,0:T(8,128)(2,1)S(1)}, u32[]{:S(2)}, u32[]{:S(2)}) collective-permute-start(bf16[128,256]{1,0:T(8,128)(2,1)S(1)} %get-tuple-element.96), channel_id=1, source_target_pairs={{1,2},{3,4},{5,6},{7,8},{9,10},{11,12},{13,14},{15,16},{17,18},{19... | collective-permute-start | bytes 196616 | tf_op jit(solution)/shard_map/ppermute | solution.py:449
  81.0 7.0 %all-gather.10 = bf16[256,256]{1,0:T(8,128)(2,1)S(1)} all-gather(bf16[128,256]{1,0:T(8,128)(2,1)S(1)} %get-tuple-element.95), channel_id=12, replica_groups={{0,1},{2,3},{4,5},{6,7},{8,9},{10,11},{12,13},{14,15},{16,17},{18,19},{..., dimensions={0}, use_global_device_ids=true | all-gather | bytes 196608 | tf_op jit(solution)/shard_map/all_gather | solution.py:355
  88.0 2.3 %shard_map.141 = bf16[2,1024,128]{2,1,0:T(8,128)(2,1)} custom-call(bf16[1024,256]{1,0:T(8,128)(2,1)S(1)} %get-tuple-element.93.h, bf16[1024,256]{1,0:T(8,128)(2,1)S(1)} %get-tuple-element.94.m, bf16[2,128,256]{2,1,0:T(8,128)(2,1)S(1)} %get-tuple-element.54.pick, bf16[2,128,256]{2,1,0:T(8,128)(2,1)S(1)} %bitcast.23, ...), custom_call_target="tpu_custom_call" | custom-call | tf_op jit(solution)/shard_map/pallas_call | solution.py:451
  (12 shorter events, 4.8 us)
Async XLA Ops:
  1.2 20.4 %collective-permute-start.1 = (bf16[1040,128]{1,0:T(8,128)(2,1)S(1)}, bf16[1040,128]{1,0:T(8,128)(2,1)S(1)}, u32[]{:S(2)}, u32[]{:S(2)}) collective-permute-start(bf16[1040,128]{1,0:T(8,128)(2,1)S(1)} %shard_map.129.nxt.pack), channel_id=1, source_target_pairs={{0,384},{1,385},{2,386},{3,387},{4,388},{5,389},{6,390},{7,391},{8... | collective-permute-start | bytes 798728 | tf_op jit(solution)/shard_map/ppermute | solution.py:358
  13.3 23.9 %collective-permute-start.2 = (bf16[1040,128]{1,0:T(8,128)(2,1)S(1)}, bf16[1040,128]{1,0:T(8,128)(2,1)S(1)}, u32[]{:S(2)}, u32[]{:S(2)}) collective-permute-start(bf16[1040,128]{1,0:T(8,128)(2,1)S(1)} %shard_map.129.nxt.pack), channel_id=1, source_target_pairs={{0,256},{128,384},{1,257},{129,385},{2,258},{130,386},{3,259},{131... | collective-permute-start | bytes 798728 | tf_op jit(solution)/shard_map/ppermute | solution.py:358
  14.6 6.9 %collective-permute-start = (bf16[256,256]{1,0:T(8,128)(2,1)S(1)}, bf16[256,256]{1,0:T(8,128)(2,1)S(1)}, u32[]{:S(2)}, u32[]{:S(2)}) collective-permute-start(bf16[256,256]{1,0:T(8,128)(2,1)S(1)} %get-tuple-element.57), channel_id=1, source_target_pairs={{1,2},{3,4},{5,6},{7,8},{9,10},{11,12},{13,14},{15,16},{17,18},{19... | collective-permute-start | bytes 393224 | tf_op jit(solution)/shard_map/ppermute | solution.py:397
  18.9 34.7 %collective-permute-start.3 = (bf16[1040,128]{1,0:T(8,128)(2,1)S(1)}, bf16[1040,128]{1,0:T(8,128)(2,1)S(1)}, u32[]{:S(2)}, u32[]{:S(2)}) collective-permute-start(bf16[1040,128]{1,0:T(8,128)(2,1)S(1)} %shard_map.129.nxt.pack), channel_id=1, source_target_pairs={{0,128},{128,256},{256,384},{1,129},{129,257},{257,385},{2,130},{1... | collective-permute-start | bytes 798728 | tf_op jit(solution)/shard_map/ppermute | solution.py:358
  79.0 8.9 %collective-permute-start.4 = (bf16[128,256]{1,0:T(8,128)(2,1)S(1)}, bf16[128,256]{1,0:T(8,128)(2,1)S(1)}, u32[]{:S(2)}, u32[]{:S(2)}) collective-permute-start(bf16[128,256]{1,0:T(8,128)(2,1)S(1)} %get-tuple-element.96), channel_id=1, source_target_pairs={{1,2},{3,4},{5,6},{7,8},{9,10},{11,12},{13,14},{15,16},{17,18},{19... | collective-permute-start | bytes 196616 | tf_op jit(solution)/shard_map/ppermute | solution.py:449

commit v3 on v2

--- a/solution.py
+++ b/solution.py
@@ -9,7 +9,6 @@
 BF = jnp.bfloat16
 F32 = jnp.float32
 VM = pl.BlockSpec(memory_space=pltpu.VMEM)
-SM = pl.BlockSpec(memory_space=pltpu.SMEM)
 HB = pl.BlockSpec(memory_space=pltpu.HBM)
 CHUNK = 256
 
@@ -100,39 +99,40 @@
     out[8 * d :] = jnp.concatenate(vectors, axis=0).astype(BF)
 
 
-def blocks_body(count, up, down, rows, cols, x, adj, q, pay, sr, sk, xs, av, sem):
+def blocks_body(ints, rows, cols, x, adj, q, pay, si, sr, sk, xs, av, sem):
     blk, d = av.shape[1], av.shape[2]
-    copies = fetch_all([(rows, sr), (cols, sk), (adj, av)], sem)
-    blocks = to_partners(up[0], down[0])
+    copies = fetch_all([(ints, si), (rows, sr), (cols, sk), (adj, av)], sem)
+    copies[0].wait()
+    blocks = to_partners(si[1], si[2])
     for i, block in enumerate(blocks):
         at = pl.ds(pl.multiple_of(block * blk, blk), blk)
-        copies.append(pltpu.make_async_copy(x.at[:, at, :], xs.at[i], sem.at[3 + i]))
+        copies.append(pltpu.make_async_copy(x.at[:, at, :], xs.at[i], sem.at[4 + i]))
         copies[-1].start()
-    for copy in copies:
+    for copy in copies[1:]:
         copy.wait()
     for i, (block, dst) in enumerate(zip(blocks, (q, pay))):
         row = block * blk + lax.broadcasted_iota(jnp.int32, (blk, d), 0)
-        keep = jnp.where(row < count[0], jnp.float32(1), jnp.float32(0)).astype(BF)
+        keep = jnp.where(row < si[0], jnp.float32(1), jnp.float32(0)).astype(BF)
         for m in range(2):
             dst[:blk, m * d : (m + 1) * d] = xs[i, m] * keep
-    pay[blk:, d:] = keep
-    far_col = jnp.where(parity() == 1, 9, 8)
-    seen = jnp.zeros((blk, d), F32)
-    for k in range(av.shape[0]):
-        hit = (sr[k] == blocks[1]) & (sk[k] == far_col)
-        seen = seen + av[k].astype(F32) * jnp.where(hit, jnp.float32(1), jnp.float32(0))
-    pay[blk:, :d] = seen.astype(BF)
+        dst[blk:, d:] = keep
+        col = jnp.where(parity() == i, 9, 8)
+        seen = jnp.zeros((blk, d), F32)
+        for k in range(av.shape[0]):
+            hit = (sr[k] == block) & (sk[k] == col)
+            seen = seen + av[k].astype(F32) * jnp.where(hit, jnp.float32(1), jnp.float32(0))
+        dst[blk:, :d] = seen.astype(BF)
 
 
 def prep_body(
-    count, up, down, rows, cols, x, adj,
+    ints, rows, cols, x, adj,
     h, dense, df, mask, pick, fpick, fsel,
-    sr, sk, xv, av, acc, sem,
+    si, sr, sk, xv, av, acc, sem,
 ):
     n, d = xv.shape[1], xv.shape[2]
     blk = av.shape[1]
     last = n // blk
-    copies = fetch_all([(rows, sr), (cols, sk), (x, xv), (adj, av)], sem)
+    copies = fetch_all([(ints, si), (rows, sr), (cols, sk), (x, xv), (adj, av)], sem)
     acc[...] = jnp.zeros_like(acc)
     wide = (blk, 2 * d)
     dom = lax.axis_index("dom")
@@ -142,18 +142,19 @@
     pick[1] = flags(jnp.logical_not(odd), wide)
     fpick[0] = flags(jnp.logical_not(odd | alone), wide)
     fpick[1] = flags(odd & jnp.logical_not(alone), wide)
-    near, far = to_partners(up[0], down[0])
+    copies[0].wait()
+    near, far = to_partners(si[1], si[2])
     fsel[0] = flags(near == far, wide)
     fsel[1] = flags(near != far, wide)
-    copies[2].wait()
+    copies[3].wait()
     for b in range(last):
         at = pl.ds(pl.multiple_of(exchange_of(near, far, b, False) * blk, blk), blk)
         row = b * blk + lax.broadcasted_iota(jnp.int32, wide, 0)
-        keep = jnp.where(row < count[0], jnp.float32(1), jnp.float32(0)).astype(BF)
+        keep = jnp.where(row < si[0], jnp.float32(1), jnp.float32(0)).astype(BF)
         mask[at, :] = keep
         both = [xv[m, b * blk : (b + 1) * blk] for m in range(2)]
         h[at, :] = jnp.concatenate(both, axis=1) * keep
-    for copy in copies[:2] + copies[3:]:
+    for copy in copies[1:3] + copies[4:]:
         copy.wait()
     for k in range(av.shape[0]):
         c = sk[k]
@@ -175,12 +176,13 @@
     return twice(pack[i * d : (i + 1) * d])
 
 
-def first_body(h, pick, haloq, halor, pack, m, halo):
+def first_body(h, pick, haloq, halor, pack, m, halo, nseen):
     w = message_weight(pack, 0)
     m[...] = silu_of_twice(dot(h[...], w))
-    blk = haloq.shape[1]
-    both = jnp.concatenate([choose(pick, haloq[0], haloq[1]), halor[:blk]], axis=0)
+    blk = nseen.shape[0]
+    both = jnp.concatenate([choose(pick, haloq[0, :blk], haloq[1, :blk]), halor[:blk]], axis=0)
     halo[...] = silu_of_twice(dot(both, w))
+    nseen[...] = choose(pick, haloq[0, blk:], haloq[1, blk:])
 
 
 def own_rows(h, m, halo, dense, mask):
@@ -223,85 +225,110 @@
         yield at, new
 
 
-def send_messages(new_h, new_m, outq, nxt, i):
+def send_messages(new_h, new_m, nxt, i):
     w = message_weight(nxt, i)
     for r in range(0, new_m.shape[0], CHUNK):
         at = slice(r, r + CHUNK)
-        out = silu_of_twice(dot(new_h[at], w))
-        new_m[at] = out
-        if r == 0:
-            outq[...] = out[: outq.shape[0]]
+        new_m[at] = silu_of_twice(dot(new_h[at], w))
 
 
 def far_block(fsel, ref, blk):
     return choose(fsel, ref[:blk], ref[blk : 2 * blk])
 
 
-def second_body(step, given, tail):
-    def body(h, m, pick, haloq, halor, dense, df, mask, fsel, pack, nxt, *rest):
-        new_h, new_m, outq = rest[:3]
-        agg, hidden, c = rest[-3:]
+def start_body(step):
+    def body(h, m, halo, dense, df, mask, fsel, pack, nxt, new_h, new_m, outq, far_h, part, *rest):
         blk = outq.shape[0]
-        if given:
-            halo = halor[...]
-        else:
-            near = choose(pick, haloq[0], haloq[1])
-            halo = jnp.concatenate([near, halor[...]], axis=0)
-        for at, new in layer(own_rows(h, m, halo, dense, mask), pack, step % 2, agg, hidden, c):
+        for at, new in layer(own_rows(h, m, halo[...], dense, mask), pack, step % 2, *rest):
             new_h[at] = new
-        send_messages(new_h, new_m, outq, nxt, (step + 1) % 2)
-        if tail:
-            rest[3][...] = far_block(fsel, new_m, blk)
-        else:
-            rest[3][...] = far_block(fsel, new_h, blk)
-            rest[4][...] = dot(df[:, : new_m.shape[0]], new_m[...])
+        send_messages(new_h, new_m, nxt, (step + 1) % 2)
+        outq[...] = new_m[:blk]
+        far_h[...] = far_block(fsel, new_h, blk)
+        part[...] = dot(df[:, : new_m.shape[0]], new_m[...])
 
     return body
 
 
-def pay_body(pick, haloq, df, far_h, part, pay):
+def pay_body(pick, haloq, df, far_h, part, pay, near_m):
     blk = far_h.shape[0]
     n = df.shape[1] - 2 * blk
     near = choose(pick, haloq[0], haloq[1])
+    near_m[...] = near
     pay[:blk] = far_h[...]
     pay[blk:] = (part[...] + dot(df[:, n : n + blk], near)).astype(BF)
 
 
-def first_of_two_body(step):
-    def body(h, m, pick, haloq, fpick, far, dense, mask, fsel, seen, pack, nxt, *rest):
-        new_h, new_m, outq, far_m, agg, hidden, c, hx, mx = rest
-        n = m.shape[0]
-        blk, d2 = hx.shape
-        d = d2 // 2
-        hx[...] = choose(fpick, far[0, :blk], far[1, :blk])
-        part = choose(fpick, far[0, blk:], far[1, blk:])
-        view = seen[blk:]
-        mx[...] = jnp.concatenate([view[:, d:], view[:, d:]], axis=1)
-        theirs = silu_of_twice(dot(hx[...], message_weight(pack, step % 2)))
-        halo = jnp.concatenate([choose(pick, haloq[0], haloq[1]), theirs], axis=0)
+def partner_layer(h, m, given, pick, seen, mine, other, is_far, dense, mask, pack, i, new_h, rest):
+    agg, hidden, c, hx, mx = rest
+    n = m.shape[0]
+    blk, d2 = hx.shape
+    d = d2 // 2
+    hx[...] = choose(pick, given[0, :blk], given[1, :blk])
+    part = choose(pick, given[0, blk:], given[1, blk:])
+    mx[...] = jnp.concatenate([seen[:, d:], seen[:, d:]], axis=1)
+    theirs = silu_of_twice(dot(hx[...], message_weight(pack, i)))
+    halo = jnp.concatenate([other, theirs] if is_far else [theirs, other], axis=0)
+    chunks = own_rows(h, m, halo, dense, mask)
+    chunks.append(
+        (slice(n, n + blk), hx, lambda: part.astype(F32) + dot(seen[:, :d], mine), mx)
+    )
+    for at, new in layer(chunks, pack, i, agg, hidden, c):
+        if at.start < n:
+            new_h[at] = new
+        else:
+            hx[...] = new
+
+
+def far_layer_body(step):
+    def body(h, m, near_m, fpick, far, dense, mask, fsel, seen, pack, nxt, *rest):
+        new_h, new_m, pay, far_m = rest[:4]
+        rest = rest[4:]
+        n, blk = m.shape[0], far_m.shape[0]
         mine = far_block(fsel, m, blk)
-        chunks = own_rows(h, m, halo, dense, mask)
-        chunks.append(
-            (slice(n, n + blk), hx, lambda: part.astype(F32) + dot(view[:, :d], mine), mx)
+        partner_layer(
+            h, m, far, fpick, seen[blk:], mine, near_m[...], True, dense, mask, pack, step % 2,
+            new_h, rest,
         )
-        for at, new in layer(chunks, pack, step % 2, agg, hidden, c):
-            if at.start < n:
-                new_h[at] = new
-            else:
-                hx[...] = new
-        send_messages(new_h, new_m, outq, nxt, (step + 1) % 2)
-        far_m[...] = silu_of_twice(dot(hx[...], message_weight(nxt, (step + 1) % 2)))
+        send_messages(new_h, new_m, nxt, (step + 1) % 2)
+        theirs = silu_of_twice(dot(rest[3][...], message_weight(nxt, (step + 1) % 2)))
+        far_m[...] = theirs
+        pay[:blk] = new_h[:blk]
+        part = dot(dense[:blk, :n], new_m[...]) + dot(dense[:blk, n + blk :], theirs)
+        pay[blk:] = part.astype(BF)
 
     return body
 
 
+def near_layer_body(step, tail):
+    def body(h, m, far_m, pick, near, dense, df, mask, fsel, nseen, pack, nxt, *rest):
+        new_h, new_m, pay, near_m = rest[:4]
+        rest = rest[4:]
+        n, blk = m.shape[0], near_m.shape[0]
+        partner_layer(
+            h, m, near, pick, nseen[...], m[:blk], far_m[...], False, dense, mask, pack, step % 2,
+            new_h, rest,
+        )
+        send_messages(new_h, new_m, nxt, (step + 1) % 2)
+        theirs = silu_of_twice(dot(rest[3][...], message_weight(nxt, (step + 1) % 2)))
+        near_m[...] = theirs
+        if tail:
+            pay[...] = far_block(fsel, new_m, blk)
+        else:
+            pay[:blk] = far_block(fsel, new_h, blk)
+            part = dot(df[:, :n], new_m[...]) + dot(df[:, n : n + blk], theirs)
+            pay[blk:] = part.astype(BF)
+
+    return body
+
+
 def last_body(step):
-    def body(h, m, pick, haloq, halor, dense, mask, pack, up, down, out, *rest):
-        agg, hidden, c, stage, sem = rest
+    def body(h, m, near_m, fpick, far, dense, mask, pack, ints, out, agg, hidden, c, stage, si, sem):
         d = pack.shape[1]
-        blk = halor.shape[0]
-        halo = jnp.concatenate([choose(pick, haloq[0], haloq[1]), halor[...]], axis=0)
-        near, far = to_partners(up[0], down[0])
+        blk = near_m.shape[0]
+        (asked,) = fetch_all([(ints, si)], sem)
+        halo = jnp.concatenate([near_m[...], choose(fpick, far[0], far[1])], axis=0)
+        asked.wait()
+        near, far = to_partners(si[1], si[2])
         copies = []
         for at, new in layer(own_rows(h, m, halo, dense, mask), pack, step % 2, agg, hidden, c):
             stage[0, at] = new[:, :d]
@@ -312,7 +339,7 @@
                     pltpu.make_async_copy(
                         stage.at[:, b * blk : (b + 1) * blk, :],
                         out.at[:, pl.ds(to, blk), :],
-                        sem.at[b],
+                        sem.at[1 + b],
                     )
                 )
                 copies[-1].start()
@@ -360,7 +387,17 @@
     def integers(*sizes):
         return [pltpu.SMEM((k,), jnp.int32) for k in sizes]
 
+    def far_gather(q, step):
+        groups = []
+        for section in range(sections):
+            begun = layers * (sections - 1 - section) <= step + 1
+            groups += [
+                [section * doms + i for i in pair] for pair in (far_pairs if begun else near_pairs)
+            ]
+        return lax.all_gather(q, ("section", "dom"), axis_index_groups=groups)
+
     wide = s(blk, 2 * d)
+    both = s(2 * blk, 2 * d)
     rows = s(n, 2 * d)
     two = s(2, blk, 2 * d)
     span = n + 2 * blk
@@ -382,29 +419,30 @@
         ],
     )(*weights)
     packs = [fetch(own, sections - 1)]
-    graph = [counts, send_up, send_down, *in_hbm(row_blocks, col_blocks, features, adjacency)]
+    ints = jnp.concatenate([counts, send_up, send_down, jnp.zeros((125,), jnp.int32)])
+    graph = in_hbm(ints, row_blocks, col_blocks, features, adjacency)
     q, pay = call(
         blocks_body,
-        (wide, s(2 * blk, 2 * d)),
-        [SM] * 3 + [HB] * 4,
-        integers(count_k, count_k)
+        (both, both),
+        [HB] * 5,
+        integers(128, count_k, count_k)
         + [
             pltpu.VMEM((2, 2, blk, d), BF),
             pltpu.VMEM(adjacency.shape, BF),
-            pltpu.SemaphoreType.DMA((5,)),
+            pltpu.SemaphoreType.DMA((6,)),
         ],
     )(*graph)
     seen = lax.ppermute(pay, "dom", across)
     prep = call(
         prep_body,
         (rows, s(n, span), s(blk, span), rows, two, two, two),
-        [SM] * 3 + [HB] * 4,
-        integers(count_k, count_k)
+        [HB] * 5,
+        integers(128, count_k, count_k)
         + [
             pltpu.VMEM(features.shape, BF),
             pltpu.VMEM(adjacency.shape, BF),
             pltpu.VMEM((n // blk, n // blk + 2, blk, blk), F32),
-            pltpu.SemaphoreType.DMA((4,)),
+            pltpu.SemaphoreType.DMA((5,)),
         ],
         16,
     )
@@ -413,7 +451,7 @@
     haloq = near_gather(q)
     later, haloq = lax.optimization_barrier((own, haloq))
     packs += [fetch(later, k) for k in range(sections - 2, 0, -1)] + [own]
-    m, halo = call(first_body, (rows, s(2 * blk, 2 * d)), [VM] * 5)(h, pick, haloq, seen, packs[0])
+    m, halo, nseen = call(first_body, (rows, both, wide), [VM] * 5)(h, pick, haloq, seen, packs[0])
 
     def stages(k):
         return [
@@ -422,41 +460,35 @@
             pltpu.VMEM((k, 2 * d), F32),
         ]
 
-    def second(step, halo, given):
+    def weights_at(step):
+        return packs[step // layers], packs[(step + 1) // layers]
+
+    h, m, q, far_h, part = call(
+        start_body(0), (rows, rows, wide, wide, s(blk, 2 * d, dtype=F32)), [VM] * 9, stages(n)
+    )(h, m, halo, dense, df, mask, fsel, *weights_at(0))
+    pay, near_m = call(pay_body, (both, wide), [VM] * 5)(pick, near_gather(q), df, far_h, part)
+    more = stages(n + blk) + [pltpu.VMEM((blk, 2 * d), BF)] * 2
+    for step in range(1, steps - 1, 2):
+        asked = far_gather(pay, step)
+        h, m, pay, far_m = call(
+            far_layer_body(step), (rows, rows, both, wide), [VM] * 11, more
+        )(h, m, near_m, fpick, asked, dense, mask, fsel, seen, *weights_at(step))
+        asked = near_gather(pay)
+        step += 1
         tail = step + 2 == steps
-        outs = (rows, rows, wide, wide) + (() if tail else (s(blk, 2 * d, dtype=F32),))
-        return call(second_body(step, given, tail), outs, [VM] * 11, stages(n))(
-            h, m, pick, haloq, halo, dense, df, mask, fsel,
-            packs[step // layers], packs[(step + 1) // layers],
-        )
-
-    h, m, q, *far = second(0, halo, True)
-    for step in range(1, steps - 1, 2):
-        haloq = near_gather(q)
-        pay = call(pay_body, s(2 * blk, 2 * d), [VM] * 5)(pick, haloq, df, *far)
-        asked = lax.all_gather(pay, "dom", axis_index_groups=far_pairs)
-        h, m, q, far_m = call(
-            first_of_two_body(step),
-            (rows, rows, wide, wide),
-            [VM] * 12,
-            stages(n + blk) + [pltpu.VMEM((blk, 2 * d), BF)] * 2,
-        )(
-            h, m, pick, haloq, fpick, asked, dense, mask, fsel, seen,
-            packs[step // layers], packs[(step + 1) // layers],
-        )
-        haloq = near_gather(q)
-        h, m, q, *far = second(step + 1, far_m, False)
-    far_m = lax.ppermute(far[0], "dom", across)
-    haloq = near_gather(q)
+        h, m, pay, near_m = call(
+            near_layer_body(step, tail), (rows, rows, wide if tail else both, wide), [VM] * 12, more
+        )(h, m, far_m, pick, asked, dense, df, mask, fsel, nseen, *weights_at(step))
     out = call(
         last_body(steps - 1),
         s(2, n, d),
-        [VM] * 8 + [SM] * 2,
+        [VM] * 8 + [HB],
         stages(n)
         + [pltpu.VMEM((2, n, d), BF)]
-        + [pltpu.SemaphoreType.DMA((n // blk,))],
+        + integers(128)
+        + [pltpu.SemaphoreType.DMA((1 + n // blk,))],
         spaces=HB,
-    )(h, m, pick, haloq, far_m, dense, mask, packs[-1], send_up, send_down)
+    )(h, m, near_m, fpick, far_gather(pay, steps - 1), dense, mask, packs[-1], graph[0])
     return out[None]
 
 

time: 90.8 us -> 86.8 us (0.956)
  the two profiles are of different devices: /device:TPU:33 before, /device:TPU:36 now
where the time goes in v3:
time: 86.8 us; the launch traced here: 86.5 us
  blocking collectives  42.9 us (49%)
  Pallas kernels  24.5 us (28%)
  starting transfers between devices  16.3 us (19%)
  between operations  2.26 us (3%)
    all_gather x4, blocking collectives, far_gather(): return lax.all_gather(q, ('section', 'dom'), axis_index_groups=groups)  32.8 us
    ppermute x1, starting transfers between devices, shards(): seen = lax.ppermute(pay, 'dom', across)  10.6 us
    all_gather x5, blocking collectives, near_gather(): return lax.all_gather(q, 'dom', axis_index_groups=near_pairs)  10.1 us
    pallas_call x3, Pallas kernels, shards(): call(far_layer_body(step), (rows, rows, both, wide), [VM] * 11, more)  7.14 us
    pallas_call x3, Pallas kernels, shards(): call(near_layer_body(step, tail), (rows, rows, wide if tail else both, wi...  6.83 us
    ppermute x3, starting transfers between devices, fetch(): lax.ppermute(own, 'section', [(i, i + k) for i in range(sections - k)])  5.68 us
    pallas_call x1, Pallas kernels, shards(): call(last_body(steps - 1), s(2, n, d), [VM] * 8 + [HB], stages(n) + [pltp...  3 us
    pallas_call x1, Pallas kernels, shards(): call(blocks_body, (both, both), [HB] * 5, integers(128, count_k, count_k)...  2.02 us
  transfers between devices with their start and end apart: 4, of which 0 were waited for; matrix products, arithmetic and copies ran while one was open for 1% of the time, Pallas kernels for 13%

profile of v3, /device:TPU:36, one launch (start us, length us, event | category | flops | bytes accessed | tf_op | source)
XLA Modules:
  0.0 86.5 jit_solution(17499862574719810439)
XLA Ops:
  0.0 1.1 %shard_map.129.nxt.pack = bf16[1040,128]{1,0:T(8,128)(2,1)S(1)} custom-call(bf16[2,128,128]{2,1,0:T(8,128)(2,1)} %wm.1, bf16[2,256,128]{2,1,0:T(8,128)(2,1)} %wh.1, bf16[2,128]{1,0:T(2,128)(2,1)} %bh.1, bf16[2,128,128]{2,1,0:T(8,128)(2,1)} %wo.1, bf16[2,128]{1,0:T(2,128)(2,1)} %bo.1, bf16[2,128]{1,0:T(2,128)(2,1)} %gain.1), custom_call_target="tpu_custom_call" | custom-call | tf_op jit(solution)/shard_map/pallas_call | solution.py:407
  1.2 0.7 collective-permute-start.1
  4.4 1.9 %shard_map.127 = (bf16[1024,256]{1,0:T(8,128)(2,1)S(1)}, bf16[1024,1280]{1,0:T(8,128)(2,1)S(1)}, bf16[128,1280]{1,0:T(8,128)(2,1)S(1)}, bf16[1024,256]{1,0:T(8,1...) custom-call(s32[128]{0:T(128)} %pad_add_fusion.ints, ...), custom_call_target="tpu_custom_call" | custom-call | tf_op jit(solution)/shard_map/pallas_call | solution.py:449
  6.3 2.0 %shard_map.128 = (bf16[256,256]{1,0:T(8,128)(2,1)S(1)}, bf16[256,256]{1,0:T(8,128)(2,1)S(1)}) custom-call(s32[128]{0:T(128)} %pad_add_fusion.ints, s32[24]{0:T(128)} %rows.3, s32[24]{0:T(128)} %cols.3, bf16[2,1024,128]{2,1,0:T(8,128)(2,1)} %x.3, bf16[24,128,128]{2,1,0:T(8,128)(2,1)} %adj.3), custom_call_target="tpu_custom_call" | custom-call | tf_op jit(solution)/shard_map/pallas_call | solution.py:424
  8.4 2.0 %all-gather = bf16[512,256]{1,0:T(8,128)(2,1)S(1)} all-gather(bf16[256,256]{1,0:T(8,128)(2,1)S(1)} %get-tuple-element.56), channel_id=2, replica_groups={{0,1},{2,3},{4,5},{6,7},{8,9},{10,11},{12,13},{14,15},{16,17},{18,19},{..., dimensions={0}, use_global_device_ids=true | all-gather | bytes 393216 | tf_op jit(solution)/shard_map/all_gather | solution.py:382
  10.4 1.3 %collective-permute-start.2 = (bf16[1040,128]{1,0:T(8,128)(2,1)S(1)}, bf16[1040,128]{1,0:T(8,128)(2,1)S(1)}, u32[]{:S(2)}, u32[]{:S(2)}) collective-permute-start(bf16[1040,128]{1,0:T(8,128)(2,1)S(1)} %shard_map.129.nxt.pack), channel_id=1, source_target_pairs={{0,256},{128,384},{1,257},{129,385},{2,258},{130,386},{3,259},{131... | collective-permute-start | bytes 798728 | tf_op jit(solution)/shard_map/ppermute | solution.py:385
  11.7 10.6 %collective-permute-start = (bf16[256,256]{1,0:T(8,128)(2,1)S(1)}, bf16[256,256]{1,0:T(8,128)(2,1)S(1)}, u32[]{:S(2)}, u32[]{:S(2)}) collective-permute-start(bf16[256,256]{1,0:T(8,128)(2,1)S(1)} %get-tuple-element.58), channel_id=1, source_target_pairs={{1,2},{3,4},{5,6},{7,8},{9,10},{11,12},{13,14},{15,16},{17,18},{19... | collective-permute-start | bytes 393224 | tf_op jit(solution)/shard_map/ppermute | solution.py:435
  22.2 3.7 %collective-permute-start.3 = (bf16[1040,128]{1,0:T(8,128)(2,1)S(1)}, bf16[1040,128]{1,0:T(8,128)(2,1)S(1)}, u32[]{:S(2)}, u32[]{:S(2)}) collective-permute-start(bf16[1040,128]{1,0:T(8,128)(2,1)S(1)} %shard_map.129.nxt.pack), channel_id=1, source_target_pairs={{0,128},{128,256},{256,384},{1,129},{129,257},{257,385},{2,130},{1... | collective-permute-start | bytes 798728 | tf_op jit(solution)/shard_map/ppermute | solution.py:385
  26.4 1.9 %shard_map.131 = (bf16[1024,256]{1,0:T(8,128)(2,1)S(1)}, bf16[1024,256]{1,0:T(8,128)(2,1)S(1)}, bf16[128,256]{1,0:T(8,128)(2,1)S(1)}, bf16[128,256]{1,0:T(8,128)(2,1)S(1)}, f32[128,256]{1,0:T(8,128)S(1)}) custom-call(bf16[1024,256]{1,0:T(8,128)(2,1)S(1)} %get-tuple-element.52.h, bf16[1024,256]{1,0:T(8,128)(2,1)S(1)} %get-tuple-element.59.m, ...), custom_call_target="tpu_custom_call" | custom-call | tf_op jit(solution)/shard_map/pallas_call | solution.py:466
  28.3 1.9 %all-gather.1 = bf16[256,256]{1,0:T(8,128)(2,1)S(1)} all-gather(bf16[128,256]{1,0:T(8,128)(2,1)S(1)} %get-tuple-element.67), channel_id=3, replica_groups={{0,1},{2,3},{4,5},{6,7},{8,9},{10,11},{12,13},{14,15},{16,17},{18,19},{..., dimensions={0}, use_global_device_ids=true | all-gather | bytes 196608 | tf_op jit(solution)/shard_map/all_gather | solution.py:382
  30.3 8.4 %all-gather.2 = bf16[512,256]{1,0:T(8,128)(2,1)S(1)} all-gather(bf16[256,256]{1,0:T(8,128)(2,1)S(1)} %get-tuple-element.72), channel_id=4, replica_groups={{0,1},{2,3},{4,5},{6,7},{8,9},{10,11},{12,13},{14,15},{16,17},{18,19},{..., dimensions={0}, use_global_device_ids=true | all-gather | bytes 393216 | tf_op jit(solution)/shard_map/all_gather | solution.py:397
  38.7 2.4 %shard_map.133 = (bf16[1024,256]{1,0:T(8,128)(2,1)S(1)}, bf16[1024,256]{1,0:T(8,128)(2,1)S(1)}, bf16[256,256]{1,0:T(8,128)(2,1)S(1)}, bf16[128,256]{1,0:T(8,128)(2,1)S(1)}) custom-call(bf16[1024,256]{1,0:T(8,128)(2,1)S(1)} %get-tuple-element.65.h, bf16[1024,256]{1,0:T(8,128)(2,1)S(1)} %get-tuple-element.66.m, bf16[128,256]{1,0:T(8,128)(2,1)S(1)} %get-tuple-element.70.near_m, ...), custom_call_target="tpu_custom_call" | custom-call | tf_op jit(solution)/shard_map/pallas_call | solution.py:473
  41.1 2.0 %all-gather.3 = bf16[512,256]{1,0:T(8,128)(2,1)S(1)} all-gather(bf16[256,256]{1,0:T(8,128)(2,1)S(1)} %get-tuple-element.77), channel_id=5, replica_groups={{0,1},{2,3},{4,5},{6,7},{8,9},{10,11},{12,13},{14,15},{16,17},{18,19},{..., dimensions={0}, use_global_device_ids=true | all-gather | bytes 393216 | tf_op jit(solution)/shard_map/all_gather | solution.py:382
  43.1 2.4 %shard_map.134 = (bf16[1024,256]{1,0:T(8,128)(2,1)S(1)}, bf16[1024,256]{1,0:T(8,128)(2,1)S(1)}, bf16[256,256]{1,0:T(8,128)(2,1)S(1)}, bf16[128,256]{1,0:T(8,128)(2,1)S(1)}) custom-call(bf16[1024,256]{1,0:T(8,128)(2,1)S(1)} %get-tuple-element.74.h, bf16[1024,256]{1,0:T(8,128)(2,1)S(1)} %get-tuple-element.75.m, bf16[128,256]{1,0:T(8,128)(2,1)S(1)} %get-tuple-element.76.far_m, ...), custom_call_target="tpu_custom_call" | custom-call | tf_op jit(solution)/shard_map/pallas_call | solution.py:479
  45.5 8.4 %all-gather.4 = bf16[512,256]{1,0:T(8,128)(2,1)S(1)} all-gather(bf16[256,256]{1,0:T(8,128)(2,1)S(1)} %get-tuple-element.82), channel_id=6, replica_groups={{0,1},{2,3},{4,5},{6,7},{8,9},{10,11},{12,13},{14,15},{16,17},{18,19},{..., dimensions={0}, use_global_device_ids=true | all-gather | bytes 393216 | tf_op jit(solution)/shard_map/all_gather | solution.py:397
  53.9 2.4 %shard_map.135 = (bf16[1024,256]{1,0:T(8,128)(2,1)S(1)}, bf16[1024,256]{1,0:T(8,128)(2,1)S(1)}, bf16[256,256]{1,0:T(8,128)(2,1)S(1)}, bf16[128,256]{1,0:T(8,128)(2,1)S(1)}) custom-call(bf16[1024,256]{1,0:T(8,128)(2,1)S(1)} %get-tuple-element.79.h, bf16[1024,256]{1,0:T(8,128)(2,1)S(1)} %get-tuple-element.80.m, bf16[128,256]{1,0:T(8,128)(2,1)S(1)} %get-tuple-element.81.near_m, ...), custom_call_target="tpu_custom_call" | custom-call | tf_op jit(solution)/shard_map/pallas_call | solution.py:473
  56.3 2.2 %all-gather.5 = bf16[512,256]{1,0:T(8,128)(2,1)S(1)} all-gather(bf16[256,256]{1,0:T(8,128)(2,1)S(1)} %get-tuple-element.86), channel_id=7, replica_groups={{0,1},{2,3},{4,5},{6,7},{8,9},{10,11},{12,13},{14,15},{16,17},{18,19},{..., dimensions={0}, use_global_device_ids=true | all-gather | bytes 393216 | tf_op jit(solution)/shard_map/all_gather | solution.py:382
  58.4 2.4 %shard_map.136 = (bf16[1024,256]{1,0:T(8,128)(2,1)S(1)}, bf16[1024,256]{1,0:T(8,128)(2,1)S(1)}, bf16[256,256]{1,0:T(8,128)(2,1)S(1)}, bf16[128,256]{1,0:T(8,128)(2,1)S(1)}) custom-call(bf16[1024,256]{1,0:T(8,128)(2,1)S(1)} %get-tuple-element.83.h, bf16[1024,256]{1,0:T(8,128)(2,1)S(1)} %get-tuple-element.84.m, bf16[128,256]{1,0:T(8,128)(2,1)S(1)} %get-tuple-element.85.far_m, ...), custom_call_target="tpu_custom_call" | custom-call | tf_op jit(solution)/shard_map/pallas_call | solution.py:479
  60.8 8.4 %all-gather.6 = bf16[512,256]{1,0:T(8,128)(2,1)S(1)} all-gather(bf16[256,256]{1,0:T(8,128)(2,1)S(1)} %get-tuple-element.90), channel_id=8, replica_groups={{1,2},{3,4},{5,6},{7,8},{9,10},{11,12},{13,14},{15,16},{17,18},{19,20},..., dimensions={0}, use_global_device_ids=true | all-gather | bytes 393216 | tf_op jit(solution)/shard_map/all_gather | solution.py:397
  69.2 2.4 %shard_map.137 = (bf16[1024,256]{1,0:T(8,128)(2,1)S(1)}, bf16[1024,256]{1,0:T(8,128)(2,1)S(1)}, bf16[256,256]{1,0:T(8,128)(2,1)S(1)}, bf16[128,256]{1,0:T(8,128)(2,1)S(1)}) custom-call(bf16[1024,256]{1,0:T(8,128)(2,1)S(1)} %get-tuple-element.87.h, bf16[1024,256]{1,0:T(8,128)(2,1)S(1)} %get-tuple-element.88.m, bf16[128,256]{1,0:T(8,128)(2,1)S(1)} %get-tuple-element.89.near_m, ...), custom_call_target="tpu_custom_call" | custom-call | tf_op jit(solution)/shard_map/pallas_call | solution.py:473
  71.6 2.0 %all-gather.7 = bf16[512,256]{1,0:T(8,128)(2,1)S(1)} all-gather(bf16[256,256]{1,0:T(8,128)(2,1)S(1)} %get-tuple-element.94), channel_id=9, replica_groups={{0,1},{2,3},{4,5},{6,7},{8,9},{10,11},{12,13},{14,15},{16,17},{18,19},{..., dimensions={0}, use_global_device_ids=true | all-gather | bytes 393216 | tf_op jit(solution)/shard_map/all_gather | solution.py:382
  73.6 2.1 %shard_map.138 = (bf16[1024,256]{1,0:T(8,128)(2,1)S(1)}, bf16[1024,256]{1,0:T(8,128)(2,1)S(1)}, bf16[128,256]{1,0:T(8,128)(2,1)S(1)}, bf16[128,256]{1,0:T(8,128)(2,1)S(1)}) custom-call(bf16[1024,256]{1,0:T(8,128)(2,1)S(1)} %get-tuple-element.91.h, bf16[1024,256]{1,0:T(8,128)(2,1)S(1)} %get-tuple-element.92.m, bf16[128,256]{1,0:T(8,128)(2,1)S(1)} %get-tuple-element.93.far_m, ...), custom_call_target="tpu_custom_call" | custom-call | tf_op jit(solution)/shard_map/pallas_call | solution.py:479
  75.6 7.7 %all-gather.8 = bf16[256,256]{1,0:T(8,128)(2,1)S(1)} all-gather(bf16[128,256]{1,0:T(8,128)(2,1)S(1)} %get-tuple-element.98), channel_id=10, replica_groups={{1,2},{3,4},{5,6},{7,8},{9,10},{11,12},{13,14},{15,16},{17,18},{19,20},..., dimensions={0}, use_global_device_ids=true | all-gather | bytes 196608 | tf_op jit(solution)/shard_map/all_gather | solution.py:397
  83.3 3.0 %shard_map.139 = bf16[2,1024,128]{2,1,0:T(8,128)(2,1)} custom-call(bf16[1024,256]{1,0:T(8,128)(2,1)S(1)} %get-tuple-element.95.h, bf16[1024,256]{1,0:T(8,128)(2,1)S(1)} %get-tuple-element.96.m, bf16[128,256]{1,0:T(8,128)(2,1)S(1)} %get-tuple-element.97.near_m, bf16[2,128,256]{2,1,0:T(8,128)(2,1)S(1)} %get-tuple-element.71.fpick, ...), custom_call_target="tpu_custom_call" | custom-call | tf_op jit(solution)/shard_map/pallas_call | solution.py:482
  (8 shorter events, 1.1 us)
Async XLA Ops:
  1.2 24.8 %collective-permute-start.1 = (bf16[1040,128]{1,0:T(8,128)(2,1)S(1)}, bf16[1040,128]{1,0:T(8,128)(2,1)S(1)}, u32[]{:S(2)}, u32[]{:S(2)}) collective-permute-start(bf16[1040,128]{1,0:T(8,128)(2,1)S(1)} %shard_map.129.nxt.pack), channel_id=1, source_target_pairs={{0,384},{1,385},{2,386},{3,387},{4,388},{5,389},{6,390},{7,391},{8... | collective-permute-start | bytes 798728 | tf_op jit(solution)/shard_map/ppermute | solution.py:385
  10.4 28.3 %collective-permute-start.2 = (bf16[1040,128]{1,0:T(8,128)(2,1)S(1)}, bf16[1040,128]{1,0:T(8,128)(2,1)S(1)}, u32[]{:S(2)}, u32[]{:S(2)}) collective-permute-start(bf16[1040,128]{1,0:T(8,128)(2,1)S(1)} %shard_map.129.nxt.pack), channel_id=1, source_target_pairs={{0,256},{128,384},{1,257},{129,385},{2,258},{130,386},{3,259},{131... | collective-permute-start | bytes 798728 | tf_op jit(solution)/shard_map/ppermute | solution.py:385
  11.7 14.3 %collective-permute-start = (bf16[256,256]{1,0:T(8,128)(2,1)S(1)}, bf16[256,256]{1,0:T(8,128)(2,1)S(1)}, u32[]{:S(2)}, u32[]{:S(2)}) collective-permute-start(bf16[256,256]{1,0:T(8,128)(2,1)S(1)} %get-tuple-element.58), channel_id=1, source_target_pairs={{1,2},{3,4},{5,6},{7,8},{9,10},{11,12},{13,14},{15,16},{17,18},{19... | collective-permute-start | bytes 393224 | tf_op jit(solution)/shard_map/ppermute | solution.py:435
  22.2 31.6 %collective-permute-start.3 = (bf16[1040,128]{1,0:T(8,128)(2,1)S(1)}, bf16[1040,128]{1,0:T(8,128)(2,1)S(1)}, u32[]{:S(2)}, u32[]{:S(2)}) collective-permute-start(bf16[1040,128]{1,0:T(8,128)(2,1)S(1)} %shard_map.129.nxt.pack), channel_id=1, source_target_pairs={{0,128},{128,256},{256,384},{1,129},{129,257},{257,385},{2,130},{1... | collective-permute-start | bytes 798728 | tf_op jit(solution)/shard_map/ppermute | solution.py:385

commit v4 on v3

--- a/solution.py
+++ b/solution.py
@@ -9,8 +9,10 @@
 BF = jnp.bfloat16
 F32 = jnp.float32
 VM = pl.BlockSpec(memory_space=pltpu.VMEM)
+SM = pl.BlockSpec(memory_space=pltpu.SMEM)
 HB = pl.BlockSpec(memory_space=pltpu.HBM)
-CHUNK = 256
+CHUNK = 512
+LOCAL_FIRST = True
 
 
 def call(body, outs, ins, scratch=(), room=8, spaces=None):
@@ -99,20 +101,19 @@
     out[8 * d :] = jnp.concatenate(vectors, axis=0).astype(BF)
 
 
-def blocks_body(ints, rows, cols, x, adj, q, pay, si, sr, sk, xs, av, sem):
+def blocks_body(count, up, down, rows, cols, x, adj, q, pay, sr, sk, xs, av, sem):
     blk, d = av.shape[1], av.shape[2]
-    copies = fetch_all([(ints, si), (rows, sr), (cols, sk), (adj, av)], sem)
-    copies[0].wait()
-    blocks = to_partners(si[1], si[2])
+    copies = fetch_all([(rows, sr), (cols, sk), (adj, av)], sem)
+    blocks = to_partners(up[0], down[0])
     for i, block in enumerate(blocks):
         at = pl.ds(pl.multiple_of(block * blk, blk), blk)
-        copies.append(pltpu.make_async_copy(x.at[:, at, :], xs.at[i], sem.at[4 + i]))
+        copies.append(pltpu.make_async_copy(x.at[:, at, :], xs.at[i], sem.at[3 + i]))
         copies[-1].start()
-    for copy in copies[1:]:
+    for copy in copies:
         copy.wait()
     for i, (block, dst) in enumerate(zip(blocks, (q, pay))):
         row = block * blk + lax.broadcasted_iota(jnp.int32, (blk, d), 0)
-        keep = jnp.where(row < si[0], jnp.float32(1), jnp.float32(0)).astype(BF)
+        keep = jnp.where(row < count[0], jnp.float32(1), jnp.float32(0)).astype(BF)
         for m in range(2):
             dst[:blk, m * d : (m + 1) * d] = xs[i, m] * keep
         dst[blk:, d:] = keep
@@ -125,14 +126,14 @@
 
 
 def prep_body(
-    ints, rows, cols, x, adj,
+    count, up, down, rows, cols, x, adj,
     h, dense, df, mask, pick, fpick, fsel,
-    si, sr, sk, xv, av, acc, sem,
+    sr, sk, xv, av, acc, sem,
 ):
     n, d = xv.shape[1], xv.shape[2]
     blk = av.shape[1]
     last = n // blk
-    copies = fetch_all([(ints, si), (rows, sr), (cols, sk), (x, xv), (adj, av)], sem)
+    copies = fetch_all([(rows, sr), (cols, sk), (x, xv), (adj, av)], sem)
     acc[...] = jnp.zeros_like(acc)
     wide = (blk, 2 * d)
     dom = lax.axis_index("dom")
@@ -142,19 +143,18 @@
     pick[1] = flags(jnp.logical_not(odd), wide)
     fpick[0] = flags(jnp.logical_not(odd | alone), wide)
     fpick[1] = flags(odd & jnp.logical_not(alone), wide)
-    copies[0].wait()
-    near, far = to_partners(si[1], si[2])
+    near, far = to_partners(up[0], down[0])
     fsel[0] = flags(near == far, wide)
     fsel[1] = flags(near != far, wide)
-    copies[3].wait()
+    copies[2].wait()
     for b in range(last):
         at = pl.ds(pl.multiple_of(exchange_of(near, far, b, False) * blk, blk), blk)
         row = b * blk + lax.broadcasted_iota(jnp.int32, wide, 0)
-        keep = jnp.where(row < si[0], jnp.float32(1), jnp.float32(0)).astype(BF)
+        keep = jnp.where(row < count[0], jnp.float32(1), jnp.float32(0)).astype(BF)
         mask[at, :] = keep
         both = [xv[m, b * blk : (b + 1) * blk] for m in range(2)]
         h[at, :] = jnp.concatenate(both, axis=1) * keep
-    for copy in copies[1:3] + copies[4:]:
+    for copy in copies[:2] + copies[3:]:
         copy.wait()
     for k in range(av.shape[0]):
         c = sk[k]
@@ -185,18 +185,19 @@
     nseen[...] = choose(pick, haloq[0, blk:], haloq[1, blk:])
 
 
-def own_rows(h, m, halo, dense, mask):
+def layer(h, m, halo, dense, mask, pack, i, agg, hidden, c, extra=None):
+    d = pack.shape[1]
     n = m.shape[0]
-
-    def aggregate(at):
-        return lambda: dot(dense[at, :n], m[...]) + dot(dense[at, n:], halo)
-
-    chunks = [slice(r, r + CHUNK) for r in range(0, n, CHUNK)]
-    return [(at, h.at[at], aggregate(at), mask.at[at]) for at in chunks]
-
-
-def layer(chunks, pack, i, agg, hidden, c):
-    d = pack.shape[1]
+    own = [slice(r, r + CHUNK) for r in range(0, n, CHUNK)]
+    chunks = list(own)
+    if extra:
+        chunks[-1] = slice(n - CHUNK, agg.shape[0])
+
+    def rows(ref, at, j):
+        if at.stop <= n:
+            return ref[at]
+        return jnp.concatenate([ref[at.start : n], extra[j][...]], axis=0)
+
     wh = pack[2 * d + i * 2 * d : 2 * d + (i + 1) * 2 * d]
     wo = twice(pack[6 * d + i * d : 6 * d + (i + 1) * d])
     v = pack[8 * d :].astype(F32)
@@ -205,24 +206,36 @@
         r = v[j + i : j + i + 1]
         return jnp.concatenate([r, r], axis=1)
 
-    for at, _, aggregate, _ in chunks:
-        agg[at] = aggregate().astype(BF)
+    if LOCAL_FIRST:
+        for at in own:
+            c[at] = dot(dense[at, :n], m[...])
+        halo = halo()
+        for at in own:
+            agg[at] = (c[at] + dot(dense[at, n:], halo)).astype(BF)
+    else:
+        halo = halo()
+        for at in own:
+            agg[at] = (dot(dense[at, :n], m[...]) + dot(dense[at, n:], halo)).astype(BF)
+    if extra:
+        agg[n:] = extra[2]().astype(BF)
     b = row(0)
-    for at, h, _, _ in chunks:
+    for at in chunks:
+        now = rows(h, at, 0)
         pre = [
-            dot(jnp.concatenate([h[:, s : s + d], agg[at, s : s + d]], axis=1), wh) for s in (0, d)
+            dot(jnp.concatenate([now[:, s : s + d], agg[at, s : s + d]], axis=1), wh)
+            for s in (0, d)
         ]
         hidden[at] = silu_of_twice(jnp.concatenate(pre, axis=1) + b)
     b = row(2) + row(4)
-    for at, _, _, _ in chunks:
+    for at in chunks:
         c[at] = dot(hidden[at], wo) + b
     mean = twice(jnp.full((d, d), 1.0 / d, BF))
     gain = row(6)
-    for at, h, _, mask in chunks:
+    for at in chunks:
         now = c[at]
         var = dot((now * now).astype(BF), mean)
-        new = (h[...].astype(F32) + now * lax.rsqrt(var + 1e-05) * gain).astype(BF) * mask[...]
-        yield at, new
+        new = (rows(h, at, 0).astype(F32) + now * lax.rsqrt(var + 1e-05) * gain).astype(BF)
+        yield at, new * rows(mask, at, 1)
 
 
 def send_messages(new_h, new_m, nxt, i):
@@ -239,7 +252,7 @@
 def start_body(step):
     def body(h, m, halo, dense, df, mask, fsel, pack, nxt, new_h, new_m, outq, far_h, part, *rest):
         blk = outq.shape[0]
-        for at, new in layer(own_rows(h, m, halo[...], dense, mask), pack, step % 2, *rest):
+        for at, new in layer(h, m, lambda: halo[...], dense, mask, pack, step % 2, *rest):
             new_h[at] = new
         send_messages(new_h, new_m, nxt, (step + 1) % 2)
         outq[...] = new_m[:blk]
@@ -264,19 +277,21 @@
     blk, d2 = hx.shape
     d = d2 // 2
     hx[...] = choose(pick, given[0, :blk], given[1, :blk])
-    part = choose(pick, given[0, blk:], given[1, blk:])
     mx[...] = jnp.concatenate([seen[:, d:], seen[:, d:]], axis=1)
-    theirs = silu_of_twice(dot(hx[...], message_weight(pack, i)))
-    halo = jnp.concatenate([other, theirs] if is_far else [theirs, other], axis=0)
-    chunks = own_rows(h, m, halo, dense, mask)
-    chunks.append(
-        (slice(n, n + blk), hx, lambda: part.astype(F32) + dot(seen[:, :d], mine), mx)
-    )
-    for at, new in layer(chunks, pack, i, agg, hidden, c):
-        if at.start < n:
-            new_h[at] = new
-        else:
-            hx[...] = new
+
+    def halo():
+        theirs = silu_of_twice(dot(hx[...], message_weight(pack, i)))
+        return jnp.concatenate([other, theirs] if is_far else [theirs, other], axis=0)
+
+    def part():
+        given_part = choose(pick, given[0, blk:], given[1, blk:]).astype(F32)
+        return given_part + dot(seen[:, :d], mine)
+
+    extra = (hx, mx, part)
+    for at, new in layer(h, m, halo, dense, mask, pack, i, agg, hidden, c, extra):
+        new_h[at.start : min(at.stop, n)] = new[: n - at.start]
+        if at.stop > n:
+            hx[...] = new[n - at.start :]
 
 
 def far_layer_body(step):
@@ -322,24 +337,26 @@
 
 
 def last_body(step):
-    def body(h, m, near_m, fpick, far, dense, mask, pack, ints, out, agg, hidden, c, stage, si, sem):
+    def body(h, m, near_m, fpick, far, dense, mask, pack, up, down, out, *rest):
+        agg, hidden, c, stage, sem = rest
         d = pack.shape[1]
         blk = near_m.shape[0]
-        (asked,) = fetch_all([(ints, si)], sem)
-        halo = jnp.concatenate([near_m[...], choose(fpick, far[0], far[1])], axis=0)
-        asked.wait()
-        near, far = to_partners(si[1], si[2])
+
+        def halo():
+            return jnp.concatenate([near_m[...], choose(fpick, far[0], far[1])], axis=0)
+
+        ends = to_partners(up[0], down[0])
         copies = []
-        for at, new in layer(own_rows(h, m, halo, dense, mask), pack, step % 2, agg, hidden, c):
+        for at, new in layer(h, m, halo, dense, mask, pack, step % 2, agg, hidden, c):
             stage[0, at] = new[:, :d]
             stage[1, at] = new[:, d:]
             for b in range(at.start // blk, at.stop // blk):
-                to = pl.multiple_of(exchange_of(near, far, b, True) * blk, blk)
+                to = pl.multiple_of(exchange_of(*ends, b, True) * blk, blk)
                 copies.append(
                     pltpu.make_async_copy(
                         stage.at[:, b * blk : (b + 1) * blk, :],
                         out.at[:, pl.ds(to, blk), :],
-                        sem.at[1 + b],
+                        sem.at[b],
                     )
                 )
                 copies[-1].start()
@@ -419,30 +436,29 @@
         ],
     )(*weights)
     packs = [fetch(own, sections - 1)]
-    ints = jnp.concatenate([counts, send_up, send_down, jnp.zeros((125,), jnp.int32)])
-    graph = in_hbm(ints, row_blocks, col_blocks, features, adjacency)
+    graph = [counts, send_up, send_down, *in_hbm(row_blocks, col_blocks, features, adjacency)]
     q, pay = call(
         blocks_body,
         (both, both),
-        [HB] * 5,
-        integers(128, count_k, count_k)
+        [SM] * 3 + [HB] * 4,
+        integers(count_k, count_k)
         + [
             pltpu.VMEM((2, 2, blk, d), BF),
             pltpu.VMEM(adjacency.shape, BF),
-            pltpu.SemaphoreType.DMA((6,)),
+            pltpu.SemaphoreType.DMA((5,)),
         ],
     )(*graph)
     seen = lax.ppermute(pay, "dom", across)
     prep = call(
         prep_body,
         (rows, s(n, span), s(blk, span), rows, two, two, two),
-        [HB] * 5,
-        integers(128, count_k, count_k)
+        [SM] * 3 + [HB] * 4,
+        integers(count_k, count_k)
         + [
             pltpu.VMEM(features.shape, BF),
             pltpu.VMEM(adjacency.shape, BF),
             pltpu.VMEM((n // blk, n // blk + 2, blk, blk), F32),
-            pltpu.SemaphoreType.DMA((5,)),
+            pltpu.SemaphoreType.DMA((4,)),
         ],
         16,
     )
@@ -482,13 +498,12 @@
     out = call(
         last_body(steps - 1),
         s(2, n, d),
-        [VM] * 8 + [HB],
+        [VM] * 8 + [SM] * 2,
         stages(n)
         + [pltpu.VMEM((2, n, d), BF)]
-        + integers(128)
-        + [pltpu.SemaphoreType.DMA((1 + n // blk,))],
+        + [pltpu.SemaphoreType.DMA((n // blk,))],
         spaces=HB,
-    )(h, m, near_m, fpick, far_gather(pay, steps - 1), dense, mask, packs[-1], graph[0])
+    )(h, m, near_m, fpick, far_gather(pay, steps - 1), dense, mask, packs[-1], send_up, send_down)
     return out[None]
 
 

time: 86.8 us -> 84.5 us (0.974)
  Pallas kernels: 24.5 us -> 22.8 us
    pallas_call x2, Pallas kernels: 5.02 us -> 4 us  [the longest x1 2.44 us: shards(): call(last_body(steps - 1), s(2, n, d), [VM] * 8 + [SM] * 2, stages(n) + [...]
  transfers between devices with their start and end apart: 4 -> 4, of which waited for: 0 -> 0; matrix products, arithmetic and copies ran while one was open for 1% -> 0% of each run, Pallas kernels for 13% -> 12%
where the time goes in v4:
time: 84.5 us; the launch traced here: 84.2 us
  blocking collectives  42.9 us (51%)
  Pallas kernels  22.8 us (27%)
  starting transfers between devices  16.3 us (19%)
  between operations  2.24 us (3%)
    all_gather x4, blocking collectives, far_gather(): return lax.all_gather(q, ('section', 'dom'), axis_index_groups=groups)  33 us
    ppermute x1, starting transfers between devices, shards(): seen = lax.ppermute(pay, 'dom', across)  10.6 us
    all_gather x5, blocking collectives, near_gather(): return lax.all_gather(q, 'dom', axis_index_groups=near_pairs)  9.88 us
    pallas_call x3, Pallas kernels, shards(): call(far_layer_body(step), (rows, rows, both, wide), [VM] * 11, more)  6.75 us
    pallas_call x3, Pallas kernels, shards(): call(near_layer_body(step, tail), (rows, rows, wide if tail else both, wi...  6.57 us
    ppermute x3, starting transfers between devices, fetch(): lax.ppermute(own, 'section', [(i, i + k) for i in range(sections - k)])  5.68 us
    pallas_call x1, Pallas kernels, shards(): call(last_body(steps - 1), s(2, n, d), [VM] * 8 + [SM] * 2, stages(n) + [...  2.44 us
    pallas_call x1, Pallas kernels, shards(): h, dense, df, mask, pick, fpick, fsel = prep(*graph)  1.92 us
  transfers between devices with their start and end apart: 4, of which 0 were waited for; matrix products, arithmetic and copies ran while one was open for 0% of the time, Pallas kernels for 12%

profile of v4, /device:TPU:36, one launch (start us, length us, event | category | flops | bytes accessed | tf_op | source)
XLA Modules:
  0.0 84.2 jit_solution(14233880035572221110)
XLA Ops:
  0.0 1.1 %shard_map.129.nxt.pack = bf16[1040,128]{1,0:T(8,128)(2,1)S(1)} custom-call(bf16[2,128,128]{2,1,0:T(8,128)(2,1)} %wm.1, bf16[2,256,128]{2,1,0:T(8,128)(2,1)} %wh.1, bf16[2,128]{1,0:T(2,128)(2,1)} %bh.1, bf16[2,128,128]{2,1,0:T(8,128)(2,1)} %wo.1, bf16[2,128]{1,0:T(2,128)(2,1)} %bo.1, bf16[2,128]{1,0:T(2,128)(2,1)} %gain.1), custom_call_target="tpu_custom_call" | custom-call | tf_op jit(solution)/shard_map/pallas_call | solution.py:424
  1.2 0.7 collective-permute-start.1
  3.8 1.9 %shard_map.127 = (bf16[1024,256]{1,0:T(8,128)(2,1)S(1)}, bf16[1024,1280]{1,0:T(8,128)(2,1)S(1)}, bf16[128,1280]{1,0:T(8,128)(2,1)S(1)}, bf16[1024,256]{1,0:T(8,1...) custom-call(s32[1]{0:T(128)S(6)} %copy.14.count, ...), custom_call_target="tpu_custom_call" | custom-call | tf_op jit(solution)/shard_map/pallas_call | solution.py:465
  5.7 1.6 %shard_map.128 = (bf16[256,256]{1,0:T(8,128)(2,1)S(1)}, bf16[256,256]{1,0:T(8,128)(2,1)S(1)}) custom-call(s32[1]{0:T(128)S(6)} %copy.14.count, s32[1]{0:T(128)S(6)} %copy.15.up, s32[1]{0:T(128)S(6)} %copy.16.down, s32[24]{0:T(128)} %rows.3, s32[24]{0:T(128)} %cols.3, bf16[2,1024,128]{2,1,0:T(8,128)(2,1)} %x.3, bf16[24,128,128]{2,1,0:T(8,128)(2,1)} %adj.3), custom_call_target="tpu_custom_call" | custom-call | tf_op jit(solution)/shard_map/pallas_call | solution.py:440
  7.3 2.0 %all-gather = bf16[512,256]{1,0:T(8,128)(2,1)S(1)} all-gather(bf16[256,256]{1,0:T(8,128)(2,1)S(1)} %get-tuple-element.56), channel_id=2, replica_groups={{0,1},{2,3},{4,5},{6,7},{8,9},{10,11},{12,13},{14,15},{16,17},{18,19},{..., dimensions={0}, use_global_device_ids=true | all-gather | bytes 393216 | tf_op jit(solution)/shard_map/all_gather | solution.py:399
  9.3 1.3 %collective-permute-start.2 = (bf16[1040,128]{1,0:T(8,128)(2,1)S(1)}, bf16[1040,128]{1,0:T(8,128)(2,1)S(1)}, u32[]{:S(2)}, u32[]{:S(2)}) collective-permute-start(bf16[1040,128]{1,0:T(8,128)(2,1)S(1)} %shard_map.129.nxt.pack), channel_id=1, source_target_pairs={{0,256},{128,384},{1,257},{129,385},{2,258},{130,386},{3,259},{131... | collective-permute-start | bytes 798728 | tf_op jit(solution)/shard_map/ppermute | solution.py:402
  10.6 10.6 %collective-permute-start = (bf16[256,256]{1,0:T(8,128)(2,1)S(1)}, bf16[256,256]{1,0:T(8,128)(2,1)S(1)}, u32[]{:S(2)}, u32[]{:S(2)}) collective-permute-start(bf16[256,256]{1,0:T(8,128)(2,1)S(1)} %get-tuple-element.58), channel_id=1, source_target_pairs={{1,2},{3,4},{5,6},{7,8},{9,10},{11,12},{13,14},{15,16},{17,18},{19... | collective-permute-start | bytes 393224 | tf_op jit(solution)/shard_map/ppermute | solution.py:451
  21.1 3.7 %collective-permute-start.3 = (bf16[1040,128]{1,0:T(8,128)(2,1)S(1)}, bf16[1040,128]{1,0:T(8,128)(2,1)S(1)}, u32[]{:S(2)}, u32[]{:S(2)}) collective-permute-start(bf16[1040,128]{1,0:T(8,128)(2,1)S(1)} %shard_map.129.nxt.pack), channel_id=1, source_target_pairs={{0,128},{128,256},{256,384},{1,129},{129,257},{257,385},{2,130},{1... | collective-permute-start | bytes 798728 | tf_op jit(solution)/shard_map/ppermute | solution.py:402
  25.3 1.9 %shard_map.131 = (bf16[1024,256]{1,0:T(8,128)(2,1)S(1)}, bf16[1024,256]{1,0:T(8,128)(2,1)S(1)}, bf16[128,256]{1,0:T(8,128)(2,1)S(1)}, bf16[128,256]{1,0:T(8,128)(2,1)S(1)}, f32[128,256]{1,0:T(8,128)S(1)}) custom-call(bf16[1024,256]{1,0:T(8,128)(2,1)S(1)} %get-tuple-element.52.h, bf16[1024,256]{1,0:T(8,128)(2,1)S(1)} %get-tuple-element.59.m, ...), custom_call_target="tpu_custom_call" | custom-call | tf_op jit(solution)/shard_map/pallas_call | solution.py:482
  27.2 1.9 %all-gather.1 = bf16[256,256]{1,0:T(8,128)(2,1)S(1)} all-gather(bf16[128,256]{1,0:T(8,128)(2,1)S(1)} %get-tuple-element.67), channel_id=3, replica_groups={{0,1},{2,3},{4,5},{6,7},{8,9},{10,11},{12,13},{14,15},{16,17},{18,19},{..., dimensions={0}, use_global_device_ids=true | all-gather | bytes 196608 | tf_op jit(solution)/shard_map/all_gather | solution.py:399
  29.2 8.4 %all-gather.2 = bf16[512,256]{1,0:T(8,128)(2,1)S(1)} all-gather(bf16[256,256]{1,0:T(8,128)(2,1)S(1)} %get-tuple-element.72), channel_id=4, replica_groups={{0,1},{2,3},{4,5},{6,7},{8,9},{10,11},{12,13},{14,15},{16,17},{18,19},{..., dimensions={0}, use_global_device_ids=true | all-gather | bytes 393216 | tf_op jit(solution)/shard_map/all_gather | solution.py:414
  37.6 2.3 %shard_map.133 = (bf16[1024,256]{1,0:T(8,128)(2,1)S(1)}, bf16[1024,256]{1,0:T(8,128)(2,1)S(1)}, bf16[256,256]{1,0:T(8,128)(2,1)S(1)}, bf16[128,256]{1,0:T(8,128)(2,1)S(1)}) custom-call(bf16[1024,256]{1,0:T(8,128)(2,1)S(1)} %get-tuple-element.65.h, bf16[1024,256]{1,0:T(8,128)(2,1)S(1)} %get-tuple-element.66.m, bf16[128,256]{1,0:T(8,128)(2,1)S(1)} %get-tuple-element.70.near_m, ...), custom_call_target="tpu_custom_call" | custom-call | tf_op jit(solution)/shard_map/pallas_call | solution.py:489
  39.9 2.0 %all-gather.3 = bf16[512,256]{1,0:T(8,128)(2,1)S(1)} all-gather(bf16[256,256]{1,0:T(8,128)(2,1)S(1)} %get-tuple-element.77), channel_id=5, replica_groups={{0,1},{2,3},{4,5},{6,7},{8,9},{10,11},{12,13},{14,15},{16,17},{18,19},{..., dimensions={0}, use_global_device_ids=true | all-gather | bytes 393216 | tf_op jit(solution)/shard_map/all_gather | solution.py:399
  41.9 2.3 %shard_map.134 = (bf16[1024,256]{1,0:T(8,128)(2,1)S(1)}, bf16[1024,256]{1,0:T(8,128)(2,1)S(1)}, bf16[256,256]{1,0:T(8,128)(2,1)S(1)}, bf16[128,256]{1,0:T(8,128)(2,1)S(1)}) custom-call(bf16[1024,256]{1,0:T(8,128)(2,1)S(1)} %get-tuple-element.74.h, bf16[1024,256]{1,0:T(8,128)(2,1)S(1)} %get-tuple-element.75.m, bf16[128,256]{1,0:T(8,128)(2,1)S(1)} %get-tuple-element.76.far_m, ...), custom_call_target="tpu_custom_call" | custom-call | tf_op jit(solution)/shard_map/pallas_call | solution.py:495
  44.2 8.4 %all-gather.4 = bf16[512,256]{1,0:T(8,128)(2,1)S(1)} all-gather(bf16[256,256]{1,0:T(8,128)(2,1)S(1)} %get-tuple-element.82), channel_id=6, replica_groups={{0,1},{2,3},{4,5},{6,7},{8,9},{10,11},{12,13},{14,15},{16,17},{18,19},{..., dimensions={0}, use_global_device_ids=true | all-gather | bytes 393216 | tf_op jit(solution)/shard_map/all_gather | solution.py:414
  52.5 2.2 %shard_map.135 = (bf16[1024,256]{1,0:T(8,128)(2,1)S(1)}, bf16[1024,256]{1,0:T(8,128)(2,1)S(1)}, bf16[256,256]{1,0:T(8,128)(2,1)S(1)}, bf16[128,256]{1,0:T(8,128)(2,1)S(1)}) custom-call(bf16[1024,256]{1,0:T(8,128)(2,1)S(1)} %get-tuple-element.79.h, bf16[1024,256]{1,0:T(8,128)(2,1)S(1)} %get-tuple-element.80.m, bf16[128,256]{1,0:T(8,128)(2,1)S(1)} %get-tuple-element.81.near_m, ...), custom_call_target="tpu_custom_call" | custom-call | tf_op jit(solution)/shard_map/pallas_call | solution.py:489
  54.8 2.0 %all-gather.5 = bf16[512,256]{1,0:T(8,128)(2,1)S(1)} all-gather(bf16[256,256]{1,0:T(8,128)(2,1)S(1)} %get-tuple-element.86), channel_id=7, replica_groups={{0,1},{2,3},{4,5},{6,7},{8,9},{10,11},{12,13},{14,15},{16,17},{18,19},{..., dimensions={0}, use_global_device_ids=true | all-gather | bytes 393216 | tf_op jit(solution)/shard_map/all_gather | solution.py:399
  56.8 2.2 %shard_map.136 = (bf16[1024,256]{1,0:T(8,128)(2,1)S(1)}, bf16[1024,256]{1,0:T(8,128)(2,1)S(1)}, bf16[256,256]{1,0:T(8,128)(2,1)S(1)}, bf16[128,256]{1,0:T(8,128)(2,1)S(1)}) custom-call(bf16[1024,256]{1,0:T(8,128)(2,1)S(1)} %get-tuple-element.83.h, bf16[1024,256]{1,0:T(8,128)(2,1)S(1)} %get-tuple-element.84.m, bf16[128,256]{1,0:T(8,128)(2,1)S(1)} %get-tuple-element.85.far_m, ...), custom_call_target="tpu_custom_call" | custom-call | tf_op jit(solution)/shard_map/pallas_call | solution.py:495
  59.0 8.6 %all-gather.6 = bf16[512,256]{1,0:T(8,128)(2,1)S(1)} all-gather(bf16[256,256]{1,0:T(8,128)(2,1)S(1)} %get-tuple-element.90), channel_id=8, replica_groups={{1,2},{3,4},{5,6},{7,8},{9,10},{11,12},{13,14},{15,16},{17,18},{19,20},..., dimensions={0}, use_global_device_ids=true | all-gather | bytes 393216 | tf_op jit(solution)/shard_map/all_gather | solution.py:414
  67.6 2.3 %shard_map.137 = (bf16[1024,256]{1,0:T(8,128)(2,1)S(1)}, bf16[1024,256]{1,0:T(8,128)(2,1)S(1)}, bf16[256,256]{1,0:T(8,128)(2,1)S(1)}, bf16[128,256]{1,0:T(8,128)(2,1)S(1)}) custom-call(bf16[1024,256]{1,0:T(8,128)(2,1)S(1)} %get-tuple-element.87.h, bf16[1024,256]{1,0:T(8,128)(2,1)S(1)} %get-tuple-element.88.m, bf16[128,256]{1,0:T(8,128)(2,1)S(1)} %get-tuple-element.89.near_m, ...), custom_call_target="tpu_custom_call" | custom-call | tf_op jit(solution)/shard_map/pallas_call | solution.py:489
  69.9 2.0 %all-gather.7 = bf16[512,256]{1,0:T(8,128)(2,1)S(1)} all-gather(bf16[256,256]{1,0:T(8,128)(2,1)S(1)} %get-tuple-element.94), channel_id=9, replica_groups={{0,1},{2,3},{4,5},{6,7},{8,9},{10,11},{12,13},{14,15},{16,17},{18,19},{..., dimensions={0}, use_global_device_ids=true | all-gather | bytes 393216 | tf_op jit(solution)/shard_map/all_gather | solution.py:399
  71.9 2.0 %shard_map.138 = (bf16[1024,256]{1,0:T(8,128)(2,1)S(1)}, bf16[1024,256]{1,0:T(8,128)(2,1)S(1)}, bf16[128,256]{1,0:T(8,128)(2,1)S(1)}, bf16[128,256]{1,0:T(8,128)(2,1)S(1)}) custom-call(bf16[1024,256]{1,0:T(8,128)(2,1)S(1)} %get-tuple-element.91.h, bf16[1024,256]{1,0:T(8,128)(2,1)S(1)} %get-tuple-element.92.m, bf16[128,256]{1,0:T(8,128)(2,1)S(1)} %get-tuple-element.93.far_m, ...), custom_call_target="tpu_custom_call" | custom-call | tf_op jit(solution)/shard_map/pallas_call | solution.py:495
  73.9 7.7 %all-gather.8 = bf16[256,256]{1,0:T(8,128)(2,1)S(1)} all-gather(bf16[128,256]{1,0:T(8,128)(2,1)S(1)} %get-tuple-element.98), channel_id=10, replica_groups={{1,2},{3,4},{5,6},{7,8},{9,10},{11,12},{13,14},{15,16},{17,18},{19,20},..., dimensions={0}, use_global_device_ids=true | all-gather | bytes 196608 | tf_op jit(solution)/shard_map/all_gather | solution.py:414
  81.6 2.4 %shard_map.139 = bf16[2,1024,128]{2,1,0:T(8,128)(2,1)} custom-call(bf16[1024,256]{1,0:T(8,128)(2,1)S(1)} %get-tuple-element.95.h, bf16[1024,256]{1,0:T(8,128)(2,1)S(1)} %get-tuple-element.96.m, bf16[128,256]{1,0:T(8,128)(2,1)S(1)} %get-tuple-element.97.near_m, bf16[2,128,256]{2,1,0:T(8,128)(2,1)S(1)} %get-tuple-element.71.fpick, ...), custom_call_target="tpu_custom_call" | custom-call | tf_op jit(solution)/shard_map/pallas_call | solution.py:498
  (6 shorter events, 0.5 us)
Async XLA Ops:
  1.2 23.7 %collective-permute-start.1 = (bf16[1040,128]{1,0:T(8,128)(2,1)S(1)}, bf16[1040,128]{1,0:T(8,128)(2,1)S(1)}, u32[]{:S(2)}, u32[]{:S(2)}) collective-permute-start(bf16[1040,128]{1,0:T(8,128)(2,1)S(1)} %shard_map.129.nxt.pack), channel_id=1, source_target_pairs={{0,384},{1,385},{2,386},{3,387},{4,388},{5,389},{6,390},{7,391},{8... | collective-permute-start | bytes 798728 | tf_op jit(solution)/shard_map/ppermute | solution.py:402
  9.3 28.3 %collective-permute-start.2 = (bf16[1040,128]{1,0:T(8,128)(2,1)S(1)}, bf16[1040,128]{1,0:T(8,128)(2,1)S(1)}, u32[]{:S(2)}, u32[]{:S(2)}) collective-permute-start(bf16[1040,128]{1,0:T(8,128)(2,1)S(1)} %shard_map.129.nxt.pack), channel_id=1, source_target_pairs={{0,256},{128,384},{1,257},{129,385},{2,258},{130,386},{3,259},{131... | collective-permute-start | bytes 798728 | tf_op jit(solution)/shard_map/ppermute | solution.py:402
  10.6 14.3 %collective-permute-start = (bf16[256,256]{1,0:T(8,128)(2,1)S(1)}, bf16[256,256]{1,0:T(8,128)(2,1)S(1)}, u32[]{:S(2)}, u32[]{:S(2)}) collective-permute-start(bf16[256,256]{1,0:T(8,128)(2,1)S(1)} %get-tuple-element.58), channel_id=1, source_target_pairs={{1,2},{3,4},{5,6},{7,8},{9,10},{11,12},{13,14},{15,16},{17,18},{19... | collective-permute-start | bytes 393224 | tf_op jit(solution)/shard_map/ppermute | solution.py:451
  21.1 31.4 %collective-permute-start.3 = (bf16[1040,128]{1,0:T(8,128)(2,1)S(1)}, bf16[1040,128]{1,0:T(8,128)(2,1)S(1)}, u32[]{:S(2)}, u32[]{:S(2)}) collective-permute-start(bf16[1040,128]{1,0:T(8,128)(2,1)S(1)} %shard_map.129.nxt.pack), channel_id=1, source_target_pairs={{0,128},{128,256},{256,384},{1,129},{129,257},{257,385},{2,130},{1... | collective-permute-start | bytes 798728 | tf_op jit(solution)/shard_map/ppermute | solution.py:402

commit v5 on v4

--- a/solution.py
+++ b/solution.py
@@ -5,23 +5,22 @@
 from jax.experimental.pallas import tpu as pltpu
 from jax.sharding import PartitionSpec as P
 
-
 BF = jnp.bfloat16
 F32 = jnp.float32
 VM = pl.BlockSpec(memory_space=pltpu.VMEM)
 SM = pl.BlockSpec(memory_space=pltpu.SMEM)
 HB = pl.BlockSpec(memory_space=pltpu.HBM)
 CHUNK = 512
-LOCAL_FIRST = True
-
-
-def call(body, outs, ins, scratch=(), room=8, spaces=None):
+
+
+def call(body, outs, ins, name, scratch=(), room=8, spaces=None):
     return pl.pallas_call(
         body,
         out_shape=outs,
         in_specs=ins,
         out_specs=spaces or jax.tree.map(lambda _: VM, outs),
         scratch_shapes=list(scratch),
+        name=name,
         compiler_params=pltpu.CompilerParams(vmem_limit_bytes=room << 20),
     )
 
@@ -101,33 +100,9 @@
     out[8 * d :] = jnp.concatenate(vectors, axis=0).astype(BF)
 
 
-def blocks_body(count, up, down, rows, cols, x, adj, q, pay, sr, sk, xs, av, sem):
-    blk, d = av.shape[1], av.shape[2]
-    copies = fetch_all([(rows, sr), (cols, sk), (adj, av)], sem)
-    blocks = to_partners(up[0], down[0])
-    for i, block in enumerate(blocks):
-        at = pl.ds(pl.multiple_of(block * blk, blk), blk)
-        copies.append(pltpu.make_async_copy(x.at[:, at, :], xs.at[i], sem.at[3 + i]))
-        copies[-1].start()
-    for copy in copies:
-        copy.wait()
-    for i, (block, dst) in enumerate(zip(blocks, (q, pay))):
-        row = block * blk + lax.broadcasted_iota(jnp.int32, (blk, d), 0)
-        keep = jnp.where(row < count[0], jnp.float32(1), jnp.float32(0)).astype(BF)
-        for m in range(2):
-            dst[:blk, m * d : (m + 1) * d] = xs[i, m] * keep
-        dst[blk:, d:] = keep
-        col = jnp.where(parity() == i, 9, 8)
-        seen = jnp.zeros((blk, d), F32)
-        for k in range(av.shape[0]):
-            hit = (sr[k] == block) & (sk[k] == col)
-            seen = seen + av[k].astype(F32) * jnp.where(hit, jnp.float32(1), jnp.float32(0))
-        dst[blk:, :d] = seen.astype(BF)
-
-
 def prep_body(
     count, up, down, rows, cols, x, adj,
-    h, dense, df, mask, pick, fpick, fsel,
+    h, dense, df, mask, pick, fpick, fsel, q, view,
     sr, sk, xv, av, acc, sem,
 ):
     n, d = xv.shape[1], xv.shape[2]
@@ -169,6 +144,9 @@
             dense[r * blk : (r + 1) * blk, c * blk : (c + 1) * blk] = acc[r, c].astype(BF)
     at = pl.ds(pl.multiple_of(jnp.where(near == far, 0, 1) * blk, blk), blk)
     df[...] = dense[at, :]
+    q[:blk] = h[:blk]
+    q[blk:] = jnp.concatenate([dense[:blk, n : n + blk], mask[:blk, :d]], axis=1)
+    view[...] = jnp.concatenate([df[:, n + blk :], mask[at, :d]], axis=1)
 
 
 def message_weight(pack, i):
@@ -176,13 +154,18 @@
     return twice(pack[i * d : (i + 1) * d])
 
 
-def first_body(h, pick, haloq, halor, pack, m, halo, nseen):
+def first_body(h, pick, fsel, near, df, view, pack, m, near_m, nseen, pay):
     w = message_weight(pack, 0)
+    blk = nseen.shape[0]
+    n = m.shape[0]
+    theirs = silu_of_twice(dot(choose(pick, near[0, :blk], near[1, :blk]), w))
     m[...] = silu_of_twice(dot(h[...], w))
-    blk = nseen.shape[0]
-    both = jnp.concatenate([choose(pick, haloq[0, :blk], haloq[1, :blk]), halor[:blk]], axis=0)
-    halo[...] = silu_of_twice(dot(both, w))
-    nseen[...] = choose(pick, haloq[0, blk:], haloq[1, blk:])
+    near_m[...] = theirs
+    nseen[...] = choose(pick, near[0, blk:], near[1, blk:])
+    pay[:blk] = far_block(fsel, h, blk)
+    part = dot(df[:, :n], m[...]) + dot(df[:, n : n + blk], theirs)
+    pay[blk : 2 * blk] = part.astype(BF)
+    pay[2 * blk :] = view[...]
 
 
 def layer(h, m, halo, dense, mask, pack, i, agg, hidden, c, extra=None):
@@ -206,16 +189,11 @@
         r = v[j + i : j + i + 1]
         return jnp.concatenate([r, r], axis=1)
 
-    if LOCAL_FIRST:
-        for at in own:
-            c[at] = dot(dense[at, :n], m[...])
-        halo = halo()
-        for at in own:
-            agg[at] = (c[at] + dot(dense[at, n:], halo)).astype(BF)
-    else:
-        halo = halo()
-        for at in own:
-            agg[at] = (dot(dense[at, :n], m[...]) + dot(dense[at, n:], halo)).astype(BF)
+    for at in own:
+        c[at] = dot(dense[at, :n], m[...])
+    halo = halo()
+    for at in own:
+        agg[at] = (c[at] + dot(dense[at, n:], halo)).astype(BF)
     if extra:
         agg[n:] = extra[2]().astype(BF)
     b = row(0)
@@ -249,28 +227,6 @@
     return choose(fsel, ref[:blk], ref[blk : 2 * blk])
 
 
-def start_body(step):
-    def body(h, m, halo, dense, df, mask, fsel, pack, nxt, new_h, new_m, outq, far_h, part, *rest):
-        blk = outq.shape[0]
-        for at, new in layer(h, m, lambda: halo[...], dense, mask, pack, step % 2, *rest):
-            new_h[at] = new
-        send_messages(new_h, new_m, nxt, (step + 1) % 2)
-        outq[...] = new_m[:blk]
-        far_h[...] = far_block(fsel, new_h, blk)
-        part[...] = dot(df[:, : new_m.shape[0]], new_m[...])
-
-    return body
-
-
-def pay_body(pick, haloq, df, far_h, part, pay, near_m):
-    blk = far_h.shape[0]
-    n = df.shape[1] - 2 * blk
-    near = choose(pick, haloq[0], haloq[1])
-    near_m[...] = near
-    pay[:blk] = far_h[...]
-    pay[blk:] = (part[...] + dot(df[:, n : n + blk], near)).astype(BF)
-
-
 def partner_layer(h, m, given, pick, seen, mine, other, is_far, dense, mask, pack, i, new_h, rest):
     agg, hidden, c, hx, mx = rest
     n = m.shape[0]
@@ -284,7 +240,7 @@
         return jnp.concatenate([other, theirs] if is_far else [theirs, other], axis=0)
 
     def part():
-        given_part = choose(pick, given[0, blk:], given[1, blk:]).astype(F32)
+        given_part = choose(pick, given[0, blk : 2 * blk], given[1, blk : 2 * blk]).astype(F32)
         return given_part + dot(seen[:, :d], mine)
 
     extra = (hx, mx, part)
@@ -294,27 +250,33 @@
             hx[...] = new[n - at.start :]
 
 
-def far_layer_body(step):
+def far_layer_body(step, begin, tail):
     def body(h, m, near_m, fpick, far, dense, mask, fsel, seen, pack, nxt, *rest):
         new_h, new_m, pay, far_m = rest[:4]
-        rest = rest[4:]
         n, blk = m.shape[0], far_m.shape[0]
+        if begin:
+            seen = rest[4]
+            seen[...] = choose(fpick, far[0, 2 * blk :], far[1, 2 * blk :])
+        rest = rest[-5:]
         mine = far_block(fsel, m, blk)
         partner_layer(
-            h, m, far, fpick, seen[blk:], mine, near_m[...], True, dense, mask, pack, step % 2,
+            h, m, far, fpick, seen[...], mine, near_m[...], True, dense, mask, pack, step % 2,
             new_h, rest,
         )
         send_messages(new_h, new_m, nxt, (step + 1) % 2)
         theirs = silu_of_twice(dot(rest[3][...], message_weight(nxt, (step + 1) % 2)))
         far_m[...] = theirs
-        pay[:blk] = new_h[:blk]
-        part = dot(dense[:blk, :n], new_m[...]) + dot(dense[:blk, n + blk :], theirs)
-        pay[blk:] = part.astype(BF)
+        if tail:
+            pay[...] = new_m[:blk]
+        else:
+            pay[:blk] = new_h[:blk]
+            part = dot(dense[:blk, :n], new_m[...]) + dot(dense[:blk, n + blk :], theirs)
+            pay[blk:] = part.astype(BF)
 
     return body
 
 
-def near_layer_body(step, tail):
+def near_layer_body(step):
     def body(h, m, far_m, pick, near, dense, df, mask, fsel, nseen, pack, nxt, *rest):
         new_h, new_m, pay, near_m = rest[:4]
         rest = rest[4:]
@@ -326,24 +288,21 @@
         send_messages(new_h, new_m, nxt, (step + 1) % 2)
         theirs = silu_of_twice(dot(rest[3][...], message_weight(nxt, (step + 1) % 2)))
         near_m[...] = theirs
-        if tail:
-            pay[...] = far_block(fsel, new_m, blk)
-        else:
-            pay[:blk] = far_block(fsel, new_h, blk)
-            part = dot(df[:, :n], new_m[...]) + dot(df[:, n : n + blk], theirs)
-            pay[blk:] = part.astype(BF)
+        pay[:blk] = far_block(fsel, new_h, blk)
+        part = dot(df[:, :n], new_m[...]) + dot(df[:, n : n + blk], theirs)
+        pay[blk:] = part.astype(BF)
 
     return body
 
 
 def last_body(step):
-    def body(h, m, near_m, fpick, far, dense, mask, pack, up, down, out, *rest):
+    def body(h, m, pick, near, far_m, dense, mask, pack, up, down, out, *rest):
         agg, hidden, c, stage, sem = rest
         d = pack.shape[1]
-        blk = near_m.shape[0]
+        blk = far_m.shape[0]
 
         def halo():
-            return jnp.concatenate([near_m[...], choose(fpick, far[0], far[1])], axis=0)
+            return jnp.concatenate([choose(pick, near[0], near[1]), far_m[...]], axis=0)
 
         ends = to_partners(up[0], down[0])
         copies = []
@@ -389,7 +348,6 @@
     steps = layers * sections
     near_pairs = [[i, i + 1] for i in range(0, doms, 2)]
     far_pairs = [[i, i + 1] for i in range(1, doms - 1, 2)]
-    across = [(a, b) for a, b in far_pairs] + [(b, a) for a, b in far_pairs]
     far_pairs = far_pairs + [[0, doms - 1]]
 
     def s(*shape, dtype=BF):
@@ -407,7 +365,7 @@
     def far_gather(q, step):
         groups = []
         for section in range(sections):
-            begun = layers * (sections - 1 - section) <= step + 1
+            begun = step == 0 or layers * (sections - 1 - section) <= step + 1
             groups += [
                 [section * doms + i for i in pair] for pair in (far_pairs if begun else near_pairs)
             ]
@@ -425,6 +383,7 @@
         pack_body,
         s(layers * 4 * d + 16, d),
         [HB] * 6,
+        "pack",
         [
             pltpu.VMEM((layers, d, d), BF),
             pltpu.VMEM((layers, 2 * d, d), BF),
@@ -437,22 +396,11 @@
     )(*weights)
     packs = [fetch(own, sections - 1)]
     graph = [counts, send_up, send_down, *in_hbm(row_blocks, col_blocks, features, adjacency)]
-    q, pay = call(
-        blocks_body,
-        (both, both),
+    h, dense, df, mask, pick, fpick, fsel, q, view = call(
+        prep_body,
+        (rows, s(n, span), s(blk, span), rows, two, two, two, both, wide),
         [SM] * 3 + [HB] * 4,
-        integers(count_k, count_k)
-        + [
-            pltpu.VMEM((2, 2, blk, d), BF),
-            pltpu.VMEM(adjacency.shape, BF),
-            pltpu.SemaphoreType.DMA((5,)),
-        ],
-    )(*graph)
-    seen = lax.ppermute(pay, "dom", across)
-    prep = call(
-        prep_body,
-        (rows, s(n, span), s(blk, span), rows, two, two, two),
-        [SM] * 3 + [HB] * 4,
+        "prep",
         integers(count_k, count_k)
         + [
             pltpu.VMEM(features.shape, BF),
@@ -461,13 +409,13 @@
             pltpu.SemaphoreType.DMA((4,)),
         ],
         16,
-    )
-    h, dense, df, mask, pick, fpick, fsel = prep(*graph)
-    q, pick = lax.optimization_barrier((q, pick))
-    haloq = near_gather(q)
-    later, haloq = lax.optimization_barrier((own, haloq))
+    )(*graph)
+    near = near_gather(q)
+    later, near = lax.optimization_barrier((own, near))
     packs += [fetch(later, k) for k in range(sections - 2, 0, -1)] + [own]
-    m, halo, nseen = call(first_body, (rows, both, wide), [VM] * 5)(h, pick, haloq, seen, packs[0])
+    m, near_m, nseen, pay = call(
+        first_body, (rows, wide, wide, s(3 * blk, 2 * d)), [VM] * 7, "first"
+    )(h, pick, fsel, near, df, view, packs[0])
 
     def stages(k):
         return [
@@ -479,31 +427,36 @@
     def weights_at(step):
         return packs[step // layers], packs[(step + 1) // layers]
 
-    h, m, q, far_h, part = call(
-        start_body(0), (rows, rows, wide, wide, s(blk, 2 * d, dtype=F32)), [VM] * 9, stages(n)
-    )(h, m, halo, dense, df, mask, fsel, *weights_at(0))
-    pay, near_m = call(pay_body, (both, wide), [VM] * 5)(pick, near_gather(q), df, far_h, part)
     more = stages(n + blk) + [pltpu.VMEM((blk, 2 * d), BF)] * 2
-    for step in range(1, steps - 1, 2):
+    seen = view
+    for step in range(0, steps, 2):
+        tail = step + 2 == steps
         asked = far_gather(pay, step)
-        h, m, pay, far_m = call(
-            far_layer_body(step), (rows, rows, both, wide), [VM] * 11, more
+        h, m, pay, far_m, *kept = call(
+            far_layer_body(step, step == 0, tail),
+            (rows, rows, wide if tail else both, wide) + ((wide,) if step == 0 else ()),
+            [VM] * 11,
+            f"layer{step}",
+            more,
         )(h, m, near_m, fpick, asked, dense, mask, fsel, seen, *weights_at(step))
+        if kept:
+            seen = kept[0]
         asked = near_gather(pay)
-        step += 1
-        tail = step + 2 == steps
-        h, m, pay, near_m = call(
-            near_layer_body(step, tail), (rows, rows, wide if tail else both, wide), [VM] * 12, more
-        )(h, m, far_m, pick, asked, dense, df, mask, fsel, nseen, *weights_at(step))
+        if not tail:
+            step += 1
+            h, m, pay, near_m = call(
+                near_layer_body(step), (rows, rows, both, wide), [VM] * 12, f"layer{step}", more
+            )(h, m, far_m, pick, asked, dense, df, mask, fsel, nseen, *weights_at(step))
     out = call(
         last_body(steps - 1),
         s(2, n, d),
         [VM] * 8 + [SM] * 2,
+        f"layer{steps - 1}",
         stages(n)
         + [pltpu.VMEM((2, n, d), BF)]
         + [pltpu.SemaphoreType.DMA((n // blk,))],
         spaces=HB,
-    )(h, m, near_m, fpick, far_gather(pay, steps - 1), dense, mask, packs[-1], send_up, send_down)
+    )(h, m, pick, asked, far_m, dense, mask, packs[-1], send_up, send_down)
     return out[None]
 
 

time: 84.5 us -> 80.9 us (0.957)
  the two profiles are of different devices: /device:TPU:36 before, /device:TPU:5 now
where the time goes in v5:
time: 80.9 us; the launch traced here: 80.6 us
  blocking collectives  51.3 us (63%)
  Pallas kernels  21.7 us (27%)
  starting transfers between devices  5.4 us (7%)
  between operations  2.22 us (3%)
    all_gather x5, blocking collectives, near_gather(): return lax.all_gather(q, 'dom', axis_index_groups=near_pairs)  29.1 us
    all_gather x4, blocking collectives, far_gather(): return lax.all_gather(q, ('section', 'dom'), axis_index_groups=groups)  22.2 us
    pallas_call x4, Pallas kernels, shards(): call(far_layer_body(step, step == 0, tail), (rows, rows, wide if tail els...  8.77 us
    pallas_call x3, Pallas kernels, shards(): call(near_layer_body(step), (rows, rows, both, wide), [VM] * 12, f'layer{...  6.8 us
    ppermute x3, starting transfers between devices, fetch(): lax.ppermute(own, 'section', [(i, i + k) for i in range(sections - k)])  5.4 us
    pallas_call x1, Pallas kernels, shards(): call(last_body(steps - 1), s(2, n, d), [VM] * 8 + [SM] * 2, f'layer{steps...  2.44 us
    pallas_call x1, Pallas kernels, shards(): call(prep_body, (rows, s(n, span), s(blk, span), rows, two, two, two, bot...  1.94 us
  transfers between devices with their start and end apart: 3, of which 0 were waited for; matrix products, arithmetic and copies ran while one was open for 0% of the time, Pallas kernels for 12%

profile of v5, /device:TPU:5, one launch (start us, length us, event | category | flops | bytes accessed | tf_op | source)
XLA Modules:
  0.0 80.6 jit_solution(5713567338082178312)
XLA Ops:
  0.0 1.1 %pack.1.nxt = bf16[1040,128]{1,0:T(8,128)(2,1)S(1)} custom-call(bf16[2,128,128]{2,1,0:T(8,128)(2,1)} %wm.1, bf16[2,256,128]{2,1,0:T(8,128)(2,1)} %wh.1, bf16[2,128]{1,0:T(2,128)(2,1)} %bh.1, bf16[2,128,128]{2,1,0:T(8,128)(2,1)} %wo.1, bf16[2,128]{1,0:T(2,128)(2,1)} %bo.1, bf16[2,128]{1,0:T(2,128)(2,1)} %gain.1), custom_call_target="tpu_custom_call" | custom-call | tf_op jit(solution)/shard_map/pack/pallas_call | solution.py:382
  1.2 0.7 collective-permute-start
  3.8 1.9 %prep.1 = (bf16[1024,256]{1,0:T(8,128)(2,1)S(1)}, bf16[1024,1280]{1,0:T(8,128)(2,1)S(1)}, bf16[128,1280]{1,0:T(8,128)(2,1)S(1)}, bf16[1024,256]{1,0:T(8,128)(2,1...) custom-call(s32[1]{0:T(128)S(6)} %copy.14.count, ...), custom_call_target="tpu_custom_call" | custom-call | tf_op jit(solution)/shard_map/prep/pallas_call | solution.py:399
  5.7 2.3 %all-gather = bf16[512,256]{1,0:T(8,128)(2,1)S(1)} all-gather(bf16[256,256]{1,0:T(8,128)(2,1)S(1)} %get-tuple-element.52), channel_id=2, replica_groups={{0,1},{2,3},{4,5},{6,7},{8,9},{10,11},{12,13},{14,15},{16,17},{18,19},{..., dimensions={0}, use_global_device_ids=true | all-gather | bytes 393216 | tf_op jit(solution)/shard_map/all_gather | solution.py:357
  8.0 1.3 %collective-permute-start.1 = (bf16[1040,128]{1,0:T(8,128)(2,1)S(1)}, bf16[1040,128]{1,0:T(8,128)(2,1)S(1)}, u32[]{:S(2)}, u32[]{:S(2)}) collective-permute-start(bf16[1040,128]{1,0:T(8,128)(2,1)S(1)} %pack.1.nxt), channel_id=1, source_target_pairs={{0,256},{128,384},{1,257},{129,385},{2,258},{130,386},{3,259},{131... | collective-permute-start | bytes 798728 | tf_op jit(solution)/shard_map/ppermute | solution.py:360
  9.3 3.4 %collective-permute-start.2 = (bf16[1040,128]{1,0:T(8,128)(2,1)S(1)}, bf16[1040,128]{1,0:T(8,128)(2,1)S(1)}, u32[]{:S(2)}, u32[]{:S(2)}) collective-permute-start(bf16[1040,128]{1,0:T(8,128)(2,1)S(1)} %pack.1.nxt), channel_id=1, source_target_pairs={{0,128},{128,256},{256,384},{1,129},{129,257},{257,385},{2,130},{1... | collective-permute-start | bytes 798728 | tf_op jit(solution)/shard_map/ppermute | solution.py:360
  12.8 0.0 collective-permute-done.pack.nxt
  12.8 0.6 first.1
  13.4 6.9 %all-gather.1 = bf16[768,256]{1,0:T(8,128)(2,1)S(1)} all-gather(bf16[384,256]{1,0:T(8,128)(2,1)S(1)} %get-tuple-element.59), channel_id=3, replica_groups={{1,2},{3,4},{5,6},{7,8},{9,10},{11,12},{13,14},{15,16},{17,18},{19,20},..., dimensions={0}, use_global_device_ids=true | all-gather | bytes 589824 | tf_op jit(solution)/shard_map/all_gather | solution.py:372
  20.3 2.3 %layer0.1 = (bf16[1024,256]{1,0:T(8,128)(2,1)S(1)}, bf16[1024,256]{1,0:T(8,128)(2,1)S(1)}, bf16[256,256]{1,0:T(8,128)(2,1)S(1)}, bf16[128,256]{1,0:T(8,128)(2,1)S(1)}, bf16[128,256]{1,0:T(8,128)(2,1)S(1)}) custom-call(bf16[1024,256]{1,0:T(8,128)(2,1)S(1)} %get-tuple-element.49.h, bf16[1024,256]{1,0:T(8,128)(2,1)S(1)} %get-tuple-element.56.m, ...), custom_call_target="tpu_custom_call" | custom-call | tf_op jit(solution)/shard_map/layer0/pallas_call | solution.py:435
  22.6 10.8 %all-gather.2 = bf16[512,256]{1,0:T(8,128)(2,1)S(1)} all-gather(bf16[256,256]{1,0:T(8,128)(2,1)S(1)} %get-tuple-element.65), channel_id=4, replica_groups={{0,1},{2,3},{4,5},{6,7},{8,9},{10,11},{12,13},{14,15},{16,17},{18,19},{..., dimensions={0}, use_global_device_ids=true | all-gather | bytes 393216 | tf_op jit(solution)/shard_map/all_gather | solution.py:357
  33.3 2.3 %layer1.1 = (bf16[1024,256]{1,0:T(8,128)(2,1)S(1)}, bf16[1024,256]{1,0:T(8,128)(2,1)S(1)}, bf16[256,256]{1,0:T(8,128)(2,1)S(1)}, bf16[128,256]{1,0:T(8,128)(2,1)S(1)}) custom-call(bf16[1024,256]{1,0:T(8,128)(2,1)S(1)} %get-tuple-element.62.h, bf16[1024,256]{1,0:T(8,128)(2,1)S(1)} %get-tuple-element.63.m, bf16[128,256]{1,0:T(8,128)(2,1)S(1)} %get-tuple-element.64.far_m, ...), custom_call_target="tpu_custom_call" | custom-call | tf_op jit(solution)/shard_map/layer1/pallas_call | solution.py:447
  35.6 5.1 %all-gather.3 = bf16[512,256]{1,0:T(8,128)(2,1)S(1)} all-gather(bf16[256,256]{1,0:T(8,128)(2,1)S(1)} %get-tuple-element.71), channel_id=5, replica_groups={{0,1},{2,3},{4,5},{6,7},{8,9},{10,11},{12,13},{14,15},{16,17},{18,19},{..., dimensions={0}, use_global_device_ids=true | all-gather | bytes 393216 | tf_op jit(solution)/shard_map/all_gather | solution.py:372
  40.7 2.3 %layer2.1 = (bf16[1024,256]{1,0:T(8,128)(2,1)S(1)}, bf16[1024,256]{1,0:T(8,128)(2,1)S(1)}, bf16[256,256]{1,0:T(8,128)(2,1)S(1)}, bf16[128,256]{1,0:T(8,128)(2,1)S(1)}) custom-call(bf16[1024,256]{1,0:T(8,128)(2,1)S(1)} %get-tuple-element.68.h, bf16[1024,256]{1,0:T(8,128)(2,1)S(1)} %get-tuple-element.69.m, bf16[128,256]{1,0:T(8,128)(2,1)S(1)} %get-tuple-element.70.near_m, ...), custom_call_target="tpu_custom_call" | custom-call | tf_op jit(solution)/shard_map/layer2/pallas_call | solution.py:435
  42.9 5.3 %all-gather.4 = bf16[512,256]{1,0:T(8,128)(2,1)S(1)} all-gather(bf16[256,256]{1,0:T(8,128)(2,1)S(1)} %get-tuple-element.76), channel_id=6, replica_groups={{0,1},{2,3},{4,5},{6,7},{8,9},{10,11},{12,13},{14,15},{16,17},{18,19},{..., dimensions={0}, use_global_device_ids=true | all-gather | bytes 393216 | tf_op jit(solution)/shard_map/all_gather | solution.py:357
  48.3 2.3 %layer3.1 = (bf16[1024,256]{1,0:T(8,128)(2,1)S(1)}, bf16[1024,256]{1,0:T(8,128)(2,1)S(1)}, bf16[256,256]{1,0:T(8,128)(2,1)S(1)}, bf16[128,256]{1,0:T(8,128)(2,1)S(1)}) custom-call(bf16[1024,256]{1,0:T(8,128)(2,1)S(1)} %get-tuple-element.73.h, bf16[1024,256]{1,0:T(8,128)(2,1)S(1)} %get-tuple-element.74.m, bf16[128,256]{1,0:T(8,128)(2,1)S(1)} %get-tuple-element.75.far_m, ...), custom_call_target="tpu_custom_call" | custom-call | tf_op jit(solution)/shard_map/layer3/pallas_call | solution.py:447
  50.5 5.1 %all-gather.5 = bf16[512,256]{1,0:T(8,128)(2,1)S(1)} all-gather(bf16[256,256]{1,0:T(8,128)(2,1)S(1)} %get-tuple-element.80), channel_id=7, replica_groups={{0,1},{2,3},{4,5},{6,7},{8,9},{10,11},{12,13},{14,15},{16,17},{18,19},{..., dimensions={0}, use_global_device_ids=true | all-gather | bytes 393216 | tf_op jit(solution)/shard_map/all_gather | solution.py:372
  55.6 2.2 %layer4.1 = (bf16[1024,256]{1,0:T(8,128)(2,1)S(1)}, bf16[1024,256]{1,0:T(8,128)(2,1)S(1)}, bf16[256,256]{1,0:T(8,128)(2,1)S(1)}, bf16[128,256]{1,0:T(8,128)(2,1)S(1)}) custom-call(bf16[1024,256]{1,0:T(8,128)(2,1)S(1)} %get-tuple-element.77.h, bf16[1024,256]{1,0:T(8,128)(2,1)S(1)} %get-tuple-element.78.m, bf16[128,256]{1,0:T(8,128)(2,1)S(1)} %get-tuple-element.79.near_m, ...), custom_call_target="tpu_custom_call" | custom-call | tf_op jit(solution)/shard_map/layer4/pallas_call | solution.py:435
  57.9 5.5 %all-gather.6 = bf16[512,256]{1,0:T(8,128)(2,1)S(1)} all-gather(bf16[256,256]{1,0:T(8,128)(2,1)S(1)} %get-tuple-element.84), channel_id=8, replica_groups={{0,1},{2,3},{4,5},{6,7},{8,9},{10,11},{12,13},{14,15},{16,17},{18,19},{..., dimensions={0}, use_global_device_ids=true | all-gather | bytes 393216 | tf_op jit(solution)/shard_map/all_gather | solution.py:357
  63.4 2.3 %layer5.1 = (bf16[1024,256]{1,0:T(8,128)(2,1)S(1)}, bf16[1024,256]{1,0:T(8,128)(2,1)S(1)}, bf16[256,256]{1,0:T(8,128)(2,1)S(1)}, bf16[128,256]{1,0:T(8,128)(2,1)S(1)}) custom-call(bf16[1024,256]{1,0:T(8,128)(2,1)S(1)} %get-tuple-element.81.h, bf16[1024,256]{1,0:T(8,128)(2,1)S(1)} %get-tuple-element.82.m, bf16[128,256]{1,0:T(8,128)(2,1)S(1)} %get-tuple-element.83.far_m, ...), custom_call_target="tpu_custom_call" | custom-call | tf_op jit(solution)/shard_map/layer5/pallas_call | solution.py:447
  65.6 5.1 %all-gather.7 = bf16[512,256]{1,0:T(8,128)(2,1)S(1)} all-gather(bf16[256,256]{1,0:T(8,128)(2,1)S(1)} %get-tuple-element.88), channel_id=9, replica_groups={{1,2},{3,4},{5,6},{7,8},{9,10},{11,12},{13,14},{15,16},{17,18},{19,20},..., dimensions={0}, use_global_device_ids=true | all-gather | bytes 393216 | tf_op jit(solution)/shard_map/all_gather | solution.py:372
  70.7 2.0 %layer6.1 = (bf16[1024,256]{1,0:T(8,128)(2,1)S(1)}, bf16[1024,256]{1,0:T(8,128)(2,1)S(1)}, bf16[128,256]{1,0:T(8,128)(2,1)S(1)}, bf16[128,256]{1,0:T(8,128)(2,1)S(1)}) custom-call(bf16[1024,256]{1,0:T(8,128)(2,1)S(1)} %get-tuple-element.85.h, bf16[1024,256]{1,0:T(8,128)(2,1)S(1)} %get-tuple-element.86.m, bf16[128,256]{1,0:T(8,128)(2,1)S(1)} %get-tuple-element.87.near_m, ...), custom_call_target="tpu_custom_call" | custom-call | tf_op jit(solution)/shard_map/layer6/pallas_call | solution.py:435
  72.7 5.2 %all-gather.8 = bf16[256,256]{1,0:T(8,128)(2,1)S(1)} all-gather(bf16[128,256]{1,0:T(8,128)(2,1)S(1)} %get-tuple-element.91), channel_id=10, replica_groups={{0,1},{2,3},{4,5},{6,7},{8,9},{10,11},{12,13},{14,15},{16,17},{18,19},{..., dimensions={0}, use_global_device_ids=true | all-gather | bytes 196608 | tf_op jit(solution)/shard_map/all_gather | solution.py:357
  78.0 2.4 %layer7.1 = bf16[2,1024,128]{2,1,0:T(8,128)(2,1)} custom-call(bf16[1024,256]{1,0:T(8,128)(2,1)S(1)} %get-tuple-element.89.h, bf16[1024,256]{1,0:T(8,128)(2,1)S(1)} %get-tuple-element.90.m, bf16[2,128,256]{2,1,0:T(8,128)(2,1)S(1)} %get-tuple-element.50.pick, bf16[2,128,256]{2,1,0:T(8,128)(2,1)S(1)} %bitcast.18, bf16[128,256]{1,0:T(8,128)(2,1)S(1)} %get-tuple-element.92.far_m, ...), custom_call_target="tpu_custom_call" | custom-call | tf_op jit(solution)/shard_map/layer7/pallas_call | solution.py:450
  (2 shorter events, 0.0 us)
Async XLA Ops:
  1.2 11.6 %collective-permute-start = (bf16[1040,128]{1,0:T(8,128)(2,1)S(1)}, bf16[1040,128]{1,0:T(8,128)(2,1)S(1)}, u32[]{:S(2)}, u32[]{:S(2)}) collective-permute-start(bf16[1040,128]{1,0:T(8,128)(2,1)S(1)} %pack.1.nxt), channel_id=1, source_target_pairs={{0,384},{1,385},{2,386},{3,387},{4,388},{5,389},{6,390},{7,391},{8... | collective-permute-start | bytes 798728 | tf_op jit(solution)/shard_map/ppermute | solution.py:360
  8.0 25.3 %collective-permute-start.1 = (bf16[1040,128]{1,0:T(8,128)(2,1)S(1)}, bf16[1040,128]{1,0:T(8,128)(2,1)S(1)}, u32[]{:S(2)}, u32[]{:S(2)}) collective-permute-start(bf16[1040,128]{1,0:T(8,128)(2,1)S(1)} %pack.1.nxt), channel_id=1, source_target_pairs={{0,256},{128,384},{1,257},{129,385},{2,258},{130,386},{3,259},{131... | collective-permute-start | bytes 798728 | tf_op jit(solution)/shard_map/ppermute | solution.py:360
  9.3 39.0 %collective-permute-start.2 = (bf16[1040,128]{1,0:T(8,128)(2,1)S(1)}, bf16[1040,128]{1,0:T(8,128)(2,1)S(1)}, u32[]{:S(2)}, u32[]{:S(2)}) collective-permute-start(bf16[1040,128]{1,0:T(8,128)(2,1)S(1)} %pack.1.nxt), channel_id=1, source_target_pairs={{0,128},{128,256},{256,384},{1,129},{129,257},{257,385},{2,130},{1... | collective-permute-start | bytes 798728 | tf_op jit(solution)/shard_map/ppermute | solution.py:360

commit v6 on v5

--- a/solution.py
+++ b/solution.py
@@ -348,7 +348,6 @@
     steps = layers * sections
     near_pairs = [[i, i + 1] for i in range(0, doms, 2)]
     far_pairs = [[i, i + 1] for i in range(1, doms - 1, 2)]
-    far_pairs = far_pairs + [[0, doms - 1]]
 
     def s(*shape, dtype=BF):
         return jax.ShapeDtypeStruct(shape, dtype)
@@ -363,12 +362,17 @@
         return [pltpu.SMEM((k,), jnp.int32) for k in sizes]
 
     def far_gather(q, step):
-        groups = []
+        groups, ends = [], []
         for section in range(sections):
+            at = section * doms
             begun = step == 0 or layers * (sections - 1 - section) <= step + 1
-            groups += [
-                [section * doms + i for i in pair] for pair in (far_pairs if begun else near_pairs)
-            ]
+            groups += [[at + i for i in pair] for pair in (far_pairs if begun else near_pairs)]
+            ends += [at] if begun else []
+        if len(ends) % 2:
+            groups.append([ends[0], ends[0] + doms - 1])
+            ends = ends[1:]
+        for a, b in zip(ends[::2], ends[1::2]):
+            groups += [[a, b], [a + doms - 1, b + doms - 1]]
         return lax.all_gather(q, ("section", "dom"), axis_index_groups=groups)
 
     wide = s(blk, 2 * d)

time: 80.9 us -> 77.8 us (0.962)
  the two profiles are of different devices: /device:TPU:5 before, /device:TPU:37 now
where the time goes in v6:
time: 77.8 us; the launch traced here: 77.5 us
  blocking collectives  48.3 us (62%)
  Pallas kernels  21.7 us (28%)
  starting transfers between devices  5.4 us (7%)
  between operations  2.22 us (3%)
    all_gather x5, blocking collectives, near_gather(): return lax.all_gather(q, 'dom', axis_index_groups=near_pairs)  26.1 us
    all_gather x4, blocking collectives, far_gather(): return lax.all_gather(q, ('section', 'dom'), axis_index_groups=groups)  22.2 us
    pallas_call x4, Pallas kernels, shards(): call(far_layer_body(step, step == 0, tail), (rows, rows, wide if tail els...  8.76 us
    pallas_call x3, Pallas kernels, shards(): call(near_layer_body(step), (rows, rows, both, wide), [VM] * 12, f'layer{...  6.8 us
    ppermute x3, starting transfers between devices, fetch(): lax.ppermute(own, 'section', [(i, i + k) for i in range(sections - k)])  5.4 us
    pallas_call x1, Pallas kernels, shards(): call(last_body(steps - 1), s(2, n, d), [VM] * 8 + [SM] * 2, f'layer{steps...  2.44 us
    pallas_call x1, Pallas kernels, shards(): call(prep_body, (rows, s(n, span), s(blk, span), rows, two, two, two, bot...  1.94 us
  transfers between devices with their start and end apart: 3, of which 0 were waited for; matrix products, arithmetic and copies ran while one was open for 0% of the time, Pallas kernels for 12%

profile of v6, /device:TPU:37, one launch (start us, length us, event | category | flops | bytes accessed | tf_op | source)
XLA Modules:
  0.0 77.5 jit_solution(10584835716079982241)
XLA Ops:
  0.0 1.1 %pack.1.nxt = bf16[1040,128]{1,0:T(8,128)(2,1)S(1)} custom-call(bf16[2,128,128]{2,1,0:T(8,128)(2,1)} %wm.1, bf16[2,256,128]{2,1,0:T(8,128)(2,1)} %wh.1, bf16[2,128]{1,0:T(2,128)(2,1)} %bh.1, bf16[2,128,128]{2,1,0:T(8,128)(2,1)} %wo.1, bf16[2,128]{1,0:T(2,128)(2,1)} %bo.1, bf16[2,128]{1,0:T(2,128)(2,1)} %gain.1), custom_call_target="tpu_custom_call" | custom-call | tf_op jit(solution)/shard_map/pack/pallas_call | solution.py:386
  1.2 0.7 collective-permute-start
  3.8 1.9 %prep.1 = (bf16[1024,256]{1,0:T(8,128)(2,1)S(1)}, bf16[1024,1280]{1,0:T(8,128)(2,1)S(1)}, bf16[128,1280]{1,0:T(8,128)(2,1)S(1)}, bf16[1024,256]{1,0:T(8,128)(2,1...) custom-call(s32[1]{0:T(128)S(6)} %copy.14.count, ...), custom_call_target="tpu_custom_call" | custom-call | tf_op jit(solution)/shard_map/prep/pallas_call | solution.py:403
  5.7 2.3 %all-gather = bf16[512,256]{1,0:T(8,128)(2,1)S(1)} all-gather(bf16[256,256]{1,0:T(8,128)(2,1)S(1)} %get-tuple-element.52), channel_id=2, replica_groups={{0,1},{2,3},{4,5},{6,7},{8,9},{10,11},{12,13},{14,15},{16,17},{18,19},{..., dimensions={0}, use_global_device_ids=true | all-gather | bytes 393216 | tf_op jit(solution)/shard_map/all_gather | solution.py:356
  8.0 1.3 %collective-permute-start.1 = (bf16[1040,128]{1,0:T(8,128)(2,1)S(1)}, bf16[1040,128]{1,0:T(8,128)(2,1)S(1)}, u32[]{:S(2)}, u32[]{:S(2)}) collective-permute-start(bf16[1040,128]{1,0:T(8,128)(2,1)S(1)} %pack.1.nxt), channel_id=1, source_target_pairs={{0,256},{128,384},{1,257},{129,385},{2,258},{130,386},{3,259},{131... | collective-permute-start | bytes 798728 | tf_op jit(solution)/shard_map/ppermute | solution.py:359
  9.3 3.4 %collective-permute-start.2 = (bf16[1040,128]{1,0:T(8,128)(2,1)S(1)}, bf16[1040,128]{1,0:T(8,128)(2,1)S(1)}, u32[]{:S(2)}, u32[]{:S(2)}) collective-permute-start(bf16[1040,128]{1,0:T(8,128)(2,1)S(1)} %pack.1.nxt), channel_id=1, source_target_pairs={{0,128},{128,256},{256,384},{1,129},{129,257},{257,385},{2,130},{1... | collective-permute-start | bytes 798728 | tf_op jit(solution)/shard_map/ppermute | solution.py:359
  12.8 0.6 first.1
  13.4 6.9 %all-gather.1 = bf16[768,256]{1,0:T(8,128)(2,1)S(1)} all-gather(bf16[384,256]{1,0:T(8,128)(2,1)S(1)} %get-tuple-element.59), channel_id=3, replica_groups={{1,2},{3,4},{5,6},{7,8},{9,10},{11,12},{13,14},{15,16},{17,18},{19,20},..., dimensions={0}, use_global_device_ids=true | all-gather | bytes 589824 | tf_op jit(solution)/shard_map/all_gather | solution.py:376
  20.3 2.3 %layer0.1 = (bf16[1024,256]{1,0:T(8,128)(2,1)S(1)}, bf16[1024,256]{1,0:T(8,128)(2,1)S(1)}, bf16[256,256]{1,0:T(8,128)(2,1)S(1)}, bf16[128,256]{1,0:T(8,128)(2,1)S(1)}, bf16[128,256]{1,0:T(8,128)(2,1)S(1)}) custom-call(bf16[1024,256]{1,0:T(8,128)(2,1)S(1)} %get-tuple-element.49.h, bf16[1024,256]{1,0:T(8,128)(2,1)S(1)} %get-tuple-element.56.m, ...), custom_call_target="tpu_custom_call" | custom-call | tf_op jit(solution)/shard_map/layer0/pallas_call | solution.py:439
  22.6 7.8 %all-gather.2 = bf16[512,256]{1,0:T(8,128)(2,1)S(1)} all-gather(bf16[256,256]{1,0:T(8,128)(2,1)S(1)} %get-tuple-element.65), channel_id=4, replica_groups={{0,1},{2,3},{4,5},{6,7},{8,9},{10,11},{12,13},{14,15},{16,17},{18,19},{..., dimensions={0}, use_global_device_ids=true | all-gather | bytes 393216 | tf_op jit(solution)/shard_map/all_gather | solution.py:356
  30.3 2.3 %layer1.1 = (bf16[1024,256]{1,0:T(8,128)(2,1)S(1)}, bf16[1024,256]{1,0:T(8,128)(2,1)S(1)}, bf16[256,256]{1,0:T(8,128)(2,1)S(1)}, bf16[128,256]{1,0:T(8,128)(2,1)S(1)}) custom-call(bf16[1024,256]{1,0:T(8,128)(2,1)S(1)} %get-tuple-element.62.h, bf16[1024,256]{1,0:T(8,128)(2,1)S(1)} %get-tuple-element.63.m, bf16[128,256]{1,0:T(8,128)(2,1)S(1)} %get-tuple-element.64.far_m, ...), custom_call_target="tpu_custom_call" | custom-call | tf_op jit(solution)/shard_map/layer1/pallas_call | solution.py:451
  32.6 5.1 %all-gather.3 = bf16[512,256]{1,0:T(8,128)(2,1)S(1)} all-gather(bf16[256,256]{1,0:T(8,128)(2,1)S(1)} %get-tuple-element.71), channel_id=5, replica_groups={{0,1},{2,3},{4,5},{6,7},{8,9},{10,11},{12,13},{14,15},{16,17},{18,19},{..., dimensions={0}, use_global_device_ids=true | all-gather | bytes 393216 | tf_op jit(solution)/shard_map/all_gather | solution.py:376
  37.7 2.3 %layer2.1 = (bf16[1024,256]{1,0:T(8,128)(2,1)S(1)}, bf16[1024,256]{1,0:T(8,128)(2,1)S(1)}, bf16[256,256]{1,0:T(8,128)(2,1)S(1)}, bf16[128,256]{1,0:T(8,128)(2,1)S(1)}) custom-call(bf16[1024,256]{1,0:T(8,128)(2,1)S(1)} %get-tuple-element.68.h, bf16[1024,256]{1,0:T(8,128)(2,1)S(1)} %get-tuple-element.69.m, bf16[128,256]{1,0:T(8,128)(2,1)S(1)} %get-tuple-element.70.near_m, ...), custom_call_target="tpu_custom_call" | custom-call | tf_op jit(solution)/shard_map/layer2/pallas_call | solution.py:439
  39.9 5.3 %all-gather.4 = bf16[512,256]{1,0:T(8,128)(2,1)S(1)} all-gather(bf16[256,256]{1,0:T(8,128)(2,1)S(1)} %get-tuple-element.76), channel_id=6, replica_groups={{0,1},{2,3},{4,5},{6,7},{8,9},{10,11},{12,13},{14,15},{16,17},{18,19},{..., dimensions={0}, use_global_device_ids=true | all-gather | bytes 393216 | tf_op jit(solution)/shard_map/all_gather | solution.py:356
  45.3 0.0 collective-permute-done.2.nxt.pack
  45.3 2.3 %layer3.1 = (bf16[1024,256]{1,0:T(8,128)(2,1)S(1)}, bf16[1024,256]{1,0:T(8,128)(2,1)S(1)}, bf16[256,256]{1,0:T(8,128)(2,1)S(1)}, bf16[128,256]{1,0:T(8,128)(2,1)S(1)}) custom-call(bf16[1024,256]{1,0:T(8,128)(2,1)S(1)} %get-tuple-element.73.h, bf16[1024,256]{1,0:T(8,128)(2,1)S(1)} %get-tuple-element.74.m, bf16[128,256]{1,0:T(8,128)(2,1)S(1)} %get-tuple-element.75.far_m, ...), custom_call_target="tpu_custom_call" | custom-call | tf_op jit(solution)/shard_map/layer3/pallas_call | solution.py:451
  47.5 5.1 %all-gather.5 = bf16[512,256]{1,0:T(8,128)(2,1)S(1)} all-gather(bf16[256,256]{1,0:T(8,128)(2,1)S(1)} %get-tuple-element.80), channel_id=7, replica_groups={{0,1},{2,3},{4,5},{6,7},{8,9},{10,11},{12,13},{14,15},{16,17},{18,19},{..., dimensions={0}, use_global_device_ids=true | all-gather | bytes 393216 | tf_op jit(solution)/shard_map/all_gather | solution.py:376
  52.6 2.2 %layer4.1 = (bf16[1024,256]{1,0:T(8,128)(2,1)S(1)}, bf16[1024,256]{1,0:T(8,128)(2,1)S(1)}, bf16[256,256]{1,0:T(8,128)(2,1)S(1)}, bf16[128,256]{1,0:T(8,128)(2,1)S(1)}) custom-call(bf16[1024,256]{1,0:T(8,128)(2,1)S(1)} %get-tuple-element.77.h, bf16[1024,256]{1,0:T(8,128)(2,1)S(1)} %get-tuple-element.78.m, bf16[128,256]{1,0:T(8,128)(2,1)S(1)} %get-tuple-element.79.near_m, ...), custom_call_target="tpu_custom_call" | custom-call | tf_op jit(solution)/shard_map/layer4/pallas_call | solution.py:439
  54.8 5.5 %all-gather.6 = bf16[512,256]{1,0:T(8,128)(2,1)S(1)} all-gather(bf16[256,256]{1,0:T(8,128)(2,1)S(1)} %get-tuple-element.84), channel_id=8, replica_groups={{0,1},{2,3},{4,5},{6,7},{8,9},{10,11},{12,13},{14,15},{16,17},{18,19},{..., dimensions={0}, use_global_device_ids=true | all-gather | bytes 393216 | tf_op jit(solution)/shard_map/all_gather | solution.py:356
  60.3 2.3 %layer5.1 = (bf16[1024,256]{1,0:T(8,128)(2,1)S(1)}, bf16[1024,256]{1,0:T(8,128)(2,1)S(1)}, bf16[256,256]{1,0:T(8,128)(2,1)S(1)}, bf16[128,256]{1,0:T(8,128)(2,1)S(1)}) custom-call(bf16[1024,256]{1,0:T(8,128)(2,1)S(1)} %get-tuple-element.81.h, bf16[1024,256]{1,0:T(8,128)(2,1)S(1)} %get-tuple-element.82.m, bf16[128,256]{1,0:T(8,128)(2,1)S(1)} %get-tuple-element.83.far_m, ...), custom_call_target="tpu_custom_call" | custom-call | tf_op jit(solution)/shard_map/layer5/pallas_call | solution.py:451
  62.6 5.1 %all-gather.7 = bf16[512,256]{1,0:T(8,128)(2,1)S(1)} all-gather(bf16[256,256]{1,0:T(8,128)(2,1)S(1)} %get-tuple-element.88), channel_id=9, replica_groups={{1,2},{3,4},{5,6},{7,8},{9,10},{11,12},{13,14},{15,16},{17,18},{19,20},..., dimensions={0}, use_global_device_ids=true | all-gather | bytes 393216 | tf_op jit(solution)/shard_map/all_gather | solution.py:376
  67.7 2.0 %layer6.1 = (bf16[1024,256]{1,0:T(8,128)(2,1)S(1)}, bf16[1024,256]{1,0:T(8,128)(2,1)S(1)}, bf16[128,256]{1,0:T(8,128)(2,1)S(1)}, bf16[128,256]{1,0:T(8,128)(2,1)S(1)}) custom-call(bf16[1024,256]{1,0:T(8,128)(2,1)S(1)} %get-tuple-element.85.h, bf16[1024,256]{1,0:T(8,128)(2,1)S(1)} %get-tuple-element.86.m, bf16[128,256]{1,0:T(8,128)(2,1)S(1)} %get-tuple-element.87.near_m, ...), custom_call_target="tpu_custom_call" | custom-call | tf_op jit(solution)/shard_map/layer6/pallas_call | solution.py:439
  69.7 5.2 %all-gather.8 = bf16[256,256]{1,0:T(8,128)(2,1)S(1)} all-gather(bf16[128,256]{1,0:T(8,128)(2,1)S(1)} %get-tuple-element.91), channel_id=10, replica_groups={{0,1},{2,3},{4,5},{6,7},{8,9},{10,11},{12,13},{14,15},{16,17},{18,19},{..., dimensions={0}, use_global_device_ids=true | all-gather | bytes 196608 | tf_op jit(solution)/shard_map/all_gather | solution.py:356
  74.9 2.4 %layer7.1 = bf16[2,1024,128]{2,1,0:T(8,128)(2,1)} custom-call(bf16[1024,256]{1,0:T(8,128)(2,1)S(1)} %get-tuple-element.89.h, bf16[1024,256]{1,0:T(8,128)(2,1)S(1)} %get-tuple-element.90.m, bf16[2,128,256]{2,1,0:T(8,128)(2,1)S(1)} %get-tuple-element.50.pick, bf16[2,128,256]{2,1,0:T(8,128)(2,1)S(1)} %bitcast.18, bf16[128,256]{1,0:T(8,128)(2,1)S(1)} %get-tuple-element.92.far_m, ...), custom_call_target="tpu_custom_call" | custom-call | tf_op jit(solution)/shard_map/layer7/pallas_call | solution.py:454
  (2 shorter events, 0.0 us)
Async XLA Ops:
  1.2 11.6 %collective-permute-start = (bf16[1040,128]{1,0:T(8,128)(2,1)S(1)}, bf16[1040,128]{1,0:T(8,128)(2,1)S(1)}, u32[]{:S(2)}, u32[]{:S(2)}) collective-permute-start(bf16[1040,128]{1,0:T(8,128)(2,1)S(1)} %pack.1.nxt), channel_id=1, source_target_pairs={{0,384},{1,385},{2,386},{3,387},{4,388},{5,389},{6,390},{7,391},{8... | collective-permute-start | bytes 798728 | tf_op jit(solution)/shard_map/ppermute | solution.py:359
  8.0 22.3 %collective-permute-start.1 = (bf16[1040,128]{1,0:T(8,128)(2,1)S(1)}, bf16[1040,128]{1,0:T(8,128)(2,1)S(1)}, u32[]{:S(2)}, u32[]{:S(2)}) collective-permute-start(bf16[1040,128]{1,0:T(8,128)(2,1)S(1)} %pack.1.nxt), channel_id=1, source_target_pairs={{0,256},{128,384},{1,257},{129,385},{2,258},{130,386},{3,259},{131... | collective-permute-start | bytes 798728 | tf_op jit(solution)/shard_map/ppermute | solution.py:359
  9.3 35.9 %collective-permute-start.2 = (bf16[1040,128]{1,0:T(8,128)(2,1)S(1)}, bf16[1040,128]{1,0:T(8,128)(2,1)S(1)}, u32[]{:S(2)}, u32[]{:S(2)}) collective-permute-start(bf16[1040,128]{1,0:T(8,128)(2,1)S(1)} %pack.1.nxt), channel_id=1, source_target_pairs={{0,128},{128,256},{256,384},{1,129},{129,257},{257,385},{2,130},{1... | collective-permute-start | bytes 798728 | tf_op jit(solution)/shard_map/ppermute | solution.py:359

commit v7 on v6

--- a/solution.py
+++ b/solution.py
@@ -81,7 +81,7 @@
     return first(second(block)) if back else second(first(block))
 
 
-def pack_body(wm, wh, bh, wo, bo, gain, out, am, ah, ao, vb, vo, vg, sem):
+def pack_weights(wm, wh, bh, wo, bo, gain, out, am, ah, ao, vb, vo, vg, sem):
     d = wm.shape[2]
     for copy in fetch_all([(wm, am), (wh, ah), (wo, ao), (bh, vb), (bo, vo), (gain, vg)], sem):
         copy.wait()
@@ -98,6 +98,28 @@
     pad = jnp.zeros((8, d), F32)
     vectors = [vb[...].astype(F32) * 0.5, high, b - high, vg[...].astype(F32), pad]
     out[8 * d :] = jnp.concatenate(vectors, axis=0).astype(BF)
+
+
+def sends_no_weights():
+    return lax.axis_index("section") == lax.axis_size("section") - 1
+
+
+def pack_body(*refs):
+    @pl.when(jnp.logical_not(sends_no_weights()))
+    def _():
+        pack_weights(*refs)
+
+
+def pack_late_body(packed, *refs):
+    out = refs[6]
+
+    @pl.when(sends_no_weights())
+    def _():
+        pack_weights(*refs)
+
+    @pl.when(jnp.logical_not(sends_no_weights()))
+    def _():
+        out[...] = packed[...]
 
 
 def prep_body(
@@ -367,10 +389,10 @@
             at = section * doms
             begun = step == 0 or layers * (sections - 1 - section) <= step + 1
             groups += [[at + i for i in pair] for pair in (far_pairs if begun else near_pairs)]
-            ends += [at] if begun else []
-        if len(ends) % 2:
-            groups.append([ends[0], ends[0] + doms - 1])
-            ends = ends[1:]
+            if begun and (step == 0 or section >= sections - 2):
+                ends.append(at)
+            elif begun:
+                groups.append([at, at + doms - 1])
         for a, b in zip(ends[::2], ends[1::2]):
             groups += [[a, b], [a + doms - 1, b + doms - 1]]
         return lax.all_gather(q, ("section", "dom"), axis_index_groups=groups)
@@ -383,21 +405,17 @@
     count_k = adjacency.shape[0]
     vec = pltpu.VMEM((layers, d), BF)
     weights = in_hbm(w_message, w_hidden, b_hidden, w_out, b_out, gain)
-    own = call(
-        pack_body,
-        s(layers * 4 * d + 16, d),
-        [HB] * 6,
-        "pack",
-        [
-            pltpu.VMEM((layers, d, d), BF),
-            pltpu.VMEM((layers, 2 * d, d), BF),
-            pltpu.VMEM((layers, d, d), BF),
-            vec,
-            vec,
-            vec,
-            pltpu.SemaphoreType.DMA((6,)),
-        ],
-    )(*weights)
+    packed = s(layers * 4 * d + 16, d)
+    pack_scratch = [
+        pltpu.VMEM((layers, d, d), BF),
+        pltpu.VMEM((layers, 2 * d, d), BF),
+        pltpu.VMEM((layers, d, d), BF),
+        vec,
+        vec,
+        vec,
+        pltpu.SemaphoreType.DMA((6,)),
+    ]
+    own = call(pack_body, packed, [HB] * 6, "pack", pack_scratch)(*weights)
     packs = [fetch(own, sections - 1)]
     graph = [counts, send_up, send_down, *in_hbm(row_blocks, col_blocks, features, adjacency)]
     h, dense, df, mask, pick, fpick, fsel, q, view = call(
@@ -416,7 +434,10 @@
     )(*graph)
     near = near_gather(q)
     later, near = lax.optimization_barrier((own, near))
-    packs += [fetch(later, k) for k in range(sections - 2, 0, -1)] + [own]
+    packs += [fetch(later, k) for k in range(sections - 2, 0, -1)]
+    own = call(pack_late_body, packed, [VM] + [HB] * 6, "pack_late", pack_scratch)(later, *weights)
+    own, near = lax.optimization_barrier((own, near))
+    packs.append(own)
     m, near_m, nseen, pay = call(
         first_body, (rows, wide, wide, s(3 * blk, 2 * d)), [VM] * 7, "first"
     )(h, pick, fsel, near, df, view, packs[0])

time: 77.8 us -> 79.4 us (1.021)
  the two profiles are of different devices: /device:TPU:37 before, /device:TPU:3 now
where the time goes in v7:
time: 79.4 us; the launch traced here: 79.1 us
  blocking collectives  49.3 us (62%)
  Pallas kernels  21.8 us (27%)
  starting transfers between devices  5.87 us (7%)
  between operations  2.22 us (3%)
    all_gather x5, blocking collectives, near_gather(): return lax.all_gather(q, 'dom', axis_index_groups=near_pairs)  30.5 us
    all_gather x4, blocking collectives, far_gather(): return lax.all_gather(q, ('section', 'dom'), axis_index_groups=groups)  18.8 us
    pallas_call x4, Pallas kernels, shards(): call(far_layer_body(step, step == 0, tail), (rows, rows, wide if tail els...  8.76 us
    pallas_call x3, Pallas kernels, shards(): call(near_layer_body(step), (rows, rows, both, wide), [VM] * 12, f'layer{...  6.8 us
    ppermute x3, starting transfers between devices, fetch(): lax.ppermute(own, 'section', [(i, i + k) for i in range(sections - k)])  5.87 us
    pallas_call x1, Pallas kernels, shards(): call(last_body(steps - 1), s(2, n, d), [VM] * 8 + [SM] * 2, f'layer{steps...  2.44 us
    pallas_call x1, Pallas kernels, shards(): call(prep_body, (rows, s(n, span), s(blk, span), rows, two, two, two, bot...  1.94 us
  transfers between devices with their start and end apart: 3, of which 0 were waited for; matrix products, arithmetic and copies ran while one was open for 0% of the time, Pallas kernels for 12%

profile of v7, /device:TPU:3, one launch (start us, length us, event | category | flops | bytes accessed | tf_op | source)
XLA Modules:
  0.0 79.1 jit_solution(2485417856563873270)
XLA Ops:
  0.0 1.1 %pack.1.packed = bf16[1040,128]{1,0:T(8,128)(2,1)S(1)} custom-call(bf16[2,128,128]{2,1,0:T(8,128)(2,1)} %refs_0_.3, bf16[2,256,128]{2,1,0:T(8,128)(2,1)} %refs_1_.3, bf16[2,128]{1,0:T(2,128)(2,1)} %refs_2_.3, bf16[2,128,128]{2,1,0:T(8,128)(2,1)} %refs_3_.3, bf16[2,128]{1,0:T(2,128)(2,1)} %refs_4_.3, bf16[2,128]{1,0:T(2,128)(2,1)} %refs_5_.3), custom_call_target="tpu_custom_call" | custom-call | tf_op jit(solution)/shard_map/pack/pallas_call | solution.py:418
  1.2 0.7 collective-permute-start
  3.8 1.9 %prep.1 = (bf16[1024,256]{1,0:T(8,128)(2,1)S(1)}, bf16[1024,1280]{1,0:T(8,128)(2,1)S(1)}, bf16[128,1280]{1,0:T(8,128)(2,1)S(1)}, bf16[1024,256]{1,0:T(8,128)(2,1...) custom-call(s32[1]{0:T(128)S(6)} %copy.14.count, ...), custom_call_target="tpu_custom_call" | custom-call | tf_op jit(solution)/shard_map/prep/pallas_call | solution.py:421
  5.7 2.3 %all-gather = bf16[512,256]{1,0:T(8,128)(2,1)S(1)} all-gather(bf16[256,256]{1,0:T(8,128)(2,1)S(1)} %get-tuple-element.54), channel_id=2, replica_groups={{0,1},{2,3},{4,5},{6,7},{8,9},{10,11},{12,13},{14,15},{16,17},{18,19},{..., dimensions={0}, use_global_device_ids=true | all-gather | bytes 393216 | tf_op jit(solution)/shard_map/all_gather | solution.py:378
  8.0 3.3 %collective-permute-start.1 = (bf16[1040,128]{1,0:T(8,128)(2,1)S(1)}, bf16[1040,128]{1,0:T(8,128)(2,1)S(1)}, u32[]{:S(2)}, u32[]{:S(2)}) collective-permute-start(bf16[1040,128]{1,0:T(8,128)(2,1)S(1)} %pack.1.packed), channel_id=1, source_target_pairs={{0,256},{128,384},{1,257},{129,385},{2,258},{130,386},{3,259},{131... | collective-permute-start | bytes 798728 | tf_op jit(solution)/shard_map/ppermute | solution.py:381
  11.3 1.9 %collective-permute-start.2 = (bf16[1040,128]{1,0:T(8,128)(2,1)S(1)}, bf16[1040,128]{1,0:T(8,128)(2,1)S(1)}, u32[]{:S(2)}, u32[]{:S(2)}) collective-permute-start(bf16[1040,128]{1,0:T(8,128)(2,1)S(1)} %pack.1.packed), channel_id=1, source_target_pairs={{0,128},{128,256},{256,384},{1,129},{129,257},{257,385},{2,130},{1... | collective-permute-start | bytes 798728 | tf_op jit(solution)/shard_map/ppermute | solution.py:381
  13.2 0.1 pack_late.1.nxt.pack
  13.4 0.6 first.1
  13.9 6.6 %all-gather.1 = bf16[768,256]{1,0:T(8,128)(2,1)S(1)} all-gather(bf16[384,256]{1,0:T(8,128)(2,1)S(1)} %get-tuple-element.63), channel_id=3, replica_groups={{1,2},{3,4},{5,6},{7,8},{9,10},{11,12},{13,14},{15,16},{17,18},{19,20},..., dimensions={0}, use_global_device_ids=true | all-gather | bytes 589824 | tf_op jit(solution)/shard_map/all_gather | solution.py:398
  20.6 2.2 %layer0.1 = (bf16[1024,256]{1,0:T(8,128)(2,1)S(1)}, bf16[1024,256]{1,0:T(8,128)(2,1)S(1)}, bf16[256,256]{1,0:T(8,128)(2,1)S(1)}, bf16[128,256]{1,0:T(8,128)(2,1)S(1)}, bf16[128,256]{1,0:T(8,128)(2,1)S(1)}) custom-call(bf16[1024,256]{1,0:T(8,128)(2,1)S(1)} %get-tuple-element.51.h, bf16[1024,256]{1,0:T(8,128)(2,1)S(1)} %get-tuple-element.60.m, ...), custom_call_target="tpu_custom_call" | custom-call | tf_op jit(solution)/shard_map/layer0/pallas_call | solution.py:460
  22.8 11.8 %all-gather.2 = bf16[512,256]{1,0:T(8,128)(2,1)S(1)} all-gather(bf16[256,256]{1,0:T(8,128)(2,1)S(1)} %get-tuple-element.69), channel_id=4, replica_groups={{0,1},{2,3},{4,5},{6,7},{8,9},{10,11},{12,13},{14,15},{16,17},{18,19},{..., dimensions={0}, use_global_device_ids=true | all-gather | bytes 393216 | tf_op jit(solution)/shard_map/all_gather | solution.py:378
  34.6 2.3 %layer1.1 = (bf16[1024,256]{1,0:T(8,128)(2,1)S(1)}, bf16[1024,256]{1,0:T(8,128)(2,1)S(1)}, bf16[256,256]{1,0:T(8,128)(2,1)S(1)}, bf16[128,256]{1,0:T(8,128)(2,1)S(1)}) custom-call(bf16[1024,256]{1,0:T(8,128)(2,1)S(1)} %get-tuple-element.66.h, bf16[1024,256]{1,0:T(8,128)(2,1)S(1)} %get-tuple-element.67.m, bf16[128,256]{1,0:T(8,128)(2,1)S(1)} %get-tuple-element.68.far_m, ...), custom_call_target="tpu_custom_call" | custom-call | tf_op jit(solution)/shard_map/layer1/pallas_call | solution.py:472
  36.9 2.0 %all-gather.3 = bf16[512,256]{1,0:T(8,128)(2,1)S(1)} all-gather(bf16[256,256]{1,0:T(8,128)(2,1)S(1)} %get-tuple-element.74), channel_id=5, replica_groups={{0,1},{2,3},{4,5},{6,7},{8,9},{10,11},{12,13},{14,15},{16,17},{18,19},{..., dimensions={0}, use_global_device_ids=true | all-gather | bytes 393216 | tf_op jit(solution)/shard_map/all_gather | solution.py:398
  38.9 2.3 %layer2.1 = (bf16[1024,256]{1,0:T(8,128)(2,1)S(1)}, bf16[1024,256]{1,0:T(8,128)(2,1)S(1)}, bf16[256,256]{1,0:T(8,128)(2,1)S(1)}, bf16[128,256]{1,0:T(8,128)(2,1)S(1)}) custom-call(bf16[1024,256]{1,0:T(8,128)(2,1)S(1)} %get-tuple-element.71.h, bf16[1024,256]{1,0:T(8,128)(2,1)S(1)} %get-tuple-element.72.m, bf16[128,256]{1,0:T(8,128)(2,1)S(1)} %get-tuple-element.73.near_m, ...), custom_call_target="tpu_custom_call" | custom-call | tf_op jit(solution)/shard_map/layer2/pallas_call | solution.py:460
  41.2 2.0 %all-gather.4 = bf16[512,256]{1,0:T(8,128)(2,1)S(1)} all-gather(bf16[256,256]{1,0:T(8,128)(2,1)S(1)} %get-tuple-element.79), channel_id=6, replica_groups={{0,1},{2,3},{4,5},{6,7},{8,9},{10,11},{12,13},{14,15},{16,17},{18,19},{..., dimensions={0}, use_global_device_ids=true | all-gather | bytes 393216 | tf_op jit(solution)/shard_map/all_gather | solution.py:378
  43.2 2.3 %layer3.1 = (bf16[1024,256]{1,0:T(8,128)(2,1)S(1)}, bf16[1024,256]{1,0:T(8,128)(2,1)S(1)}, bf16[256,256]{1,0:T(8,128)(2,1)S(1)}, bf16[128,256]{1,0:T(8,128)(2,1)S(1)}) custom-call(bf16[1024,256]{1,0:T(8,128)(2,1)S(1)} %get-tuple-element.76.h, bf16[1024,256]{1,0:T(8,128)(2,1)S(1)} %get-tuple-element.77.m, bf16[128,256]{1,0:T(8,128)(2,1)S(1)} %get-tuple-element.78.far_m, ...), custom_call_target="tpu_custom_call" | custom-call | tf_op jit(solution)/shard_map/layer3/pallas_call | solution.py:472
  45.4 5.1 %all-gather.5 = bf16[512,256]{1,0:T(8,128)(2,1)S(1)} all-gather(bf16[256,256]{1,0:T(8,128)(2,1)S(1)} %get-tuple-element.83), channel_id=7, replica_groups={{0,1},{2,3},{4,5},{6,7},{8,9},{10,11},{12,13},{14,15},{16,17},{18,19},{..., dimensions={0}, use_global_device_ids=true | all-gather | bytes 393216 | tf_op jit(solution)/shard_map/all_gather | solution.py:398
  50.5 2.2 %layer4.1 = (bf16[1024,256]{1,0:T(8,128)(2,1)S(1)}, bf16[1024,256]{1,0:T(8,128)(2,1)S(1)}, bf16[256,256]{1,0:T(8,128)(2,1)S(1)}, bf16[128,256]{1,0:T(8,128)(2,1)S(1)}) custom-call(bf16[1024,256]{1,0:T(8,128)(2,1)S(1)} %get-tuple-element.80.h, bf16[1024,256]{1,0:T(8,128)(2,1)S(1)} %get-tuple-element.81.m, bf16[128,256]{1,0:T(8,128)(2,1)S(1)} %get-tuple-element.82.near_m, ...), custom_call_target="tpu_custom_call" | custom-call | tf_op jit(solution)/shard_map/layer4/pallas_call | solution.py:460
  52.8 9.2 %all-gather.6 = bf16[512,256]{1,0:T(8,128)(2,1)S(1)} all-gather(bf16[256,256]{1,0:T(8,128)(2,1)S(1)} %get-tuple-element.87), channel_id=8, replica_groups={{0,1},{2,3},{4,5},{6,7},{8,9},{10,11},{12,13},{14,15},{16,17},{18,19},{..., dimensions={0}, use_global_device_ids=true | all-gather | bytes 393216 | tf_op jit(solution)/shard_map/all_gather | solution.py:378
  61.9 2.3 %layer5.1 = (bf16[1024,256]{1,0:T(8,128)(2,1)S(1)}, bf16[1024,256]{1,0:T(8,128)(2,1)S(1)}, bf16[256,256]{1,0:T(8,128)(2,1)S(1)}, bf16[128,256]{1,0:T(8,128)(2,1)S(1)}) custom-call(bf16[1024,256]{1,0:T(8,128)(2,1)S(1)} %get-tuple-element.84.h, bf16[1024,256]{1,0:T(8,128)(2,1)S(1)} %get-tuple-element.85.m, bf16[128,256]{1,0:T(8,128)(2,1)S(1)} %get-tuple-element.86.far_m, ...), custom_call_target="tpu_custom_call" | custom-call | tf_op jit(solution)/shard_map/layer5/pallas_call | solution.py:472
  64.2 5.1 %all-gather.7 = bf16[512,256]{1,0:T(8,128)(2,1)S(1)} all-gather(bf16[256,256]{1,0:T(8,128)(2,1)S(1)} %get-tuple-element.92), channel_id=9, replica_groups={{1,2},{3,4},{5,6},{7,8},{9,10},{11,12},{13,14},{15,16},{17,18},{19,20},..., dimensions={0}, use_global_device_ids=true | all-gather | bytes 393216 | tf_op jit(solution)/shard_map/all_gather | solution.py:398
  69.3 2.0 %layer6.1 = (bf16[1024,256]{1,0:T(8,128)(2,1)S(1)}, bf16[1024,256]{1,0:T(8,128)(2,1)S(1)}, bf16[128,256]{1,0:T(8,128)(2,1)S(1)}, bf16[128,256]{1,0:T(8,128)(2,1)S(1)}) custom-call(bf16[1024,256]{1,0:T(8,128)(2,1)S(1)} %get-tuple-element.89.h, bf16[1024,256]{1,0:T(8,128)(2,1)S(1)} %get-tuple-element.90.m, bf16[128,256]{1,0:T(8,128)(2,1)S(1)} %get-tuple-element.91.near_m, ...), custom_call_target="tpu_custom_call" | custom-call | tf_op jit(solution)/shard_map/layer6/pallas_call | solution.py:460
  71.3 5.2 %all-gather.8 = bf16[256,256]{1,0:T(8,128)(2,1)S(1)} all-gather(bf16[128,256]{1,0:T(8,128)(2,1)S(1)} %get-tuple-element.95), channel_id=10, replica_groups={{0,1},{2,3},{4,5},{6,7},{8,9},{10,11},{12,13},{14,15},{16,17},{18,19},{..., dimensions={0}, use_global_device_ids=true | all-gather | bytes 196608 | tf_op jit(solution)/shard_map/all_gather | solution.py:378
  76.5 2.4 %layer7.1 = bf16[2,1024,128]{2,1,0:T(8,128)(2,1)} custom-call(bf16[1024,256]{1,0:T(8,128)(2,1)S(1)} %get-tuple-element.93.h, bf16[1024,256]{1,0:T(8,128)(2,1)S(1)} %get-tuple-element.94.m, bf16[2,128,256]{2,1,0:T(8,128)(2,1)S(1)} %get-tuple-element.52.pick, bf16[2,128,256]{2,1,0:T(8,128)(2,1)S(1)} %bitcast.18, bf16[128,256]{1,0:T(8,128)(2,1)S(1)} %get-tuple-element.96.far_m, ...), custom_call_target="tpu_custom_call" | custom-call | tf_op jit(solution)/shard_map/layer7/pallas_call | solution.py:475
  (3 shorter events, 0.0 us)
Async XLA Ops:
  1.2 12.2 %collective-permute-start = (bf16[1040,128]{1,0:T(8,128)(2,1)S(1)}, bf16[1040,128]{1,0:T(8,128)(2,1)S(1)}, u32[]{:S(2)}, u32[]{:S(2)}) collective-permute-start(bf16[1040,128]{1,0:T(8,128)(2,1)S(1)} %pack.1.packed), channel_id=1, source_target_pairs={{0,384},{1,385},{2,386},{3,387},{4,388},{5,389},{6,390},{7,391},{8... | collective-permute-start | bytes 798728 | tf_op jit(solution)/shard_map/ppermute | solution.py:381
  8.0 26.6 %collective-permute-start.1 = (bf16[1040,128]{1,0:T(8,128)(2,1)S(1)}, bf16[1040,128]{1,0:T(8,128)(2,1)S(1)}, u32[]{:S(2)}, u32[]{:S(2)}) collective-permute-start(bf16[1040,128]{1,0:T(8,128)(2,1)S(1)} %pack.1.packed), channel_id=1, source_target_pairs={{0,256},{128,384},{1,257},{129,385},{2,258},{130,386},{3,259},{131... | collective-permute-start | bytes 798728 | tf_op jit(solution)/shard_map/ppermute | solution.py:381
  11.3 31.8 %collective-permute-start.2 = (bf16[1040,128]{1,0:T(8,128)(2,1)S(1)}, bf16[1040,128]{1,0:T(8,128)(2,1)S(1)}, u32[]{:S(2)}, u32[]{:S(2)}) collective-permute-start(bf16[1040,128]{1,0:T(8,128)(2,1)S(1)} %pack.1.packed), channel_id=1, source_target_pairs={{0,128},{128,256},{256,384},{1,129},{129,257},{257,385},{2,130},{1... | collective-permute-start | bytes 798728 | tf_op jit(solution)/shard_map/ppermute | solution.py:381

commit v8 on v7

--- a/solution.py
+++ b/solution.py
@@ -384,17 +384,14 @@
         return [pltpu.SMEM((k,), jnp.int32) for k in sizes]
 
     def far_gather(q, step):
-        groups, ends = [], []
-        for section in range(sections):
-            at = section * doms
-            begun = step == 0 or layers * (sections - 1 - section) <= step + 1
-            groups += [[at + i for i in pair] for pair in (far_pairs if begun else near_pairs)]
-            if begun and (step == 0 or section >= sections - 2):
-                ends.append(at)
-            elif begun:
-                groups.append([at, at + doms - 1])
-        for a, b in zip(ends[::2], ends[1::2]):
-            groups += [[a, b], [a + doms - 1, b + doms - 1]]
+        groups = []
+        for section in range(0, sections, 2):
+            begun = step == 0 or layers * (sections - 2 - section) <= step + 1
+            a, b = section * doms, (section + 1) * doms
+            for at in (a, b):
+                groups += [[at + i for i in pair] for pair in (far_pairs if begun else near_pairs)]
+            if begun:
+                groups += [[a, b], [a + doms - 1, b + doms - 1]]
         return lax.all_gather(q, ("section", "dom"), axis_index_groups=groups)
 
     wide = s(blk, 2 * d)

time: 79.4 us -> 76.8 us (0.967)
  the two profiles are of different devices: /device:TPU:3 before, /device:TPU:37 now
where the time goes in v8:
time: 76.8 us; the launch traced here: 76.5 us
  blocking collectives  48.2 us (63%)
  Pallas kernels  21.8 us (28%)
  starting transfers between devices  4.31 us (6%)
  between operations  2.22 us (3%)
    all_gather x5, blocking collectives, near_gather(): return lax.all_gather(q, 'dom', axis_index_groups=near_pairs)  26.1 us
    all_gather x4, blocking collectives, far_gather(): return lax.all_gather(q, ('section', 'dom'), axis_index_groups=groups)  22.2 us
    pallas_call x4, Pallas kernels, shards(): call(far_layer_body(step, step == 0, tail), (rows, rows, wide if tail els...  8.76 us
    pallas_call x3, Pallas kernels, shards(): call(near_layer_body(step), (rows, rows, both, wide), [VM] * 12, f'layer{...  6.8 us
    ppermute x3, starting transfers between devices, fetch(): lax.ppermute(own, 'section', [(i, i + k) for i in range(sections - k)])  4.31 us
    pallas_call x1, Pallas kernels, shards(): call(last_body(steps - 1), s(2, n, d), [VM] * 8 + [SM] * 2, f'layer{steps...  2.44 us
    pallas_call x1, Pallas kernels, shards(): call(prep_body, (rows, s(n, span), s(blk, span), rows, two, two, two, bot...  1.94 us
  transfers between devices with their start and end apart: 3, of which 0 were waited for; matrix products, arithmetic and copies ran while one was open for 0% of the time, Pallas kernels for 12%

profile of v8, /device:TPU:37, one launch (start us, length us, event | category | flops | bytes accessed | tf_op | source)
XLA Modules:
  0.0 76.5 jit_solution(4668521213524010332)
XLA Ops:
  0.0 1.1 %pack.1.packed = bf16[1040,128]{1,0:T(8,128)(2,1)S(1)} custom-call(bf16[2,128,128]{2,1,0:T(8,128)(2,1)} %refs_0_.3, bf16[2,256,128]{2,1,0:T(8,128)(2,1)} %refs_1_.3, bf16[2,128]{1,0:T(2,128)(2,1)} %refs_2_.3, bf16[2,128,128]{2,1,0:T(8,128)(2,1)} %refs_3_.3, bf16[2,128]{1,0:T(2,128)(2,1)} %refs_4_.3, bf16[2,128]{1,0:T(2,128)(2,1)} %refs_5_.3), custom_call_target="tpu_custom_call" | custom-call | tf_op jit(solution)/shard_map/pack/pallas_call | solution.py:415
  1.2 0.7 collective-permute-start
  3.8 1.9 %prep.1 = (bf16[1024,256]{1,0:T(8,128)(2,1)S(1)}, bf16[1024,1280]{1,0:T(8,128)(2,1)S(1)}, bf16[128,1280]{1,0:T(8,128)(2,1)S(1)}, bf16[1024,256]{1,0:T(8,128)(2,1...) custom-call(s32[1]{0:T(128)S(6)} %copy.14.count, ...), custom_call_target="tpu_custom_call" | custom-call | tf_op jit(solution)/shard_map/prep/pallas_call | solution.py:418
  5.7 2.3 %all-gather = bf16[512,256]{1,0:T(8,128)(2,1)S(1)} all-gather(bf16[256,256]{1,0:T(8,128)(2,1)S(1)} %get-tuple-element.54), channel_id=2, replica_groups={{0,1},{2,3},{4,5},{6,7},{8,9},{10,11},{12,13},{14,15},{16,17},{18,19},{..., dimensions={0}, use_global_device_ids=true | all-gather | bytes 393216 | tf_op jit(solution)/shard_map/all_gather | solution.py:378
  8.0 1.3 %collective-permute-start.1 = (bf16[1040,128]{1,0:T(8,128)(2,1)S(1)}, bf16[1040,128]{1,0:T(8,128)(2,1)S(1)}, u32[]{:S(2)}, u32[]{:S(2)}) collective-permute-start(bf16[1040,128]{1,0:T(8,128)(2,1)S(1)} %pack.1.packed), channel_id=1, source_target_pairs={{0,256},{128,384},{1,257},{129,385},{2,258},{130,386},{3,259},{131... | collective-permute-start | bytes 798728 | tf_op jit(solution)/shard_map/ppermute | solution.py:381
  9.3 2.3 %collective-permute-start.2 = (bf16[1040,128]{1,0:T(8,128)(2,1)S(1)}, bf16[1040,128]{1,0:T(8,128)(2,1)S(1)}, u32[]{:S(2)}, u32[]{:S(2)}) collective-permute-start(bf16[1040,128]{1,0:T(8,128)(2,1)S(1)} %pack.1.packed), channel_id=1, source_target_pairs={{0,128},{128,256},{256,384},{1,129},{129,257},{257,385},{2,130},{1... | collective-permute-start | bytes 798728 | tf_op jit(solution)/shard_map/ppermute | solution.py:381
  11.7 0.1 pack_late.1.nxt.pack
  11.8 0.6 first.1
  12.4 6.9 %all-gather.1 = bf16[768,256]{1,0:T(8,128)(2,1)S(1)} all-gather(bf16[384,256]{1,0:T(8,128)(2,1)S(1)} %get-tuple-element.63), channel_id=3, replica_groups={{1,2},{3,4},{5,6},{7,8},{9,10},{11,12},{13,14},{15,16},{17,18},{19,20},..., dimensions={0}, use_global_device_ids=true | all-gather | bytes 589824 | tf_op jit(solution)/shard_map/all_gather | solution.py:395
  19.3 2.2 %layer0.1 = (bf16[1024,256]{1,0:T(8,128)(2,1)S(1)}, bf16[1024,256]{1,0:T(8,128)(2,1)S(1)}, bf16[256,256]{1,0:T(8,128)(2,1)S(1)}, bf16[128,256]{1,0:T(8,128)(2,1)S(1)}, bf16[128,256]{1,0:T(8,128)(2,1)S(1)}) custom-call(bf16[1024,256]{1,0:T(8,128)(2,1)S(1)} %get-tuple-element.51.h, bf16[1024,256]{1,0:T(8,128)(2,1)S(1)} %get-tuple-element.60.m, ...), custom_call_target="tpu_custom_call" | custom-call | tf_op jit(solution)/shard_map/layer0/pallas_call | solution.py:457
  21.6 7.8 %all-gather.2 = bf16[512,256]{1,0:T(8,128)(2,1)S(1)} all-gather(bf16[256,256]{1,0:T(8,128)(2,1)S(1)} %get-tuple-element.69), channel_id=4, replica_groups={{0,1},{2,3},{4,5},{6,7},{8,9},{10,11},{12,13},{14,15},{16,17},{18,19},{..., dimensions={0}, use_global_device_ids=true | all-gather | bytes 393216 | tf_op jit(solution)/shard_map/all_gather | solution.py:378
  29.3 2.3 %layer1.1 = (bf16[1024,256]{1,0:T(8,128)(2,1)S(1)}, bf16[1024,256]{1,0:T(8,128)(2,1)S(1)}, bf16[256,256]{1,0:T(8,128)(2,1)S(1)}, bf16[128,256]{1,0:T(8,128)(2,1)S(1)}) custom-call(bf16[1024,256]{1,0:T(8,128)(2,1)S(1)} %get-tuple-element.66.h, bf16[1024,256]{1,0:T(8,128)(2,1)S(1)} %get-tuple-element.67.m, bf16[128,256]{1,0:T(8,128)(2,1)S(1)} %get-tuple-element.68.far_m, ...), custom_call_target="tpu_custom_call" | custom-call | tf_op jit(solution)/shard_map/layer1/pallas_call | solution.py:469
  31.6 5.1 %all-gather.3 = bf16[512,256]{1,0:T(8,128)(2,1)S(1)} all-gather(bf16[256,256]{1,0:T(8,128)(2,1)S(1)} %get-tuple-element.74), channel_id=5, replica_groups={{0,1},{2,3},{4,5},{6,7},{8,9},{10,11},{12,13},{14,15},{16,17},{18,19},{..., dimensions={0}, use_global_device_ids=true | all-gather | bytes 393216 | tf_op jit(solution)/shard_map/all_gather | solution.py:395
  36.7 2.3 %layer2.1 = (bf16[1024,256]{1,0:T(8,128)(2,1)S(1)}, bf16[1024,256]{1,0:T(8,128)(2,1)S(1)}, bf16[256,256]{1,0:T(8,128)(2,1)S(1)}, bf16[128,256]{1,0:T(8,128)(2,1)S(1)}) custom-call(bf16[1024,256]{1,0:T(8,128)(2,1)S(1)} %get-tuple-element.71.h, bf16[1024,256]{1,0:T(8,128)(2,1)S(1)} %get-tuple-element.72.m, bf16[128,256]{1,0:T(8,128)(2,1)S(1)} %get-tuple-element.73.near_m, ...), custom_call_target="tpu_custom_call" | custom-call | tf_op jit(solution)/shard_map/layer2/pallas_call | solution.py:457
  38.9 5.3 %all-gather.4 = bf16[512,256]{1,0:T(8,128)(2,1)S(1)} all-gather(bf16[256,256]{1,0:T(8,128)(2,1)S(1)} %get-tuple-element.79), channel_id=6, replica_groups={{0,1},{2,3},{4,5},{6,7},{8,9},{10,11},{12,13},{14,15},{16,17},{18,19},{..., dimensions={0}, use_global_device_ids=true | all-gather | bytes 393216 | tf_op jit(solution)/shard_map/all_gather | solution.py:378
  44.2 2.3 %layer3.1 = (bf16[1024,256]{1,0:T(8,128)(2,1)S(1)}, bf16[1024,256]{1,0:T(8,128)(2,1)S(1)}, bf16[256,256]{1,0:T(8,128)(2,1)S(1)}, bf16[128,256]{1,0:T(8,128)(2,1)S(1)}) custom-call(bf16[1024,256]{1,0:T(8,128)(2,1)S(1)} %get-tuple-element.76.h, bf16[1024,256]{1,0:T(8,128)(2,1)S(1)} %get-tuple-element.77.m, bf16[128,256]{1,0:T(8,128)(2,1)S(1)} %get-tuple-element.78.far_m, ...), custom_call_target="tpu_custom_call" | custom-call | tf_op jit(solution)/shard_map/layer3/pallas_call | solution.py:469
  46.5 5.1 %all-gather.5 = bf16[512,256]{1,0:T(8,128)(2,1)S(1)} all-gather(bf16[256,256]{1,0:T(8,128)(2,1)S(1)} %get-tuple-element.83), channel_id=7, replica_groups={{1,2},{3,4},{5,6},{7,8},{9,10},{11,12},{13,14},{15,16},{17,18},{19,20},..., dimensions={0}, use_global_device_ids=true | all-gather | bytes 393216 | tf_op jit(solution)/shard_map/all_gather | solution.py:395
  51.6 2.2 %layer4.1 = (bf16[1024,256]{1,0:T(8,128)(2,1)S(1)}, bf16[1024,256]{1,0:T(8,128)(2,1)S(1)}, bf16[256,256]{1,0:T(8,128)(2,1)S(1)}, bf16[128,256]{1,0:T(8,128)(2,1)S(1)}) custom-call(bf16[1024,256]{1,0:T(8,128)(2,1)S(1)} %get-tuple-element.80.h, bf16[1024,256]{1,0:T(8,128)(2,1)S(1)} %get-tuple-element.81.m, bf16[128,256]{1,0:T(8,128)(2,1)S(1)} %get-tuple-element.82.near_m, ...), custom_call_target="tpu_custom_call" | custom-call | tf_op jit(solution)/shard_map/layer4/pallas_call | solution.py:457
  53.8 5.5 %all-gather.6 = bf16[512,256]{1,0:T(8,128)(2,1)S(1)} all-gather(bf16[256,256]{1,0:T(8,128)(2,1)S(1)} %get-tuple-element.87), channel_id=8, replica_groups={{0,1},{2,3},{4,5},{6,7},{8,9},{10,11},{12,13},{14,15},{16,17},{18,19},{..., dimensions={0}, use_global_device_ids=true | all-gather | bytes 393216 | tf_op jit(solution)/shard_map/all_gather | solution.py:378
  59.3 2.3 %layer5.1 = (bf16[1024,256]{1,0:T(8,128)(2,1)S(1)}, bf16[1024,256]{1,0:T(8,128)(2,1)S(1)}, bf16[256,256]{1,0:T(8,128)(2,1)S(1)}, bf16[128,256]{1,0:T(8,128)(2,1)S(1)}) custom-call(bf16[1024,256]{1,0:T(8,128)(2,1)S(1)} %get-tuple-element.84.h, bf16[1024,256]{1,0:T(8,128)(2,1)S(1)} %get-tuple-element.85.m, bf16[128,256]{1,0:T(8,128)(2,1)S(1)} %get-tuple-element.86.far_m, ...), custom_call_target="tpu_custom_call" | custom-call | tf_op jit(solution)/shard_map/layer5/pallas_call | solution.py:469
  61.6 5.1 %all-gather.7 = bf16[512,256]{1,0:T(8,128)(2,1)S(1)} all-gather(bf16[256,256]{1,0:T(8,128)(2,1)S(1)} %get-tuple-element.92), channel_id=9, replica_groups={{1,2},{3,4},{5,6},{7,8},{9,10},{11,12},{13,14},{15,16},{17,18},{19,20},..., dimensions={0}, use_global_device_ids=true | all-gather | bytes 393216 | tf_op jit(solution)/shard_map/all_gather | solution.py:395
  66.7 2.0 %layer6.1 = (bf16[1024,256]{1,0:T(8,128)(2,1)S(1)}, bf16[1024,256]{1,0:T(8,128)(2,1)S(1)}, bf16[128,256]{1,0:T(8,128)(2,1)S(1)}, bf16[128,256]{1,0:T(8,128)(2,1)S(1)}) custom-call(bf16[1024,256]{1,0:T(8,128)(2,1)S(1)} %get-tuple-element.89.h, bf16[1024,256]{1,0:T(8,128)(2,1)S(1)} %get-tuple-element.90.m, bf16[128,256]{1,0:T(8,128)(2,1)S(1)} %get-tuple-element.91.near_m, ...), custom_call_target="tpu_custom_call" | custom-call | tf_op jit(solution)/shard_map/layer6/pallas_call | solution.py:457
  68.7 5.2 %all-gather.8 = bf16[256,256]{1,0:T(8,128)(2,1)S(1)} all-gather(bf16[128,256]{1,0:T(8,128)(2,1)S(1)} %get-tuple-element.95), channel_id=10, replica_groups={{0,1},{2,3},{4,5},{6,7},{8,9},{10,11},{12,13},{14,15},{16,17},{18,19},{..., dimensions={0}, use_global_device_ids=true | all-gather | bytes 196608 | tf_op jit(solution)/shard_map/all_gather | solution.py:378
  73.9 2.4 %layer7.1 = bf16[2,1024,128]{2,1,0:T(8,128)(2,1)} custom-call(bf16[1024,256]{1,0:T(8,128)(2,1)S(1)} %get-tuple-element.93.h, bf16[1024,256]{1,0:T(8,128)(2,1)S(1)} %get-tuple-element.94.m, bf16[2,128,256]{2,1,0:T(8,128)(2,1)S(1)} %get-tuple-element.52.pick, bf16[2,128,256]{2,1,0:T(8,128)(2,1)S(1)} %bitcast.18, bf16[128,256]{1,0:T(8,128)(2,1)S(1)} %get-tuple-element.96.far_m, ...), custom_call_target="tpu_custom_call" | custom-call | tf_op jit(solution)/shard_map/layer7/pallas_call | solution.py:472
  (3 shorter events, 0.0 us)
Async XLA Ops:
  1.2 10.6 %collective-permute-start = (bf16[1040,128]{1,0:T(8,128)(2,1)S(1)}, bf16[1040,128]{1,0:T(8,128)(2,1)S(1)}, u32[]{:S(2)}, u32[]{:S(2)}) collective-permute-start(bf16[1040,128]{1,0:T(8,128)(2,1)S(1)} %pack.1.packed), channel_id=1, source_target_pairs={{0,384},{1,385},{2,386},{3,387},{4,388},{5,389},{6,390},{7,391},{8... | collective-permute-start | bytes 798728 | tf_op jit(solution)/shard_map/ppermute | solution.py:381
  8.0 21.3 %collective-permute-start.1 = (bf16[1040,128]{1,0:T(8,128)(2,1)S(1)}, bf16[1040,128]{1,0:T(8,128)(2,1)S(1)}, u32[]{:S(2)}, u32[]{:S(2)}) collective-permute-start(bf16[1040,128]{1,0:T(8,128)(2,1)S(1)} %pack.1.packed), channel_id=1, source_target_pairs={{0,256},{128,384},{1,257},{129,385},{2,258},{130,386},{3,259},{131... | collective-permute-start | bytes 798728 | tf_op jit(solution)/shard_map/ppermute | solution.py:381
  9.3 34.9 %collective-permute-start.2 = (bf16[1040,128]{1,0:T(8,128)(2,1)S(1)}, bf16[1040,128]{1,0:T(8,128)(2,1)S(1)}, u32[]{:S(2)}, u32[]{:S(2)}) collective-permute-start(bf16[1040,128]{1,0:T(8,128)(2,1)S(1)} %pack.1.packed), channel_id=1, source_target_pairs={{0,128},{128,256},{256,384},{1,129},{129,257},{257,385},{2,130},{1... | collective-permute-start | bytes 798728 | tf_op jit(solution)/shard_map/ppermute | solution.py:381
